TPU v7x, 128 devices: a whole 4x4x4 slice. The times are simulated.
128 devices in a mesh: shot: 4 (over x_lo, core), sub: 32 (over x_hi, z, y).
Axes of the slice: x: 4 (x_hi: 2, x_lo: 2; x = x_hi * 2 + x_lo), y: 4, z: 4, core: 2. Of those that a mesh axis runs over, the one named last changes fastest.
Arguments:
- velocity: float32 [512, 128, 256], P(('shot', 'sub')), may hold values from 1.5 to 4.5
- density: float32 [512, 128, 256], P(('shot', 'sub')), may hold values from 1 to 3
- aperture_start: int32 [4], P('shot'), may hold values from 0 to 96
- source_cell: int32 [4], P('shot'), may hold values from 0 to 4194303
- receiver_cells: int32 [4, 256], P('shot'), may hold values from 0 to 4194303, as said below
- wavelet: float32 [4, 4], P('shot'), may hold values from -6 to 6
- observed: float32 [4, 4, 256], P('shot'), may hold values from -6 to 6
- forward_old: float32 [4, 128, 128, 256], P('shot', 'sub'), may hold values from -6 to 6
- forward_now: float32 [4, 128, 128, 256], P('shot', 'sub'), may hold values from -6 to 6
- adjoint_later: float32 [4, 128, 128, 256], P('shot', 'sub'), may hold values from -6 to 6
- adjoint_now: float32 [4, 128, 128, 256], P('shot', 'sub'), may hold values from -6 to 6
Outputs:
- gradient: float32 [512, 128, 256], P(('shot', 'sub'))
- forward_last: float32 [4, 128, 128, 256], P('shot', 'sub')
- adjoint_first: float32 [4, 128, 128, 256], P('shot', 'sub')
Inputs may be any that keep to these rules, and one draw needn't show every extreme that they name: `aperture_start`: the aperture of a shot lies inside the model. `receiver_cells`: several receivers of a shot may share a cell; their injections add up.
All inputs are finite; a program needn't handle non-finite values.
Results may differ from a plain program's by a relative error of at most 0.00002.
Values sent between devices are 32-bit elements; how exact they have to be, the bound alone decides.
No kernel may reach another device: no remote copies, remote signals or barrier semaphores. Data moves between devices by JAX's collectives and lax.ppermute only.
A program may use at most 64 MiB of HBM per device.

v0:
```python
import jax
import jax.numpy as jnp
from jax import lax
from jax.sharding import PartitionSpec as P

lap_coeffs = (-205.0 / 72.0, 8.0 / 5.0, -1.0 / 5.0, 8.0 / 315.0, -1.0 / 560.0)
diff_coeffs = (4.0 / 5.0, -1.0 / 5.0, 4.0 / 105.0, -1.0 / 280.0)
time_step_sq = 0.0088


def with_halo(block, sides, width):
    for axis, dim in sides:
        count = lax.axis_size(axis)
        forward = [(i, i + 1) for i in range(count - 1)]
        backward = [(target, source) for source, target in forward]
        low = lax.ppermute(
            lax.slice_in_dim(block, block.shape[dim] - width, None, axis=dim), axis, forward
        )
        high = lax.ppermute(lax.slice_in_dim(block, 0, width, axis=dim), axis, backward)
        block = jnp.concatenate([low, block, high], axis=dim)
    return block


def passed_along(value, axis, steps):
    count = lax.axis_size(axis)
    pairs = [(source, (source + steps) % count) for source in range(count)]
    return lax.ppermute(value, axis, pairs)


def offset_view(padded, direction, offset):
    starts = [4, 4, 4]
    starts[direction] = 4 + offset
    extent = [padded.shape[0] - 8, padded.shape[1] - 8, padded.shape[2] - 8]
    return lax.slice(
        padded, starts, [starts[0] + extent[0], starts[1] + extent[1], starts[2] + extent[2]]
    )


def laplacian(padded):
    summed = 3.0 * lap_coeffs[0] * offset_view(padded, 0, 0)
    for direction in range(3):
        for reach in range(1, 5):
            summed = summed + lap_coeffs[reach] * (
                offset_view(padded, direction, reach) + offset_view(padded, direction, -reach)
            )
    return summed


def derivative(padded, direction):
    summed = diff_coeffs[0] * (
        offset_view(padded, direction, 1) - offset_view(padded, direction, -1)
    )
    for reach in range(2, 5):
        summed = summed + diff_coeffs[reach - 1] * (
            offset_view(padded, direction, reach) - offset_view(padded, direction, -reach)
        )
    return summed


def advance(padded, previous, speed_sq, slopes):
    current = offset_view(padded, 0, 0)
    operator = laplacian(padded)
    for direction in range(3):
        operator = operator - slopes[direction] * derivative(padded, direction)
    return 2.0 * current - previous + speed_sq * operator


def propagate(current, previous, speed_sq, slopes):
    rimmed = with_halo(current, (("sub", 0),), 4)
    padded = jnp.pad(rimmed, ((0, 0), (4, 4), (4, 4)))
    return advance(padded, previous, speed_sq, slopes)


def local_slots(field, cells_wanted, first_cell):
    count_cells = field.shape[0] * field.shape[1] * field.shape[2]
    local_index = cells_wanted - first_cell
    is_local = (local_index >= 0) & (local_index < count_cells)
    clipped = jnp.clip(local_index, 0, count_cells - 1)
    return (is_local, clipped)


def sample_local(field, cells_wanted, first_cell):
    is_local, clipped = local_slots(field, cells_wanted, first_cell)
    return jnp.where(is_local, field.reshape(-1)[clipped], 0.0)


def inject_local(field, cells_wanted, amounts, first_cell):
    is_local, clipped = local_slots(field, cells_wanted, first_cell)
    flattened = field.reshape(-1).at[clipped].add(jnp.where(is_local, amounts, 0.0))
    return flattened.reshape(field.shape)


def on_device(
    velocity,
    density,
    aperture_start,
    source_cell,
    receiver_cells,
    wavelet,
    observed,
    forward_old,
    forward_now,
    adjoint_later,
    adjoint_now,
):
    slab_rows = velocity.shape[0]
    slab_cells = velocity.shape[0] * velocity.shape[1] * velocity.shape[2]
    groups = lax.axis_size("shot")
    columns = lax.axis_size("sub")
    column = lax.axis_index("sub")
    sections = (columns - 1).bit_length()
    start_slab = aperture_start[0]
    block_index = start_slab // columns
    offset = start_slab % columns
    upper_block = (block_index + 1) % groups
    every_speed, every_density = (
        lax.all_gather(velocity, "shot", axis=0, tiled=True),
        lax.all_gather(density, "shot", axis=0, tiled=True),
    )
    lower_speed = lax.dynamic_slice_in_dim(every_speed, block_index * slab_rows, slab_rows, 0)
    lower_density = lax.dynamic_slice_in_dim(every_density, block_index * slab_rows, slab_rows, 0)
    upper_speed = lax.dynamic_slice_in_dim(every_speed, upper_block * slab_rows, slab_rows, 0)
    upper_density = lax.dynamic_slice_in_dim(every_density, upper_block * slab_rows, slab_rows, 0)
    carried = jnp.stack([lower_speed, lower_density, upper_speed, upper_density])
    for bit_index in range(sections):
        stride = 1 << bit_index
        arrived = passed_along(carried, "sub", columns - stride)
        inside = column + stride < columns
        turned = jnp.where(inside, arrived, jnp.concatenate([arrived[2:], arrived[:2]], 0))
        active = offset // stride % 2 == 1
        carried = jnp.where(active, turned, carried)
    speed = carried[0]
    mass = carried[1]
    speed_sq = time_step_sq * speed * speed
    log_rim = with_halo(jnp.log(mass), (("sub", 0),), 4)
    log_padded = jnp.pad(log_rim, ((0, 0), (4, 4), (4, 4)))
    slopes = [derivative(log_padded, direction) for direction in range(3)]
    first_cell = column * slab_cells
    steps_count = wavelet.shape[1]
    fields = [forward_old[0], forward_now[0]]
    samples = []
    for step_index in range(steps_count):
        advanced = propagate(fields[-1], fields[-2], speed_sq, slopes)
        advanced = inject_local(
            advanced, source_cell, wavelet[0, step_index : step_index + 1], first_cell
        )
        sampled = sample_local(advanced, receiver_cells[0], first_cell)
        sampled = lax.psum(sampled, "sub")
        samples.append(sampled)
        fields.append(advanced)
    recorded = jnp.stack(samples)
    residual = recorded - observed[0]
    later_field = adjoint_later[0]
    current = adjoint_now[0]
    summed = jnp.zeros(current.shape, jnp.float32)
    for step_index in reversed(range(steps_count)):
        earlier = propagate(current, later_field, speed_sq, slopes)
        earlier = inject_local(earlier, receiver_cells[0], residual[step_index], first_cell)
        curvature = fields[step_index + 2] - 2.0 * fields[step_index + 1] + fields[step_index]
        summed = summed + earlier * curvature
        later_field = current
        current = earlier
    image_term = 2.0 / speed * summed
    returning = jnp.stack([image_term, jnp.zeros_like(image_term)])
    for bit_index in range(sections):
        stride = 1 << bit_index
        arrived = passed_along(returning, "sub", stride)
        inside = column >= stride
        turned = jnp.where(inside, arrived, arrived[::-1])
        active = offset // stride % 2 == 1
        returning = jnp.where(active, turned, returning)
    pieces = [
        jnp.where(group_index == block_index, returning[0], 0.0)
        + jnp.where(group_index == upper_block, returning[1], 0.0)
        for group_index in range(groups)
    ]
    gradient = lax.psum_scatter(jnp.concatenate(pieces, 0), "shot", scatter_dimension=0, tiled=True)
    return (gradient, fields[-1][None], current[None])


def solution(mesh):
    placed = (
        P(("shot", "sub"), None, None),
        P(("shot", "sub"), None, None),
        P("shot"),
        P("shot"),
        P("shot", None),
        P("shot", None),
        P("shot", None, None),
        P("shot", "sub", None, None),
        P("shot", "sub", None, None),
        P("shot", "sub", None, None),
        P("shot", "sub", None, None),
    )
    return jax.shard_map(
        on_device,
        mesh=mesh,
        in_specs=placed,
        out_specs=(
            P(("shot", "sub"), None, None),
            P("shot", "sub", None, None),
            P("shot", "sub", None, None),
        ),
        check_vma=False,
    )
```

profile of v0, /device:TPU:0, one launch (start us, length us, event | category | flops | bytes accessed | tf_op | source)
XLA Modules:
  0.0 854.0 jit_solution(16127009426923571803)
XLA Ops:
  9.4 31.7 %all-gather.3.cloned.1.call-done = f32[16,128,256]{2,1,0:T(8,128)} async-done(((f32[4,128,256]{2,1,0:T(8,128)}), f32[16,128,256]{2,1,0:T(8,128)}) %all-gather.3.cloned.1.call-update) | async-done | bytes 2097168 | tf_op jit(solution)/shard_map/all_gather | solution.py:117
  42.4 30.3 %all-gather.5.cloned.1.call-done = f32[16,128,256]{2,1,0:T(8,128)} async-done(((f32[4,128,256]{2,1,0:T(8,128)}), f32[16,128,256]{2,1,0:T(8,128)}) %all-gather.5.cloned.1.call-update) | async-done | bytes 2097168 | tf_op jit(solution)/shard_map/all_gather | solution.py:118
  76.3 7.2 collective-permute-start
  83.5 45.8 %collective-permute-done = f32[4,4,128,256]{3,2,1,0:T(8,128)S(1)} collective-permute-done((f32[4,4,128,256]{3,2,1,0:T(8,128)}, f32[4,4,128,256]{3,2,1,0:T(8,128)S(1)}, u32[]{:S(2)}, u32[]{:S(2)}) %collective-permute-start) | collective-permute-done | bytes 2097184 | tf_op jit(solution)/shard_map/ppermute | solution.py:27
  135.4 46.2 %collective-permute-done.1 = f32[4,4,128,256]{3,2,1,0:T(8,128)} collective-permute-done((f32[4,4,128,256]{3,2,1,0:T(8,128)S(1)}, f32[4,4,128,256]{3,2,1,0:T(8,128)}, u32[]{:S(2)}, u32[]{:S(2)}) %collective-permute-start.1) | collective-permute-done | bytes 2097184 | tf_op jit(solution)/shard_map/ppermute | solution.py:27
  187.4 45.7 %collective-permute-done.2 = f32[4,4,128,256]{3,2,1,0:T(8,128)S(1)} collective-permute-done((f32[4,4,128,256]{3,2,1,0:T(8,128)}, f32[4,4,128,256]{3,2,1,0:T(8,128)S(1)}, u32[]{:S(2)}, u32[]{:S(2)}) %collective-permute-start.2) | collective-permute-done | bytes 2097184 | tf_op jit(solution)/shard_map/ppermute | solution.py:27
  237.9 46.3 %collective-permute-done.3 = f32[4,4,128,256]{3,2,1,0:T(8,128)} collective-permute-done((f32[4,4,128,256]{3,2,1,0:T(8,128)S(1)}, f32[4,4,128,256]{3,2,1,0:T(8,128)}, u32[]{:S(2)}, u32[]{:S(2)}) %collective-permute-start.3) | collective-permute-done | bytes 2097184 | tf_op jit(solution)/shard_map/ppermute | solution.py:27
  289.6 6.8 collective-permute-start.10
  297.7 41.2 %collective-permute-done.4 = f32[4,4,128,256]{3,2,1,0:T(8,128)} collective-permute-done((f32[4,4,128,256]{3,2,1,0:T(8,128)S(1)}, f32[4,4,128,256]{3,2,1,0:T(8,128)}, u32[]{:S(2)}, u32[]{:S(2)}) %collective-permute-start.4) | collective-permute-done | bytes 2097184 | tf_op jit(solution)/shard_map/ppermute | solution.py:27
  345.4 4.6 collective-permute-start.8
  358.2 6.0 fusion.49
  366.8 4.4 collective-permute-start.12
  373.8 6.1 collective-permute-start.6
  393.6 5.5 collective-permute-start.14
  407.3 6.6 collective-permute-done.13
  425.6 6.6 collective-permute-start.16
  433.4 5.1 fusion.50
  438.5 10.5 %gather_fusion = f32[256]{0:T(256)S(1)} fusion(f32[131072]{0:T(1024)} %copy-done.4, s32[1024]{0:T(1024)} %pad_clamp_fusion), kind=kCustom, calls=%fused_computation | custom fusion | bytes 3072 | tf_op jit(solution)/shard_map/gather | solution.py:84
  452.2 10.3 %gather_fusion.2 = f32[256]{0:T(256)S(1)} fusion(f32[131072]{0:T(1024)} %fusion.53, s32[1024]{0:T(1024)S(1)} %copy-done.40), kind=kCustom, calls=%fused_computation.2 | custom fusion | bytes 3072 | tf_op jit(solution)/shard_map/gather | solution.py:84
  474.7 91.3 %all-reduce.10 = (f32[1,256]{1,0:T(1,128)S(1)}, f32[1,256]{1,0:T(1,128)S(1)}, f32[1,256]{1,0:T(1,128)S(1)}, f32[1,256]{1,0:T(1,128)S(1)}) all-reduce(f32[1,256]{1,0:T(1,128)S(1)} %bitcast.128, f32[1,256]{1,0:T(1,128)S(1)} %bitcast.129, f32[1,256]{1,0:T(1,128)S(1)} %bitcast.130, ...), channel_id=1, replica_groups=mesh['shot'=4,'sub'=32] {'sub'}, use_global_device_ids=true, to_apply=%region_3.4 | all-reduce | flops 1024 | bytes 8192 | tf_op jit(solution)/shard_map/psum | solution.py:148
  571.5 8.6 %collective-permute-done.18 = f32[4,128,256]{2,1,0:T(8,128)S(1)} collective-permute-done((f32[4,128,256]{2,1,0:T(8,128)S(1)}, f32[4,128,256]{2,1,0:T(8,128)S(1)}, u32[]{:S(2)}, u32[]{:S(2)}) %collective-permute-start.18) | collective-permute-done | bytes 524320 | tf_op jit(solution)/shard_map/ppermute | solution.py:16
  589.5 4.1 scatter_fusion.1
  598.2 8.8 %collective-permute-done.20 = f32[4,128,256]{2,1,0:T(8,128)S(1)} collective-permute-done((f32[4,128,256]{2,1,0:T(8,128)S(1)}, f32[4,128,256]{2,1,0:T(8,128)S(1)}, u32[]{:S(2)}, u32[]{:S(2)}) %collective-permute-start.20) | collective-permute-done | bytes 524320 | tf_op jit(solution)/shard_map/ppermute | solution.py:16
  607.1 4.8 collective-permute-done.19
  653.1 22.1 %collective-permute-done.23 = f32[2,4,128,256]{3,2,1,0:T(8,128)S(1)} collective-permute-done((f32[2,4,128,256]{3,2,1,0:T(8,128)S(1)}, f32[2,4,128,256]{3,2,1,0:T(8,128)S(1)}, u32[]{:S(2)}, u32[]{:S(2)}) %collective-permute-start.23) | collective-permute-done | bytes 1048608 | tf_op jit(solution)/shard_map/ppermute | solution.py:27
  675.4 21.0 %collective-permute-done.24 = f32[2,4,128,256]{3,2,1,0:T(8,128)} collective-permute-done((f32[2,4,128,256]{3,2,1,0:T(8,128)S(1)}, f32[2,4,128,256]{3,2,1,0:T(8,128)}, u32[]{:S(2)}, u32[]{:S(2)}) %collective-permute-start.24) | collective-permute-done | bytes 1048608 | tf_op jit(solution)/shard_map/ppermute | solution.py:27
  698.8 22.9 %collective-permute-done.25 = f32[2,4,128,256]{3,2,1,0:T(8,128)} collective-permute-done((f32[2,4,128,256]{3,2,1,0:T(8,128)S(1)}, f32[2,4,128,256]{3,2,1,0:T(8,128)}, u32[]{:S(2)}, u32[]{:S(2)}) %collective-permute-start.25) | collective-permute-done | bytes 1048608 | tf_op jit(solution)/shard_map/ppermute | solution.py:27
  723.6 22.9 %collective-permute-start.26 = (f32[2,4,128,256]{3,2,1,0:T(8,128)S(1)}, f32[2,4,128,256]{3,2,1,0:T(8,128)S(1)}, u32[]{:S(2)}, u32[]{:S(2)}) collective-permute-start(f32[2,4,128,256]{3,2,1,0:T(8,128)S(1)} %fusion.10), channel_id=1, source_target_pairs={{0,8},{1,9},{2,10},{3,11},{4,12},{5,13},{6,14},{7,15},{8,16},{9,17... | collective-permute-start | bytes 3145736 | tf_op jit(solution)/shard_map/ppermute | solution.py:27
  746.5 22.1 %collective-permute-done.26 = f32[2,4,128,256]{3,2,1,0:T(8,128)S(1)} collective-permute-done((f32[2,4,128,256]{3,2,1,0:T(8,128)S(1)}, f32[2,4,128,256]{3,2,1,0:T(8,128)S(1)}, u32[]{:S(2)}, u32[]{:S(2)}) %collective-permute-start.26) | collective-permute-done | bytes 1048608 | tf_op jit(solution)/shard_map/ppermute | solution.py:27
  770.0 32.1 %collective-permute-start.27 = (f32[2,4,128,256]{3,2,1,0:T(8,128)S(1)}, f32[2,4,128,256]{3,2,1,0:T(8,128)S(1)}, u32[]{:S(2)}, u32[]{:S(2)}) collective-permute-start(f32[2,4,128,256]{3,2,1,0:T(8,128)S(1)} %fusion.11), channel_id=1, source_target_pairs={{0,16},{1,17},{2,18},{3,19},{4,20},{5,21},{6,22},{7,23},{8,24},{9,... | collective-permute-start | bytes 3145736 | tf_op jit(solution)/shard_map/ppermute | solution.py:27
  802.1 12.8 %collective-permute-done.27 = f32[2,4,128,256]{3,2,1,0:T(8,128)S(1)} collective-permute-done((f32[2,4,128,256]{3,2,1,0:T(8,128)S(1)}, f32[2,4,128,256]{3,2,1,0:T(8,128)S(1)}, u32[]{:S(2)}, u32[]{:S(2)}) %collective-permute-start.27) | collective-permute-done | bytes 1048608 | tf_op jit(solution)/shard_map/ppermute | solution.py:27
  816.8 30.3 %reduce-scatter.2.cloned.1.call-done = f32[4,128,256]{2,1,0:T(8,128)} async-done(((f32[16,128,256]{2,1,0:T(8,128)}), f32[4,128,256]{2,1,0:T(8,128)}) %reduce-scatter.2.cloned.1.call-update) | async-done | bytes 524304 | tf_op jit(solution)/shard_map/reduce_scatter | solution.py:177
  (224 shorter events, 166.0 us)
Async XLA Ops:
  7.2 33.9 %all-gather.3.cloned.1.call-start = ((), (), s32[]{:S(2)}) async-start(), calls=%async_computation.1 | async-start | bytes 2621440 | tf_op jit(solution)/shard_map/all_gather | solution.py:117
  7.9 64.8 %all-gather.5.cloned.1.call-start = ((), (), s32[]{:S(2)}) async-start(), calls=%async_computation.2 | async-start | bytes 2621440 | tf_op jit(solution)/shard_map/all_gather | solution.py:118
  8.6 838.4 %reduce-scatter.2.cloned.1.call-start = ((), (), s32[]{:S(2)}) async-start(), calls=%async_computation.3 | async-start | bytes 2621440 | tf_op jit(solution)/shard_map/reduce_scatter | solution.py:177
  76.3 53.1 %collective-permute-start = (f32[4,4,128,256]{3,2,1,0:T(8,128)}, f32[4,4,128,256]{3,2,1,0:T(8,128)S(1)}, u32[]{:S(2)}, u32[]{:S(2)}) collective-permute-start(f32[4,4,128,256]{3,2,1,0:T(8,128)} %pad_maximum_fusion), channel_id=1, source_target_pairs={{0,31},{1,0},{2,1},{3,2},{4,3},{5,4},{6,5},{7,6},{8,7},{9,8},{10,9... | collective-permute-start | bytes 6291464 | tf_op jit(solution)/shard_map/ppermute | solution.py:27
  132.7 48.9 %collective-permute-start.1 = (f32[4,4,128,256]{3,2,1,0:T(8,128)S(1)}, f32[4,4,128,256]{3,2,1,0:T(8,128)}, u32[]{:S(2)}, u32[]{:S(2)}) collective-permute-start(f32[4,4,128,256]{3,2,1,0:T(8,128)S(1)} %fusion.3), channel_id=1, source_target_pairs={{0,30},{1,31},{2,0},{3,1},{4,2},{5,3},{6,4},{7,5},{8,6},{9,7},{10,... | collective-permute-start | bytes 6291464 | tf_op jit(solution)/shard_map/ppermute | solution.py:27
  186.6 46.5 %collective-permute-start.2 = (f32[4,4,128,256]{3,2,1,0:T(8,128)}, f32[4,4,128,256]{3,2,1,0:T(8,128)S(1)}, u32[]{:S(2)}, u32[]{:S(2)}) collective-permute-start(f32[4,4,128,256]{3,2,1,0:T(8,128)} %fusion.4), channel_id=1, source_target_pairs={{0,28},{1,29},{2,30},{3,31},{4,0},{5,1},{6,2},{7,3},{8,4},{9,5},{1... | collective-permute-start | bytes 6291464 | tf_op jit(solution)/shard_map/ppermute | solution.py:27
  237.1 47.1 %collective-permute-start.3 = (f32[4,4,128,256]{3,2,1,0:T(8,128)S(1)}, f32[4,4,128,256]{3,2,1,0:T(8,128)}, u32[]{:S(2)}, u32[]{:S(2)}) collective-permute-start(f32[4,4,128,256]{3,2,1,0:T(8,128)S(1)} %fusion.5), channel_id=1, source_target_pairs={{0,24},{1,25},{2,26},{3,27},{4,28},{5,29},{6,30},{7,31},{8,0},{9,1... | collective-permute-start | bytes 6291464 | tf_op jit(solution)/shard_map/ppermute | solution.py:27
  288.7 50.3 %collective-permute-start.4 = (f32[4,4,128,256]{3,2,1,0:T(8,128)S(1)}, f32[4,4,128,256]{3,2,1,0:T(8,128)}, u32[]{:S(2)}, u32[]{:S(2)}) collective-permute-start(f32[4,4,128,256]{3,2,1,0:T(8,128)S(1)} %fusion.6), channel_id=1, source_target_pairs={{0,16},{1,17},{2,18},{3,19},{4,20},{5,21},{6,22},{7,23},{8,24},{9,... | collective-permute-start | bytes 6291464 | tf_op jit(solution)/shard_map/ppermute | solution.py:27
  289.6 62.2 %collective-permute-start.10 = (f32[4,128,256]{2,1,0:T(8,128)S(1)}, f32[4,128,256]{2,1,0:T(8,128)S(1)}, u32[]{:S(2)}, u32[]{:S(2)}) collective-permute-start(f32[4,128,256]{2,1,0:T(8,128)S(1)} %bitcast.106), channel_id=1, source_target_pairs={{0,1},{1,2},{2,3},{3,4},{4,5},{5,6},{6,7},{7,8},{8,9},{9,10},{10,1... | collective-permute-start | bytes 1572872 | tf_op jit(solution)/shard_map/ppermute | solution.py:16
  296.4 55.4 %collective-permute-start.9 = (f32[4,128,256]{2,1,0:T(8,128)S(1)}, f32[4,128,256]{2,1,0:T(8,128)}, u32[]{:S(2)}, u32[]{:S(2)}) collective-permute-start(f32[4,128,256]{2,1,0:T(8,128)S(1)} %bitcast.107), channel_id=1, source_target_pairs={{1,0},{2,1},{3,2},{4,3},{5,4},{6,5},{7,6},{8,7},{9,8},{10,9},{11,1... | collective-permute-start | bytes 1572872 | tf_op jit(solution)/shard_map/ppermute | solution.py:19
  344.1 11.1 %collective-permute-start.7 = (f32[4,128,256]{2,1,0:T(8,128)S(1)}, f32[4,128,256]{2,1,0:T(8,128)S(1)}, u32[]{:S(2)}, u32[]{:S(2)}) collective-permute-start(f32[4,128,256]{2,1,0:T(8,128)S(1)} %fusion.48), channel_id=1, source_target_pairs={{1,0},{2,1},{3,2},{4,3},{5,4},{6,5},{7,6},{8,7},{9,8},{10,9},{11,1... | collective-permute-start | bytes 1572872 | tf_op jit(solution)/shard_map/ppermute | solution.py:19
  345.4 11.2 %collective-permute-start.8 = (f32[4,128,256]{2,1,0:T(8,128)S(1)}, f32[4,128,256]{2,1,0:T(8,128)S(1)}, u32[]{:S(2)}, u32[]{:S(2)}) collective-permute-start(f32[4,128,256]{2,1,0:T(8,128)S(1)} %fusion.48), channel_id=1, source_target_pairs={{0,1},{1,2},{2,3},{3,4},{4,5},{5,6},{6,7},{7,8},{8,9},{9,10},{10,1... | collective-permute-start | bytes 1572872 | tf_op jit(solution)/shard_map/ppermute | solution.py:16
  366.8 16.4 %collective-permute-start.12 = (f32[4,128,256]{2,1,0:T(8,128)S(1)}, f32[4,128,256]{2,1,0:T(8,128)S(1)}, u32[]{:S(2)}, u32[]{:S(2)}) collective-permute-start(f32[4,128,256]{2,1,0:T(8,128)S(1)} %reshape.302), channel_id=1, source_target_pairs={{0,1},{1,2},{2,3},{3,4},{4,5},{5,6},{6,7},{7,8},{8,9},{9,10},{10,1... | collective-permute-start | bytes 1572872 | tf_op jit(solution)/shard_map/ppermute | solution.py:16
  371.2 14.9 %collective-permute-start.11 = (f32[4,128,256]{2,1,0:T(8,128)S(1)}, f32[4,128,256]{2,1,0:T(8,128)S(1)}, u32[]{:S(2)}, u32[]{:S(2)}) collective-permute-start(f32[4,128,256]{2,1,0:T(8,128)S(1)} %reshape.302), channel_id=1, source_target_pairs={{1,0},{2,1},{3,2},{4,3},{5,4},{6,5},{7,6},{8,7},{9,8},{10,9},{11,1... | collective-permute-start | bytes 1572872 | tf_op jit(solution)/shard_map/ppermute | solution.py:19
  372.5 29.1 %collective-permute-start.5 = (f32[4,128,256]{2,1,0:T(8,128)}, f32[4,128,256]{2,1,0:T(8,128)}, u32[]{:S(2)}, u32[]{:S(2)}) collective-permute-start(f32[4,128,256]{2,1,0:T(8,128)} %bitcast.110), channel_id=1, source_target_pairs={{1,0},{2,1},{3,2},{4,3},{5,4},{6,5},{7,6},{8,7},{9,8},{10,9},{11,1... | collective-permute-start | bytes 1572872 | tf_op jit(solution)/shard_map/ppermute | solution.py:19
  373.8 27.9 %collective-permute-start.6 = (f32[4,128,256]{2,1,0:T(8,128)}, f32[4,128,256]{2,1,0:T(8,128)}, u32[]{:S(2)}, u32[]{:S(2)}) collective-permute-start(f32[4,128,256]{2,1,0:T(8,128)} %bitcast.111), channel_id=1, source_target_pairs={{0,1},{1,2},{2,3},{3,4},{4,5},{5,6},{6,7},{7,8},{8,9},{9,10},{10,1... | collective-permute-start | bytes 1572872 | tf_op jit(solution)/shard_map/ppermute | solution.py:16
  393.6 12.5 %collective-permute-start.14 = (f32[4,128,256]{2,1,0:T(8,128)}, f32[4,128,256]{2,1,0:T(8,128)S(1)}, u32[]{:S(2)}, u32[]{:S(2)}) collective-permute-start(f32[4,128,256]{2,1,0:T(8,128)} %reshape.304), channel_id=1, source_target_pairs={{0,1},{1,2},{2,3},{3,4},{4,5},{5,6},{6,7},{7,8},{8,9},{9,10},{10,1... | collective-permute-start | bytes 1572872 | tf_op jit(solution)/shard_map/ppermute | solution.py:16
  400.4 13.5 %collective-permute-start.13 = (f32[4,128,256]{2,1,0:T(8,128)}, f32[4,128,256]{2,1,0:T(8,128)S(1)}, u32[]{:S(2)}, u32[]{:S(2)}) collective-permute-start(f32[4,128,256]{2,1,0:T(8,128)} %reshape.304), channel_id=1, source_target_pairs={{1,0},{2,1},{3,2},{4,3},{5,4},{6,5},{7,6},{8,7},{9,8},{10,9},{11,1... | collective-permute-start | bytes 1572872 | tf_op jit(solution)/shard_map/ppermute | solution.py:19
  425.6 37.0 %collective-permute-start.16 = (f32[4,128,256]{2,1,0:T(8,128)}, f32[4,128,256]{2,1,0:T(8,128)}, u32[]{:S(2)}, u32[]{:S(2)}) collective-permute-start(f32[4,128,256]{2,1,0:T(8,128)} %reshape.306), channel_id=1, source_target_pairs={{0,1},{1,2},{2,3},{3,4},{4,5},{5,6},{6,7},{7,8},{8,9},{9,10},{10,1... | collective-permute-start | bytes 1572872 | tf_op jit(solution)/shard_map/ppermute | solution.py:16
  432.1 31.6 %collective-permute-start.15 = (f32[4,128,256]{2,1,0:T(8,128)}, f32[4,128,256]{2,1,0:T(8,128)}, u32[]{:S(2)}, u32[]{:S(2)}) collective-permute-start(f32[4,128,256]{2,1,0:T(8,128)} %reshape.306), channel_id=1, source_target_pairs={{1,0},{2,1},{3,2},{4,3},{5,4},{6,5},{7,6},{8,7},{9,8},{10,9},{11,1... | collective-permute-start | bytes 1572872 | tf_op jit(solution)/shard_map/ppermute | solution.py:19
  466.9 99.2 %copy-start.39 = (s32[256,1]{0,1:T(1,128)S(1)}, s32[256,1]{0,1:T(1,128)}, u32[]{:S(2)}) copy-start(s32[256,1]{0,1:T(1,128)} %copy-done.38) | copy-start | bytes 3076
  568.7 11.4 %collective-permute-start.18 = (f32[4,128,256]{2,1,0:T(8,128)S(1)}, f32[4,128,256]{2,1,0:T(8,128)S(1)}, u32[]{:S(2)}, u32[]{:S(2)}) collective-permute-start(f32[4,128,256]{2,1,0:T(8,128)S(1)} %reshape.312), channel_id=1, source_target_pairs={{0,1},{1,2},{2,3},{3,4},{4,5},{5,6},{6,7},{7,8},{8,9},{9,10},{10,1... | collective-permute-start | bytes 1572872 | tf_op jit(solution)/shard_map/ppermute | solution.py:16
  570.2 14.1 %collective-permute-start.17 = (f32[4,128,256]{2,1,0:T(8,128)S(1)}, f32[4,128,256]{2,1,0:T(8,128)S(1)}, u32[]{:S(2)}, u32[]{:S(2)}) collective-permute-start(f32[4,128,256]{2,1,0:T(8,128)S(1)} %reshape.312), channel_id=1, source_target_pairs={{1,0},{2,1},{3,2},{4,3},{5,4},{6,5},{7,6},{8,7},{9,8},{10,9},{11,1... | collective-permute-start | bytes 1572872 | tf_op jit(solution)/shard_map/ppermute | solution.py:19
  594.8 12.2 %collective-permute-start.20 = (f32[4,128,256]{2,1,0:T(8,128)S(1)}, f32[4,128,256]{2,1,0:T(8,128)S(1)}, u32[]{:S(2)}, u32[]{:S(2)}) collective-permute-start(f32[4,128,256]{2,1,0:T(8,128)S(1)} %reshape.316), channel_id=1, source_target_pairs={{0,1},{1,2},{2,3},{3,4},{4,5},{5,6},{6,7},{7,8},{8,9},{9,10},{10,1... | collective-permute-start | bytes 1572872 | tf_op jit(solution)/shard_map/ppermute | solution.py:16
  596.9 15.0 %collective-permute-start.19 = (f32[4,128,256]{2,1,0:T(8,128)S(1)}, f32[4,128,256]{2,1,0:T(8,128)S(1)}, u32[]{:S(2)}, u32[]{:S(2)}) collective-permute-start(f32[4,128,256]{2,1,0:T(8,128)S(1)} %reshape.316), channel_id=1, source_target_pairs={{1,0},{2,1},{3,2},{4,3},{5,4},{6,5},{7,6},{8,7},{9,8},{10,9},{11,1... | collective-permute-start | bytes 1572872 | tf_op jit(solution)/shard_map/ppermute | solution.py:19
  623.1 14.1 %collective-permute-start.22 = (f32[4,128,256]{2,1,0:T(8,128)}, f32[4,128,256]{2,1,0:T(8,128)}, u32[]{:S(2)}, u32[]{:S(2)}) collective-permute-start(f32[4,128,256]{2,1,0:T(8,128)} %reshape.319), channel_id=1, source_target_pairs={{0,1},{1,2},{2,3},{3,4},{4,5},{5,6},{6,7},{7,8},{8,9},{9,10},{10,1... | collective-permute-start | bytes 1572872 | tf_op jit(solution)/shard_map/ppermute | solution.py:16
  625.3 13.1 %collective-permute-start.21 = (f32[4,128,256]{2,1,0:T(8,128)}, f32[4,128,256]{2,1,0:T(8,128)}, u32[]{:S(2)}, u32[]{:S(2)}) collective-permute-start(f32[4,128,256]{2,1,0:T(8,128)} %reshape.319), channel_id=1, source_target_pairs={{1,0},{2,1},{3,2},{4,3},{5,4},{6,5},{7,6},{8,7},{9,8},{10,9},{11,1... | collective-permute-start | bytes 1572872 | tf_op jit(solution)/shard_map/ppermute | solution.py:19
  650.6 24.6 %collective-permute-start.23 = (f32[2,4,128,256]{3,2,1,0:T(8,128)S(1)}, f32[2,4,128,256]{3,2,1,0:T(8,128)S(1)}, u32[]{:S(2)}, u32[]{:S(2)}) collective-permute-start(f32[2,4,128,256]{3,2,1,0:T(8,128)S(1)} %stack.44), channel_id=1, source_target_pairs={{0,1},{1,2},{2,3},{3,4},{4,5},{5,6},{6,7},{7,8},{8,9},{9,10},{10,1... | collective-permute-start | bytes 3145736 | tf_op jit(solution)/shard_map/ppermute | solution.py:27
  675.3 21.1 %collective-permute-start.24 = (f32[2,4,128,256]{3,2,1,0:T(8,128)S(1)}, f32[2,4,128,256]{3,2,1,0:T(8,128)}, u32[]{:S(2)}, u32[]{:S(2)}) collective-permute-start(f32[2,4,128,256]{3,2,1,0:T(8,128)S(1)} %fusion.8), channel_id=1, source_target_pairs={{0,2},{1,3},{2,4},{3,5},{4,6},{5,7},{6,8},{7,9},{8,10},{9,11},{10,... | collective-permute-start | bytes 3145736 | tf_op jit(solution)/shard_map/ppermute | solution.py:27
  698.2 23.5 %collective-permute-start.25 = (f32[2,4,128,256]{3,2,1,0:T(8,128)S(1)}, f32[2,4,128,256]{3,2,1,0:T(8,128)}, u32[]{:S(2)}, u32[]{:S(2)}) collective-permute-start(f32[2,4,128,256]{3,2,1,0:T(8,128)S(1)} %fusion.9), channel_id=1, source_target_pairs={{0,4},{1,5},{2,6},{3,7},{4,8},{5,9},{6,10},{7,11},{8,12},{9,13},{1... | collective-permute-start | bytes 3145736 | tf_op jit(solution)/shard_map/ppermute | solution.py:27
  723.6 45.0 %collective-permute-start.26 = (f32[2,4,128,256]{3,2,1,0:T(8,128)S(1)}, f32[2,4,128,256]{3,2,1,0:T(8,128)S(1)}, u32[]{:S(2)}, u32[]{:S(2)}) collective-permute-start(f32[2,4,128,256]{3,2,1,0:T(8,128)S(1)} %fusion.10), channel_id=1, source_target_pairs={{0,8},{1,9},{2,10},{3,11},{4,12},{5,13},{6,14},{7,15},{8,16},{9,17... | collective-permute-start | bytes 3145736 | tf_op jit(solution)/shard_map/ppermute | solution.py:27
  770.0 44.9 %collective-permute-start.27 = (f32[2,4,128,256]{3,2,1,0:T(8,128)S(1)}, f32[2,4,128,256]{3,2,1,0:T(8,128)S(1)}, u32[]{:S(2)}, u32[]{:S(2)}) collective-permute-start(f32[2,4,128,256]{3,2,1,0:T(8,128)S(1)} %fusion.11), channel_id=1, source_target_pairs={{0,16},{1,17},{2,18},{3,19},{4,20},{5,21},{6,22},{7,23},{8,24},{9,... | collective-permute-start | bytes 3145736 | tf_op jit(solution)/shard_map/ppermute | solution.py:27
  (44 other events, 681.7 us)
Sparse Core Ops, SparseCore 0:
  9.7 31.3 all-gather.2
  42.7 29.9 all-gather.4
  816.9 30.0 reduce-scatter.1
where the time goes:
time: 866 us; the launch traced here: 854 us
  waiting for transfers between devices  464 us (54%)
  starting transfers between devices  122 us (14%)
  other arithmetic  91.9 us (11%)
  blocking collectives  91.3 us (11%)
  local copies, waits for them, and re-layouts  66.8 us (8%)
  between operations  17.3 us (2%)
    ppermute x10, waiting for transfers between devices, passed_along(): return lax.ppermute(value, axis, pairs)  326 us
    psum x1, blocking collectives, on_device(): sampled = lax.psum(sampled, 'sub')  91.3 us
    ppermute x10, starting transfers between devices, passed_along(): return lax.ppermute(value, axis, pairs)  70.6 us
    ppermute x9, starting transfers between devices, with_halo(): lax.ppermute(lax.slice_in_dim(block, block.shape[dim] - width, None, axis...  39.8 us
    all_gather x1, waiting for transfers between devices, on_device(): lax.all_gather(velocity, 'shot', axis=0, tiled=True)  31.7 us
    add x8, other arithmetic, advance(): return 2.0 * current - previous + speed_sq * operator  31.4 us
    all_gather x1, waiting for transfers between devices, on_device(): lax.all_gather(density, 'shot', axis=0, tiled=True)  30.3 us
    reduce_scatter x1, waiting for transfers between devices, on_device(): lax.psum_scatter(jnp.concatenate(pieces, 0), 'shot', scatter_dimension=0,...  30.3 us
  transfers between devices with their start and end apart: 31, of which 24 were waited for; matrix products, arithmetic and copies ran while one was open for 7% of the time, Pallas kernels for 0%

commit v1 on v0

v1 whole, which is shorter than its diff:
```python
import functools

import jax
import jax.numpy as jnp
from jax import lax
from jax.experimental import pallas as pl
from jax.experimental.pallas import tpu as pltpu
from jax.sharding import PartitionSpec as P

lap_coeffs = (-205.0 / 72.0, 8.0 / 5.0, -1.0 / 5.0, 8.0 / 315.0, -1.0 / 560.0)
diff_coeffs = (4.0 / 5.0, -1.0 / 5.0, 4.0 / 105.0, -1.0 / 280.0)
time_step_sq = 0.0088

ROWS = 16
CELLS = 32
NZ = 256
F32 = jnp.float32


def pairs_by(move):
    pairs = []
    for shot in range(4):
        for sub in range(32):
            x = 2 * (sub // 16) + shot // 2
            target = move(x, shot % 2, (sub // 4) % 4, sub % 4)
            if target is None:
                continue
            tx, tcore, tz, ty = target
            pairs.append((shot * 32 + sub, ((tx % 2) * 2 + tcore) * 32 + (tx // 2) * 16 + tz * 4 + ty))
    return pairs


def send(value, move):
    return lax.ppermute(value, ("shot", "sub"), pairs_by(move))


def send_x(value, steps):
    return send(value, lambda x, c, z, y: ((x + steps) % 4, c, z, y))


def send_core(value):
    return send(value, lambda x, c, z, y: (x, 1 - c, z, y))


def send_z(value, steps):
    return send(value, lambda x, c, z, y: (x, c, (z + steps) % 4, y))


def send_y(value, steps):
    return send(value, lambda x, c, z, y: (x, c, z, (y + steps) % 4))


def next_rows(x, z, steps):
    group = (x // 2) * 4 + z + steps
    if group < 0 or group > 7:
        return None
    return (2 * (group // 4) + x % 2, group % 4)


def send_group(value, steps):
    def move(x, c, z, y):
        place = next_rows(x, z, steps)
        return None if place is None else (place[0], c, place[1], y)

    return send(value, move)


def send_cells(value, steps):
    return send(value, lambda x, c, z, y: (x, c, z, y + steps) if 0 <= y + steps < 4 else None)


def swap_edges(edges):
    low_rows, high_rows, low_cells, high_cells = edges
    return (
        send_group(high_rows, 1),
        send_group(low_rows, -1),
        send_cells(high_cells, 1),
        send_cells(low_cells, -1),
    )


VMEM = pltpu.VMEM
SMEM = pltpu.SMEM


def block_shape():
    return jax.ShapeDtypeStruct((ROWS, CELLS, NZ), F32)


def edge_shapes():
    rows = jax.ShapeDtypeStruct((4, CELLS, NZ), F32)
    cells = jax.ShapeDtypeStruct((ROWS, 8, NZ), F32)
    return (rows, rows, cells, cells)


def call(body, outs, n_smem, operands, scratch=()):
    specs = [pl.BlockSpec(memory_space=SMEM)] * n_smem
    specs += [pl.BlockSpec(memory_space=VMEM)] * (len(operands) - n_smem)
    return pl.pallas_call(
        body,
        out_shape=outs,
        in_specs=specs,
        out_specs=tuple(pl.BlockSpec(memory_space=VMEM) for _ in outs),
        scratch_shapes=list(scratch),
    )(*operands)


def write_edges(block, edges):
    low_rows, high_rows, low_cells, high_cells = edges
    low_rows[...] = block[0:4]
    high_rows[...] = block[ROWS - 4 : ROWS]
    low_cells[...] = block[:, 0:8, :]
    high_cells[...] = block[:, CELLS - 8 : CELLS, :]


def fill_padded(padded, block, halo):
    below, above, left, right = halo
    padded[0:4, 8 : 8 + CELLS, :] = below[...]
    padded[4 : 4 + ROWS, 8 : 8 + CELLS, :] = block[...]
    padded[4 + ROWS : 8 + ROWS, 8 : 8 + CELLS, :] = above[...]
    padded[4 : 4 + ROWS, 0:8, :] = left[...]
    padded[4 : 4 + ROWS, 8 + CELLS : 16 + CELLS, :] = right[...]


PADDED = pltpu.VMEM((ROWS + 8, CELLS + 16, NZ), F32)


def z_shifted(value, lane, reach):
    ahead = jnp.where(lane < NZ - reach, pltpu.roll(value, NZ - reach, 1), 0.0)
    behind = jnp.where(lane >= reach, pltpu.roll(value, reach, 1), 0.0)
    return ahead, behind


def views(padded, row, direction, reach, lane):
    if direction == 0:
        return (
            padded[row + 4 + reach, 8 : 8 + CELLS, :],
            padded[row + 4 - reach, 8 : 8 + CELLS, :],
        )
    if direction == 1:
        return (
            padded[row + 4, 8 + reach : 8 + CELLS + reach, :],
            padded[row + 4, 8 - reach : 8 + CELLS - reach, :],
        )
    return z_shifted(padded[row + 4, 8 : 8 + CELLS, :], lane, reach)


def operator_row(padded, row, slopes, lane):
    center = padded[row + 4, 8 : 8 + CELLS, :]
    result = (3.0 * lap_coeffs[0]) * center
    for direction in range(3):
        derived = None
        for reach in range(1, 5):
            ahead, behind = views(padded, row, direction, reach, lane)
            result = result + lap_coeffs[reach] * (ahead + behind)
            part = diff_coeffs[reach - 1] * (ahead - behind)
            derived = part if derived is None else derived + part
        result = result - slopes[direction][row] * derived
    return center, result


def lanes():
    return lax.broadcasted_iota(jnp.int32, (CELLS, NZ), 1)


def assemble_body(slots, *refs, fields):
    pieces = refs[:4]
    blocks = refs[4 : 4 + fields]
    edges = refs[4 + fields :]
    for turn in range(4):
        slot = slots[turn]
        for index in range(fields):
            blocks[index][pl.ds(slot * 4, 4)] = pieces[turn][index]
    write_edges(blocks[0], edges)


def assemble(pieces, slots, fields):
    outs = (block_shape(),) * fields + edge_shapes()
    result = call(
        functools.partial(assemble_body, fields=fields), outs, 1, (slots, *pieces)
    )
    return result[:fields], result[fields:]


def model_body(slots, p0, p1, p2, p3, log_mass, h0, h1, h2, h3, speed_sq, twice, s0, s1, s2, padded):
    fill_padded(padded, log_mass, (h0, h1, h2, h3))
    for turn, piece in enumerate((p0, p1, p2, p3)):
        slot = slots[turn]
        speed = piece[0]
        speed_sq[pl.ds(slot * 4, 4)] = time_step_sq * speed * speed
        twice[pl.ds(slot * 4, 4)] = 2.0 / speed
    lane = lanes()

    def step(row, carry):
        for direction, out in enumerate((s0, s1, s2)):
            derived = None
            for reach in range(1, 5):
                ahead, behind = views(padded, row, direction, reach, lane)
                part = diff_coeffs[reach - 1] * (ahead - behind)
                derived = part if derived is None else derived + part
            out[row] = derived
        return carry

    lax.fori_loop(0, ROWS, step, 0)


def forward_body(place, amount, now, h0, h1, h2, h3, old, speed_sq, s0, s1, s2, new, e0, e1, e2, e3, padded, *, index):
    fill_padded(padded, now, (h0, h1, h2, h3))
    lane = lanes()

    def step(row, carry):
        center, result = operator_row(padded, row, (s0, s1, s2), lane)
        new[row] = 2.0 * center - old[row] + speed_sq[row] * result
        return carry

    lax.fori_loop(0, ROWS, step, 0)

    @pl.when(place[0] > 0)
    def _():
        cell = lax.broadcasted_iota(jnp.int32, (CELLS, NZ), 0)
        hit = (cell == place[2]) & (lane == place[3])
        new[place[1]] = new[place[1]] + jnp.where(hit, amount[index], 0.0)

    write_edges(new, (e0, e1, e2, e3))


def adjoint_body(now, h0, h1, h2, h3, later, speed_sq, s0, s1, s2, hits, seen, u_next, u_here, u_before, *rest, first, last):
    rest = list(rest)
    sums = None if first else rest.pop(0)
    twice = rest.pop(0) if last else None
    new, summed = rest.pop(0), rest.pop(0)
    padded = rest.pop()
    fill_padded(padded, now, (h0, h1, h2, h3))
    lane = lanes()

    def step(row, carry):
        center, result = operator_row(padded, row, (s0, s1, s2), lane)
        ahead = u_next[row]
        value = 2.0 * center - later[row] + speed_sq[row] * result
        value = value + (hits[row] * ahead - seen[row])
        new[row] = value
        total = value * (ahead - 2.0 * u_here[row] + u_before[row])
        if sums is not None:
            total = sums[row] + total
        if twice is not None:
            total = twice[row] * total
        summed[row] = total
        return carry

    lax.fori_loop(0, ROWS, step, 0)
    if rest:
        write_edges(new, rest)


def spread_body(chunks, *refs, fields):
    pieces = refs[:4]
    outs = refs[4:]
    for turn in range(4):
        first = pl.multiple_of(chunks[turn] * CELLS, CELLS)
        for index in range(fields):
            outs[index][:, pl.ds(first, CELLS), :] = pieces[turn][index]


def spread(pieces, chunks, fields):
    outs = (jax.ShapeDtypeStruct((4, 4 * CELLS, NZ), F32),) * fields
    return call(functools.partial(spread_body, fields=fields), outs, 1, (chunks, *pieces))


def to_blocks(slabs, y):
    pieces = []
    for turn in range(4):
        first = ((y + turn) % 4) * CELLS
        cut = jnp.stack([lax.dynamic_slice_in_dim(slab, first, CELLS, 1) for slab in slabs])
        pieces.append(send_y(cut, turn) if turn else cut)
    return pieces


def to_slabs(blocks, y, shifts):
    pieces = []
    for turn in range(4):
        cut = jnp.stack(
            [
                lax.dynamic_slice_in_dim(block, ((y + turn - shift) % 4) * 4, 4, 0)
                for block, shift in zip(blocks, shifts)
            ]
        )
        pieces.append(send_y(cut, turn) if turn else cut)
    return pieces


def on_device(
    velocity,
    density,
    aperture_start,
    source_cell,
    receiver_cells,
    wavelet,
    observed,
    forward_old,
    forward_now,
    adjoint_later,
    adjoint_now,
):
    shot = lax.axis_index("shot")
    sub = lax.axis_index("sub")
    core = shot % 2
    x_hi = sub // 16
    x = 2 * x_hi + shot // 2
    z = (sub // 4) % 4
    y = sub % 4
    start = aperture_start[0]
    partner_start = send_core(aperture_start)[0]

    def wanted(first_slab):
        upper = first_slab // 4 + (y < first_slab % 4).astype(jnp.int32)
        block = jnp.clip(x_hi + (upper - z + 3) // 4, 0, 7)
        position = 2 * (block % 2) + block // 4
        return (block // 2) % 2, (position - x) % 4, upper % 4

    own_core, own_step, turn_by = wanted(start)
    pair_core, pair_step, _ = wanted(partner_start)
    low = turn_by % 2 == 1
    high = turn_by // 2 == 1
    high_back = ((turn_by + 1) // 2) % 2 == 1
    high_other = jnp.where(low, high_back, high)
    turns = jnp.arange(4, dtype=jnp.int32)
    plain_slots = (y - turns) % 4
    model_slots = (y - turns - start % 4) % 4

    def gathered(slab):
        from_below = send_x(slab, 1)
        from_above = send_x(slab, -1)
        far = jnp.concatenate([send_x(from_below[0:2], 1), send_x(from_above[2:4], -1)])

        def pick(step):
            return jnp.where(
                step < 2, jnp.where(step == 0, slab, from_above), jnp.where(step == 2, far, from_below)
            )

        other = send_core(pick(pair_step))
        return jnp.where(own_core == core, pick(own_step), other)

    def turned(slab, direction, high_bit):
        slab = jnp.where(low, send_z(slab, direction), slab)
        return jnp.where(high_bit, send_z(slab, 2), slab)

    log_slab = turned(gathered(jnp.log(density)), -1, high)
    speed_slab = turned(gathered(velocity), 1, high_other)

    (u_now, u_old), u_edges = assemble(to_blocks([forward_now[0], forward_old[0]], y), plain_slots, 2)
    (a_now, a_later), a_edges = assemble(to_blocks([adjoint_now[0], adjoint_later[0]], y), plain_slots, 2)
    u_halo = swap_edges(u_edges)
    a_halo = swap_edges(a_edges)

    group = sub // 4

    def local_place(cells):
        rows = cells // (4 * CELLS * NZ) - group * ROWS
        columns = (cells // NZ) % (4 * CELLS) - y * CELLS
        inside = (rows >= 0) & (rows < ROWS) & (columns >= 0) & (columns < CELLS)
        return inside, rows, columns, cells % NZ

    inside, rows, columns, depth = local_place(receiver_cells[0])
    line = jnp.where(inside, rows * CELLS + columns, -1)
    on_line = (jnp.arange(ROWS * CELLS)[:, None] == line[None, :]).astype(F32)
    weights = jnp.concatenate([jnp.ones_like(observed[0, :1]), observed[0]])
    at_depth = jnp.where(depth[None, :, None] == jnp.arange(NZ)[None, None, :], weights[:, :, None], 0.0)
    maps = jnp.einsum("lr,krz->klz", on_line, at_depth, precision=lax.Precision.HIGHEST)
    maps = maps.reshape(5, ROWS, CELLS, NZ)

    s_inside, s_row, s_column, s_depth = local_place(source_cell[0])
    place = jnp.stack(
        [
            s_inside.astype(jnp.int32),
            jnp.clip(s_row, 0, ROWS - 1),
            s_column,
            s_depth,
        ]
    )
    amount = wavelet[0]

    (log_block,), log_edges = assemble(to_blocks([log_slab], y), model_slots, 1)
    log_halo = swap_edges(log_edges)
    speed_pieces = to_blocks([speed_slab], y)
    speed_sq, twice, s0, s1, s2 = call(
        model_body,
        (block_shape(),) * 5,
        1,
        (model_slots, *speed_pieces, log_block, *log_halo),
        (PADDED,),
    )
    model = (speed_sq, s0, s1, s2)

    fields = [u_old, u_now]
    halo = u_halo
    for index in range(4):
        new, *edges = call(
            functools.partial(forward_body, index=index),
            (block_shape(), *edge_shapes()),
            2,
            (place, amount, fields[-1], *halo, fields[-2], *model),
            (PADDED,),
        )
        fields.append(new)
        if index < 3:
            halo = swap_edges(edges)

    current, later = a_now, a_later
    halo = a_halo
    summed = None
    for index in reversed(range(4)):
        first, last = index == 3, index == 0
        operands = (current, *halo, later, *model, maps[0], maps[index + 1])
        operands += (fields[index + 2], fields[index + 1], fields[index])
        if not first:
            operands += (summed,)
        if last:
            operands += (twice,)
        outs = (block_shape(), block_shape()) + (() if last else edge_shapes())
        new, summed, *edges = call(
            functools.partial(adjoint_body, first=first, last=last), outs, 0, operands, (PADDED,)
        )
        later, current = current, new
        if not last:
            halo = swap_edges(edges)

    oy = start % 4
    (forward_last,) = spread(to_slabs([fields[-1]], y, (0,)), plain_slots, 1)
    adjoint_first, image = spread(to_slabs([current, summed], y, (0, oy)), plain_slots, 2)

    def both(first_half, second_half):
        return jnp.concatenate([first_half, second_half])

    image = jnp.where(low, both(send_z(image[0:2], 1), send_z(image[2:4], -1)), image)
    arrived = send_z(image, 2)
    image = both(
        jnp.where(high, arrived[0:2], image[0:2]),
        jnp.where(high_other, arrived[2:4], image[2:4]),
    )
    other = send_core(image)

    def share(step):
        mine = jnp.where((own_core == core) & (own_step == step), image, 0.0)
        return mine + jnp.where((pair_core == core) & (pair_step == step), other, 0.0)

    far = share(2)
    passing_up = send_x(far[0:2], 1)
    passing_down = send_x(far[2:4], -1)
    up = share(1)
    down = share(3)
    up = send_x(both(up[0:2] + passing_up, up[2:4]), 1)
    down = send_x(both(down[0:2], down[2:4] + passing_down), -1)
    gradient = share(0) + up + down
    return (gradient, forward_last[None], adjoint_first[None])


def solution(mesh):
    placed = (
        P(("shot", "sub"), None, None),
        P(("shot", "sub"), None, None),
        P("shot"),
        P("shot"),
        P("shot", None),
        P("shot", None),
        P("shot", None, None),
        P("shot", "sub", None, None),
        P("shot", "sub", None, None),
        P("shot", "sub", None, None),
        P("shot", "sub", None, None),
    )
    return jax.shard_map(
        on_device,
        mesh=mesh,
        in_specs=placed,
        out_specs=(
            P(("shot", "sub"), None, None),
            P("shot", "sub", None, None),
            P("shot", "sub", None, None),
        ),
        check_vma=False,
    )
```

time: 866 us -> 414 us (0.48); the launches traced: 854 us -> 412 us
  waiting for transfers between devices: 464 us -> 122 us
  blocking collectives: 91.3 us -> 0 us
  other arithmetic: 91.9 us -> 12.1 us
  Pallas kernels: 0 us -> 65.3 us
  starting transfers between devices: 122 us -> 180 us
  local copies, waits for them, and re-layouts: 66.8 us -> 25.2 us
  between operations: 17.3 us -> 5.93 us
    ppermute x28 -> x77, waiting for transfers between devices: 371 us -> 122 us  [send(): return lax.ppermute(value, ('shot', 'sub'), pairs_by(move))]
    psum x1 -> x0, blocking collectives: 91.3 us -> none  [on_device(): sampled = lax.psum(sampled, 'sub')]
    pallas_call x0 -> x14, Pallas kernels: none -> 65.3 us  [call(): pl.pallas_call(body, out_shape=outs, in_specs=specs, out_specs=tuple((pl....]
    all_gather x2 -> x0, waiting for transfers between devices: 62 us -> none  [the longest x1 31.7 us: on_device(): lax.all_gather(velocity, 'shot', axis=0, tiled=True)]
    ppermute x28 -> x77, starting transfers between devices: 122 us -> 180 us  [send(): return lax.ppermute(value, ('shot', 'sub'), pairs_by(move))]
    add x9 -> x3, other arithmetic: 31.7 us -> 1.17 us  [the longest x1 0.93 us: on_device(): gradient = share(0) + up + down]
    reduce_scatter x1 -> x0, waiting for transfers between devices: 30.3 us -> none  [on_device(): lax.psum_scatter(jnp.concatenate(pieces, 0), 'shot', scatter_dimension=0,...]
    gather x4 -> x0, local copies, waits for them, and re-layouts: 24.4 us -> none  [sample_local(): return jnp.where(is_local, field.reshape(-1)[clipped], 0.0)]
  transfers between devices with their start and end apart: 31 -> 77, of which waited for: 24 -> 31; matrix products, arithmetic and copies ran while one was open for 7% -> 6% of each run, Pallas kernels for 0% -> 9%
where the time goes in v1:
time: 414 us; the launch traced here: 412 us
  starting transfers between devices  180 us (43%)
  waiting for transfers between devices  122 us (29%)
  Pallas kernels  65.3 us (16%)
  local copies, waits for them, and re-layouts  25.2 us (6%)
  other arithmetic  12.1 us (3%)
  between operations  5.93 us (1%)
    ppermute x77, starting transfers between devices, send(): return lax.ppermute(value, ('shot', 'sub'), pairs_by(move))  180 us
    ppermute x77, waiting for transfers between devices, send(): return lax.ppermute(value, ('shot', 'sub'), pairs_by(move))  122 us
    pallas_call x14, Pallas kernels, call(): pl.pallas_call(body, out_shape=outs, in_specs=specs, out_specs=tuple((pl....  65.3 us
  transfers between devices with their start and end apart: 77, of which 31 were waited for; matrix products, arithmetic and copies ran while one was open for 6% of the time, Pallas kernels for 9%

profile of v1, /device:TPU:0, one launch (start us, length us, event | category | flops | bytes accessed | tf_op | source)
XLA Modules:
  0.0 412.3 jit_solution(1420626965204484927)
XLA Ops:
  9.1 9.8 %collective-permute-done.19 = f32[4,128,256]{2,1,0:T(8,128)S(1)} collective-permute-done((f32[4,128,256]{2,1,0:T(8,128)}, f32[4,128,256]{2,1,0:T(8,128)S(1)}, u32[]{:S(2)}, u32[]{:S(2)}) %collective-permute-start.19) | collective-permute-done | bytes 524320 | tf_op jit(solution)/shard_map/ppermute | solution.py:34
  49.4 4.0 collective-permute-start.23
  55.1 9.6 %collective-permute-done.23 = f32[4,128,256]{2,1,0:T(8,128)S(1)} collective-permute-done((f32[4,128,256]{2,1,0:T(8,128)}, f32[4,128,256]{2,1,0:T(8,128)S(1)}, u32[]{:S(2)}, u32[]{:S(2)}) %collective-permute-start.23) | collective-permute-done | bytes 524320 | tf_op jit(solution)/shard_map/ppermute | solution.py:34
  70.3 12.0 %collective-permute-done.24 = f32[4,128,256]{2,1,0:T(8,128)S(1)} collective-permute-done((f32[4,128,256]{2,1,0:T(8,128)S(1)}, f32[4,128,256]{2,1,0:T(8,128)S(1)}, u32[]{:S(2)}, u32[]{:S(2)}) %collective-permute-start.24) | collective-permute-done | bytes 524320 | tf_op jit(solution)/shard_map/ppermute | solution.py:34
  83.1 8.2 %collective-permute-done.14 = f32[4,128,256]{2,1,0:T(8,128)S(1)} collective-permute-done((f32[4,128,256]{2,1,0:T(8,128)S(1)}, f32[4,128,256]{2,1,0:T(8,128)S(1)}, u32[]{:S(2)}, u32[]{:S(2)}) %collective-permute-start.14) | collective-permute-done | bytes 524320 | tf_op jit(solution)/shard_map/ppermute | solution.py:34
  117.5 4.6 %collective-permute-start.35 = (f32[4,32,256]{2,1,0:T(8,128)}, f32[4,32,256]{2,1,0:T(8,128)S(1)}, u32[]{:S(2)}, u32[]{:S(2)}) collective-permute-start(f32[4,32,256]{2,1,0:T(8,128)} %get-tuple-element.79), channel_id=1, source_target_pairs={{0,4},{1,5},{2,6},{3,7},{4,8},{5,9},{6,10},{7,11},{8,12},{9,13},{1... | collective-permute-start | bytes 393224 | tf_op jit(solution)/shard_map/ppermute | solution.py:34
  130.5 5.5 %collective-permute-done.31.h3 = f32[16,8,256]{2,1,0:T(8,128)S(1)} collective-permute-done((f32[16,8,256]{2,1,0:T(8,128)S(1)}, f32[16,8,256]{2,1,0:T(8,128)S(1)}, u32[]{:S(2)}, u32[]{:S(2)}) %collective-permute-start.31) | collective-permute-done | bytes 131104 | tf_op jit(solution)/shard_map/ppermute | solution.py:34
  138.1 5.3 %shard_map.132 = (f32[16,32,256]{2,1,0:T(8,128)}, f32[16,32,256]{2,1,0:T(8,128)}, f32[16,32,256]{2,1,0:T(8,128)}, f32[16,32,256]{2,1,0:T(8,128)}, f32[16,32,256]{2,1,0:T(8,128)}) custom-call(s32[4]{0:T(128)} %and_select_fusion.5.slots, f32[1,4,32,256]{3,2,1,0:T(8,128)} %get-tuple-element.168.p0, f32[1,4,32,256]{3,2,1,0:T(8,128)} %copy-done.28, ...), custom_call_target="tpu_custom_call" | custom-call | tf_op jit(solution)/shard_map/pallas_call | solution.py:99
  144.2 5.5 %shard_map.134 = (f32[16,32,256]{2,1,0:T(8,128)}, f32[4,32,256]{2,1,0:T(8,128)}, f32[4,32,256]{2,1,0:T(8,128)}, f32[16,8,256]{2,1,0:T(8,128)}, f32[16,8,256]{2,1,0:T(8,128)}) custom-call(s32[4]{0:T(128)} %pad_add_fusion.place, f32[4]{0:T(128)} %bitcast.80, f32[16,32,256]{2,1,0:T(8,128)} %get-tuple-element.78.now.old.u_before.u_here, ...), custom_call_target="tpu_custom_call" | custom-call | tf_op jit(solution)/shard_map/pallas_call | solution.py:99
  149.7 4.6 %collective-permute-start.39 = (f32[4,32,256]{2,1,0:T(8,128)}, f32[4,32,256]{2,1,0:T(8,128)S(1)}, u32[]{:S(2)}, u32[]{:S(2)}) collective-permute-start(f32[4,32,256]{2,1,0:T(8,128)} %get-tuple-element.85), channel_id=1, source_target_pairs={{0,4},{1,5},{2,6},{3,7},{4,8},{5,9},{6,10},{7,11},{8,12},{9,13},{1... | collective-permute-start | bytes 393224 | tf_op jit(solution)/shard_map/ppermute | solution.py:34
  165.9 5.6 %shard_map.135 = (f32[16,32,256]{2,1,0:T(8,128)}, f32[4,32,256]{2,1,0:T(8,128)}, f32[4,32,256]{2,1,0:T(8,128)}, f32[16,8,256]{2,1,0:T(8,128)}, f32[16,8,256]{2,1,0:T(8,128)}) custom-call(s32[4]{0:T(128)} %pad_add_fusion.place, f32[4]{0:T(128)} %bitcast.81, f32[16,32,256]{2,1,0:T(8,128)} %get-tuple-element.84.now.old.u_before.u_here.u_next, ...), custom_call_target="tpu_custom_call" | custom-call | tf_op jit(solution)/shard_map/pallas_call | solution.py:99
  171.5 4.5 %collective-permute-start.43 = (f32[4,32,256]{2,1,0:T(8,128)}, f32[4,32,256]{2,1,0:T(8,128)S(1)}, u32[]{:S(2)}, u32[]{:S(2)}) collective-permute-start(f32[4,32,256]{2,1,0:T(8,128)} %get-tuple-element.90), channel_id=1, source_target_pairs={{0,4},{1,5},{2,6},{3,7},{4,8},{5,9},{6,10},{7,11},{8,12},{9,13},{1... | collective-permute-start | bytes 393224 | tf_op jit(solution)/shard_map/ppermute | solution.py:34
  181.6 4.5 %collective-permute-start.1 = (f32[2,4,32,256]{3,2,1,0:T(8,128)S(1)}, f32[2,4,32,256]{3,2,1,0:T(8,128)}, u32[]{:S(2)}, u32[]{:S(2)}) collective-permute-start(f32[2,4,32,256]{3,2,1,0:T(8,128)S(1)} %pad_maximum_fusion.5), channel_id=1, source_target_pairs={{0,2},{1,3},{2,0},{3,1},{4,6},{5,7},{6,4},{7,5},{8,10},{9,11},{10,... | collective-permute-start | bytes 786440 | tf_op jit(solution)/shard_map/ppermute | solution.py:34
  187.6 5.6 %shard_map.136 = (f32[16,32,256]{2,1,0:T(8,128)}, f32[4,32,256]{2,1,0:T(8,128)}, f32[4,32,256]{2,1,0:T(8,128)}, f32[16,8,256]{2,1,0:T(8,128)}, f32[16,8,256]{2,1,0:T(8,128)}) custom-call(s32[4]{0:T(128)} %pad_add_fusion.place, f32[4]{0:T(128)} %bitcast.82, f32[16,32,256]{2,1,0:T(8,128)} %get-tuple-element.89.now.old.u_before.u_here.u_next, ...), custom_call_target="tpu_custom_call" | custom-call | tf_op jit(solution)/shard_map/pallas_call | solution.py:99
  193.3 8.5 %collective-permute-start.47 = (f32[4,32,256]{2,1,0:T(8,128)}, f32[4,32,256]{2,1,0:T(8,128)}, u32[]{:S(2)}, u32[]{:S(2)}) collective-permute-start(f32[4,32,256]{2,1,0:T(8,128)} %get-tuple-element.95), channel_id=1, source_target_pairs={{0,4},{1,5},{2,6},{3,7},{4,8},{5,9},{6,10},{7,11},{8,12},{9,13},{1... | collective-permute-start | bytes 393224 | tf_op jit(solution)/shard_map/ppermute | solution.py:34
  210.7 7.5 %collective-permute-start.3 = (f32[4,32,256]{2,1,0:T(8,128)}, f32[4,32,256]{2,1,0:T(8,128)S(1)}, u32[]{:S(2)}, u32[]{:S(2)}) collective-permute-start(f32[4,32,256]{2,1,0:T(8,128)} %get-tuple-element.64), channel_id=1, source_target_pairs={{0,4},{1,5},{2,6},{3,7},{4,8},{5,9},{6,10},{7,11},{8,12},{9,13},{1... | collective-permute-start | bytes 393224 | tf_op jit(solution)/shard_map/ppermute | solution.py:34
  231.3 5.5 %shard_map.137 = (f32[16,32,256]{2,1,0:T(8,128)}, f32[4,32,256]{2,1,0:T(8,128)}, f32[4,32,256]{2,1,0:T(8,128)}, f32[16,8,256]{2,1,0:T(8,128)}, f32[16,8,256]{2,1,0:T(8,128)}) custom-call(s32[4]{0:T(128)} %pad_add_fusion.place, f32[4]{0:T(128)} %bitcast.83, f32[16,32,256]{2,1,0:T(8,128)} %get-tuple-element.94.now.u_here.u_next, ...), custom_call_target="tpu_custom_call" | custom-call | tf_op jit(solution)/shard_map/pallas_call | solution.py:99
  237.6 6.6 %shard_map.138 = (f32[16,32,256]{2,1,0:T(8,128)}, f32[16,32,256]{2,1,0:T(8,128)}, f32[4,32,256]{2,1,0:T(8,128)}, f32[4,32,256]{2,1,0:T(8,128)}, f32[16,8,256]{2,1,0:T(8,128)}, /*index=5*/f32[16,8,256]{2,1,0:T(8,128)}) custom-call(f32[16,32,256]{2,1,0:T(8,128)} %get-tuple-element.63.now.later, f32[4,32,256]{2,1,0:T(8,128)} %copy-done.38, ...), custom_call_target="tpu_custom_call" | custom-call | tf_op jit(solution)/shard_map/pallas_call | solution.py:99
  244.2 8.2 %collective-permute-start.51 = (f32[4,32,256]{2,1,0:T(8,128)}, f32[4,32,256]{2,1,0:T(8,128)S(1)}, u32[]{:S(2)}, u32[]{:S(2)}) collective-permute-start(f32[4,32,256]{2,1,0:T(8,128)} %get-tuple-element.101), channel_id=1, source_target_pairs={{0,4},{1,5},{2,6},{3,7},{4,8},{5,9},{6,10},{7,11},{8,12},{9,13},{1... | collective-permute-start | bytes 393224 | tf_op jit(solution)/shard_map/ppermute | solution.py:34
  253.7 3.9 collective-permute-start.53
  265.3 6.8 %shard_map.139 = (f32[16,32,256]{2,1,0:T(8,128)}, f32[16,32,256]{2,1,0:T(8,128)}, f32[4,32,256]{2,1,0:T(8,128)}, f32[4,32,256]{2,1,0:T(8,128)}, f32[16,8,256]{2,1,0:T(8,128)}, /*index=5*/f32[16,8,256]{2,1,0:T(8,128)}) custom-call(f32[16,32,256]{2,1,0:T(8,128)} %get-tuple-element.100.now.later, f32[4,32,256]{2,1,0:T(8,128)} %copy-done.55, ...), custom_call_target="tpu_custom_call" | custom-call | tf_op jit(solution)/shard_map/pallas_call | solution.py:99
  272.1 8.1 %collective-permute-start.55 = (f32[4,32,256]{2,1,0:T(8,128)}, f32[4,32,256]{2,1,0:T(8,128)S(1)}, u32[]{:S(2)}, u32[]{:S(2)}) collective-permute-start(f32[4,32,256]{2,1,0:T(8,128)} %get-tuple-element.107), channel_id=1, source_target_pairs={{0,4},{1,5},{2,6},{3,7},{4,8},{5,9},{6,10},{7,11},{8,12},{9,13},{1... | collective-permute-start | bytes 393224 | tf_op jit(solution)/shard_map/ppermute | solution.py:34
  292.4 6.7 %shard_map.140 = (f32[16,32,256]{2,1,0:T(8,128)}, f32[16,32,256]{2,1,0:T(8,128)}, f32[4,32,256]{2,1,0:T(8,128)}, f32[4,32,256]{2,1,0:T(8,128)}, f32[16,8,256]{2,1,0:T(8,128)}, /*index=5*/f32[16,8,256]{2,1,0:T(8,128)}) custom-call(f32[16,32,256]{2,1,0:T(8,128)} %get-tuple-element.106.now.later, f32[4,32,256]{2,1,0:T(8,128)} %copy-done.56, ...), custom_call_target="tpu_custom_call" | custom-call | tf_op jit(solution)/shard_map/pallas_call | solution.py:99
  299.1 8.1 %collective-permute-start.59 = (f32[4,32,256]{2,1,0:T(8,128)}, f32[4,32,256]{2,1,0:T(8,128)S(1)}, u32[]{:S(2)}, u32[]{:S(2)}) collective-permute-start(f32[4,32,256]{2,1,0:T(8,128)} %get-tuple-element.113), channel_id=1, source_target_pairs={{0,4},{1,5},{2,6},{3,7},{4,8},{5,9},{6,10},{7,11},{8,12},{9,13},{1... | collective-permute-start | bytes 393224 | tf_op jit(solution)/shard_map/ppermute | solution.py:34
  313.6 4.4 %collective-permute-done.60.h1 = f32[4,32,256]{2,1,0:T(8,128)S(1)} collective-permute-done((f32[4,32,256]{2,1,0:T(8,128)}, f32[4,32,256]{2,1,0:T(8,128)S(1)}, u32[]{:S(2)}, u32[]{:S(2)}) %collective-permute-start.60) | collective-permute-done | bytes 131104 | tf_op jit(solution)/shard_map/ppermute | solution.py:34
  320.4 6.8 %shard_map.141 = (f32[16,32,256]{2,1,0:T(8,128)}, f32[16,32,256]{2,1,0:T(8,128)}) custom-call(f32[16,32,256]{2,1,0:T(8,128)} %get-tuple-element.112.now, f32[4,32,256]{2,1,0:T(8,128)} %copy-done.24, f32[4,32,256]{2,1,0:T(8,128)} %copy-done.25, f32[16,8,256]{2,1,0:T(8,128)} %copy-done.26, f32[16,8,256]{2,1,0:T(8,128)} %copy-done.27, ...), custom_call_target="tpu_custom_call" | custom-call | tf_op jit(solution)/shard_map/pallas_call | solution.py:99
  332.7 6.2 %collective-permute-done.63.refs_1_ = f32[2,4,32,256]{3,2,1,0:T(8,128)S(1)} collective-permute-done((f32[2,4,32,256]{3,2,1,0:T(8,128)S(1)}, f32[2,4,32,256]{3,2,1,0:T(8,128)S(1)}, u32[]{:S(2)}, u32[]{:S(2)}) %collective-permute-start.63) | collective-permute-done | bytes 262176 | tf_op jit(solution)/shard_map/ppermute | solution.py:34
  344.0 15.8 %collective-permute-start.67 = (f32[2,128,256]{2,1,0:T(8,128)S(1)}, f32[2,128,256]{2,1,0:T(8,128)S(1)}, u32[]{:S(2)}, u32[]{:S(2)}) collective-permute-start(f32[2,128,256]{2,1,0:T(8,128)S(1)} %get-tuple-element.144), channel_id=1, source_target_pairs={{0,12},{1,13},{2,14},{3,15},{4,0},{5,1},{6,2},{7,3},{8,4},{9,5},{1... | collective-permute-start | bytes 786440 | tf_op jit(solution)/shard_map/ppermute | solution.py:34
  367.6 10.7 %collective-permute-done.68 = f32[4,128,256]{2,1,0:T(8,128)S(1)} collective-permute-done((f32[4,128,256]{2,1,0:T(8,128)S(1)}, f32[4,128,256]{2,1,0:T(8,128)S(1)}, u32[]{:S(2)}, u32[]{:S(2)}) %collective-permute-start.68) | collective-permute-done | bytes 524320 | tf_op jit(solution)/shard_map/ppermute | solution.py:34
  380.6 6.8 %collective-permute-start.72 = (f32[2,128,256]{2,1,0:T(8,128)S(1)}, f32[2,128,256]{2,1,0:T(8,128)S(1)}, u32[]{:S(2)}, u32[]{:S(2)}) collective-permute-start(f32[2,128,256]{2,1,0:T(8,128)S(1)} %get-tuple-element.140), channel_id=1, source_target_pairs={{0,80},{1,81},{2,82},{3,83},{4,84},{5,85},{6,86},{7,87},{8,88},{9,... | collective-permute-start | bytes 786440 | tf_op jit(solution)/shard_map/ppermute | solution.py:34
  387.4 5.9 %collective-permute-done.72 = f32[2,128,256]{2,1,0:T(8,128)S(1)} collective-permute-done((f32[2,128,256]{2,1,0:T(8,128)S(1)}, f32[2,128,256]{2,1,0:T(8,128)S(1)}, u32[]{:S(2)}, u32[]{:S(2)}) %collective-permute-start.72) | collective-permute-done | bytes 262176 | tf_op jit(solution)/shard_map/ppermute | solution.py:34
  398.3 3.9 collective-permute-start.75
  (329 shorter events, 186.8 us)
Async XLA Ops:
  2.6 16.3 %collective-permute-start.19 = (f32[4,128,256]{2,1,0:T(8,128)}, f32[4,128,256]{2,1,0:T(8,128)S(1)}, u32[]{:S(2)}, u32[]{:S(2)}) collective-permute-start(f32[4,128,256]{2,1,0:T(8,128)} %log.3), channel_id=1, source_target_pairs={{0,64},{1,65},{2,66},{3,67},{4,68},{5,69},{6,70},{7,71},{8,72},{9,... | collective-permute-start | bytes 1572872 | tf_op jit(solution)/shard_map/ppermute | solution.py:34
  4.2 15.7 %collective-permute-start.18 = (f32[4,128,256]{2,1,0:T(8,128)}, f32[4,128,256]{2,1,0:T(8,128)S(1)}, u32[]{:S(2)}, u32[]{:S(2)}) collective-permute-start(f32[4,128,256]{2,1,0:T(8,128)} %log.3), channel_id=1, source_target_pairs={{0,80},{1,81},{2,82},{3,83},{4,84},{5,85},{6,86},{7,87},{8,88},{9,... | collective-permute-start | bytes 1572872 | tf_op jit(solution)/shard_map/ppermute | solution.py:34
  5.9 24.2 %collective-permute-start.8 = (f32[4,128,256]{2,1,0:T(8,128)}, f32[4,128,256]{2,1,0:T(8,128)S(1)}, u32[]{:S(2)}, u32[]{:S(2)}) collective-permute-start(f32[4,128,256]{2,1,0:T(8,128)} %param.11), channel_id=1, source_target_pairs={{0,64},{1,65},{2,66},{3,67},{4,68},{5,69},{6,70},{7,71},{8,72},{9,... | collective-permute-start | bytes 1572872 | tf_op jit(solution)/shard_map/ppermute | solution.py:34
  6.2 24.3 %collective-permute-start.7 = (f32[4,128,256]{2,1,0:T(8,128)}, f32[4,128,256]{2,1,0:T(8,128)S(1)}, u32[]{:S(2)}, u32[]{:S(2)}) collective-permute-start(f32[4,128,256]{2,1,0:T(8,128)} %param.11), channel_id=1, source_target_pairs={{0,80},{1,81},{2,82},{3,83},{4,84},{5,85},{6,86},{7,87},{8,88},{9,... | collective-permute-start | bytes 1572872 | tf_op jit(solution)/shard_map/ppermute | solution.py:34
  19.6 16.2 %collective-permute-start.20 = (f32[2,128,256]{2,1,0:T(8,128)}, f32[2,128,256]{2,1,0:T(8,128)}, u32[]{:S(2)}, u32[]{:S(2)}) collective-permute-start(f32[2,128,256]{2,1,0:T(8,128)} %slice.94), channel_id=1, source_target_pairs={{0,64},{1,65},{2,66},{3,67},{4,68},{5,69},{6,70},{7,71},{8,72},{9,... | collective-permute-start | bytes 786440 | tf_op jit(solution)/shard_map/ppermute | solution.py:34
  20.7 16.1 %collective-permute-start.21 = (f32[2,128,256]{2,1,0:T(8,128)}, f32[2,128,256]{2,1,0:T(8,128)}, u32[]{:S(2)}, u32[]{:S(2)}) collective-permute-start(f32[2,128,256]{2,1,0:T(8,128)} %slice.95), channel_id=1, source_target_pairs={{0,80},{1,81},{2,82},{3,83},{4,84},{5,85},{6,86},{7,87},{8,88},{9,... | collective-permute-start | bytes 786440 | tf_op jit(solution)/shard_map/ppermute | solution.py:34
  42.3 63.7 %collective-permute-start.32 = (f32[2,4,32,256]{3,2,1,0:T(8,128)}, f32[2,4,32,256]{3,2,1,0:T(8,128)}, u32[]{:S(2)}, u32[]{:S(2)}) collective-permute-start(f32[2,4,32,256]{3,2,1,0:T(8,128)} %pad_maximum_fusion.8), channel_id=1, source_target_pairs={{0,1},{1,2},{2,3},{3,0},{4,5},{5,6},{6,7},{7,4},{8,9},{9,10},{10,1... | collective-permute-start | bytes 786440 | tf_op jit(solution)/shard_map/ppermute | solution.py:34
  44.7 63.7 %collective-permute-start.33 = (f32[2,4,32,256]{3,2,1,0:T(8,128)}, f32[2,4,32,256]{3,2,1,0:T(8,128)}, u32[]{:S(2)}, u32[]{:S(2)}) collective-permute-start(f32[2,4,32,256]{3,2,1,0:T(8,128)} %pad_maximum_fusion.9), channel_id=1, source_target_pairs={{0,2},{1,3},{2,0},{3,1},{4,6},{5,7},{6,4},{7,5},{8,10},{9,11},{10,... | collective-permute-start | bytes 786440 | tf_op jit(solution)/shard_map/ppermute | solution.py:34
  49.4 15.4 %collective-permute-start.23 = (f32[4,128,256]{2,1,0:T(8,128)}, f32[4,128,256]{2,1,0:T(8,128)S(1)}, u32[]{:S(2)}, u32[]{:S(2)}) collective-permute-start(f32[4,128,256]{2,1,0:T(8,128)} %select_select_fusion.1), channel_id=1, source_target_pairs={{0,12},{1,13},{2,14},{3,15},{4,0},{5,1},{6,2},{7,3},{8,4},{9,5},{1... | collective-permute-start | bytes 1572872 | tf_op jit(solution)/shard_map/ppermute | solution.py:34
  53.7 57.5 %collective-permute-start.34 = (f32[2,4,32,256]{3,2,1,0:T(8,128)S(1)}, f32[2,4,32,256]{3,2,1,0:T(8,128)}, u32[]{:S(2)}, u32[]{:S(2)}) collective-permute-start(f32[2,4,32,256]{3,2,1,0:T(8,128)S(1)} %pad_maximum_fusion.10), channel_id=1, source_target_pairs={{0,3},{1,0},{2,1},{3,2},{4,7},{5,4},{6,5},{7,6},{8,11},{9,8},{10,9... | collective-permute-start | bytes 786440 | tf_op jit(solution)/shard_map/ppermute | solution.py:34
  65.8 16.4 %collective-permute-start.24 = (f32[4,128,256]{2,1,0:T(8,128)S(1)}, f32[4,128,256]{2,1,0:T(8,128)S(1)}, u32[]{:S(2)}, u32[]{:S(2)}) collective-permute-start(f32[4,128,256]{2,1,0:T(8,128)S(1)} %broadcast_select_fusion.2), channel_id=1, source_target_pairs={{0,8},{1,9},{2,10},{3,11},{4,12},{5,13},{6,14},{7,15},{8,0},{9,1},... | collective-permute-start | bytes 1572872 | tf_op jit(solution)/shard_map/ppermute | solution.py:34
  68.2 23.1 %collective-permute-start.14 = (f32[4,128,256]{2,1,0:T(8,128)S(1)}, f32[4,128,256]{2,1,0:T(8,128)S(1)}, u32[]{:S(2)}, u32[]{:S(2)}) collective-permute-start(f32[4,128,256]{2,1,0:T(8,128)S(1)} %broadcast_select_fusion.3), channel_id=1, source_target_pairs={{0,8},{1,9},{2,10},{3,11},{4,12},{5,13},{6,14},{7,15},{8,0},{9,1},... | collective-permute-start | bytes 1572872 | tf_op jit(solution)/shard_map/ppermute | solution.py:34
  92.7 19.8 %collective-permute-start.15 = (f32[1,4,32,256]{3,2,1,0:T(8,128)S(1)}, f32[1,4,32,256]{3,2,1,0:T(8,128)S(1)}, u32[]{:S(2)}, u32[]{:S(2)}) collective-permute-start(f32[1,4,32,256]{3,2,1,0:T(8,128)S(1)} %get-tuple-element.167), channel_id=1, source_target_pairs={{0,1},{1,2},{2,3},{3,0},{4,5},{5,6},{6,7},{7,4},{8,9},{9,10},{10,1... | collective-permute-start | bytes 393224 | tf_op jit(solution)/shard_map/ppermute | solution.py:34
  106.0 16.1 %collective-permute-start.17 = (f32[1,4,32,256]{3,2,1,0:T(8,128)S(1)}, f32[1,4,32,256]{3,2,1,0:T(8,128)S(1)}, u32[]{:S(2)}, u32[]{:S(2)}) collective-permute-start(f32[1,4,32,256]{3,2,1,0:T(8,128)S(1)} %get-tuple-element.165), channel_id=1, source_target_pairs={{0,3},{1,0},{2,1},{3,2},{4,7},{5,4},{6,5},{7,6},{8,11},{9,8},{10,9... | collective-permute-start | bytes 393224 | tf_op jit(solution)/shard_map/ppermute | solution.py:34
  111.2 16.0 %collective-permute-start.29 = (f32[4,32,256]{2,1,0:T(8,128)}, f32[4,32,256]{2,1,0:T(8,128)S(1)}, u32[]{:S(2)}, u32[]{:S(2)}) collective-permute-start(f32[4,32,256]{2,1,0:T(8,128)} %get-tuple-element.71), channel_id=1, source_target_pairs={{4,0},{5,1},{6,2},{7,3},{8,4},{9,5},{10,6},{11,7},{12,8},{13,9},{1... | collective-permute-start | bytes 393224 | tf_op jit(solution)/shard_map/ppermute | solution.py:34
  112.5 16.0 %collective-permute-start.30 = (f32[16,8,256]{2,1,0:T(8,128)}, f32[16,8,256]{2,1,0:T(8,128)S(1)}, u32[]{:S(2)}, u32[]{:S(2)}) collective-permute-start(f32[16,8,256]{2,1,0:T(8,128)} %get-tuple-element.72), channel_id=1, source_target_pairs={{0,1},{1,2},{2,3},{4,5},{5,6},{6,7},{8,9},{9,10},{10,11},{12,13},{... | collective-permute-start | bytes 393224 | tf_op jit(solution)/shard_map/ppermute | solution.py:34
  117.5 25.8 %collective-permute-start.35 = (f32[4,32,256]{2,1,0:T(8,128)}, f32[4,32,256]{2,1,0:T(8,128)S(1)}, u32[]{:S(2)}, u32[]{:S(2)}) collective-permute-start(f32[4,32,256]{2,1,0:T(8,128)} %get-tuple-element.79), channel_id=1, source_target_pairs={{0,4},{1,5},{2,6},{3,7},{4,8},{5,9},{6,10},{7,11},{8,12},{9,13},{1... | collective-permute-start | bytes 393224 | tf_op jit(solution)/shard_map/ppermute | solution.py:34
  122.1 21.3 %collective-permute-start.36 = (f32[4,32,256]{2,1,0:T(8,128)}, f32[4,32,256]{2,1,0:T(8,128)S(1)}, u32[]{:S(2)}, u32[]{:S(2)}) collective-permute-start(f32[4,32,256]{2,1,0:T(8,128)} %get-tuple-element.80), channel_id=1, source_target_pairs={{4,0},{5,1},{6,2},{7,3},{8,4},{9,5},{10,6},{11,7},{12,8},{13,9},{1... | collective-permute-start | bytes 393224 | tf_op jit(solution)/shard_map/ppermute | solution.py:34
  123.5 20.0 %collective-permute-start.37 = (f32[16,8,256]{2,1,0:T(8,128)}, f32[16,8,256]{2,1,0:T(8,128)S(1)}, u32[]{:S(2)}, u32[]{:S(2)}) collective-permute-start(f32[16,8,256]{2,1,0:T(8,128)} %get-tuple-element.81), channel_id=1, source_target_pairs={{0,1},{1,2},{2,3},{4,5},{5,6},{6,7},{8,9},{9,10},{10,11},{12,13},{... | collective-permute-start | bytes 393224 | tf_op jit(solution)/shard_map/ppermute | solution.py:34
  127.3 16.2 %collective-permute-start.38 = (f32[16,8,256]{2,1,0:T(8,128)}, f32[16,8,256]{2,1,0:T(8,128)S(1)}, u32[]{:S(2)}, u32[]{:S(2)}) collective-permute-start(f32[16,8,256]{2,1,0:T(8,128)} %get-tuple-element.82), channel_id=1, source_target_pairs={{1,0},{2,1},{3,2},{5,4},{6,5},{7,6},{9,8},{10,9},{11,10},{13,12},{... | collective-permute-start | bytes 393224 | tf_op jit(solution)/shard_map/ppermute | solution.py:34
  136.1 67.0 %collective-permute-start = (f32[2,4,32,256]{3,2,1,0:T(8,128)S(1)}, f32[2,4,32,256]{3,2,1,0:T(8,128)S(1)}, u32[]{:S(2)}, u32[]{:S(2)}) collective-permute-start(f32[2,4,32,256]{3,2,1,0:T(8,128)S(1)} %pad_maximum_fusion.4), channel_id=1, source_target_pairs={{0,1},{1,2},{2,3},{3,0},{4,5},{5,6},{6,7},{7,4},{8,9},{9,10},{10,1... | collective-permute-start | bytes 786440 | tf_op jit(solution)/shard_map/ppermute | solution.py:34
  181.6 26.8 %collective-permute-start.1 = (f32[2,4,32,256]{3,2,1,0:T(8,128)S(1)}, f32[2,4,32,256]{3,2,1,0:T(8,128)}, u32[]{:S(2)}, u32[]{:S(2)}) collective-permute-start(f32[2,4,32,256]{3,2,1,0:T(8,128)S(1)} %pad_maximum_fusion.5), channel_id=1, source_target_pairs={{0,2},{1,3},{2,0},{3,1},{4,6},{5,7},{6,4},{7,5},{8,10},{9,11},{10,... | collective-permute-start | bytes 786440 | tf_op jit(solution)/shard_map/ppermute | solution.py:34
  186.5 21.9 %collective-permute-start.2 = (f32[2,4,32,256]{3,2,1,0:T(8,128)}, f32[2,4,32,256]{3,2,1,0:T(8,128)}, u32[]{:S(2)}, u32[]{:S(2)}) collective-permute-start(f32[2,4,32,256]{3,2,1,0:T(8,128)} %pad_maximum_fusion.6), channel_id=1, source_target_pairs={{0,3},{1,0},{2,1},{3,2},{4,7},{5,4},{6,5},{7,6},{8,11},{9,8},{10,9... | collective-permute-start | bytes 786440 | tf_op jit(solution)/shard_map/ppermute | solution.py:34
  193.3 26.3 %collective-permute-start.47 = (f32[4,32,256]{2,1,0:T(8,128)}, f32[4,32,256]{2,1,0:T(8,128)}, u32[]{:S(2)}, u32[]{:S(2)}) collective-permute-start(f32[4,32,256]{2,1,0:T(8,128)} %get-tuple-element.95), channel_id=1, source_target_pairs={{0,4},{1,5},{2,6},{3,7},{4,8},{5,9},{6,10},{7,11},{8,12},{9,13},{1... | collective-permute-start | bytes 393224 | tf_op jit(solution)/shard_map/ppermute | solution.py:34
  201.8 19.8 %collective-permute-start.48 = (f32[4,32,256]{2,1,0:T(8,128)}, f32[4,32,256]{2,1,0:T(8,128)}, u32[]{:S(2)}, u32[]{:S(2)}) collective-permute-start(f32[4,32,256]{2,1,0:T(8,128)} %get-tuple-element.96), channel_id=1, source_target_pairs={{4,0},{5,1},{6,2},{7,3},{8,4},{9,5},{10,6},{11,7},{12,8},{13,9},{1... | collective-permute-start | bytes 393224 | tf_op jit(solution)/shard_map/ppermute | solution.py:34
  203.1 19.8 %collective-permute-start.49 = (f32[16,8,256]{2,1,0:T(8,128)}, f32[16,8,256]{2,1,0:T(8,128)S(1)}, u32[]{:S(2)}, u32[]{:S(2)}) collective-permute-start(f32[16,8,256]{2,1,0:T(8,128)} %get-tuple-element.97), channel_id=1, source_target_pairs={{0,1},{1,2},{2,3},{4,5},{5,6},{6,7},{8,9},{9,10},{10,11},{12,13},{... | collective-permute-start | bytes 393224 | tf_op jit(solution)/shard_map/ppermute | solution.py:34
  210.7 26.1 %collective-permute-start.3 = (f32[4,32,256]{2,1,0:T(8,128)}, f32[4,32,256]{2,1,0:T(8,128)S(1)}, u32[]{:S(2)}, u32[]{:S(2)}) collective-permute-start(f32[4,32,256]{2,1,0:T(8,128)} %get-tuple-element.64), channel_id=1, source_target_pairs={{0,4},{1,5},{2,6},{3,7},{4,8},{5,9},{6,10},{7,11},{8,12},{9,13},{1... | collective-permute-start | bytes 393224 | tf_op jit(solution)/shard_map/ppermute | solution.py:34
  218.3 18.6 %collective-permute-start.4 = (f32[4,32,256]{2,1,0:T(8,128)}, f32[4,32,256]{2,1,0:T(8,128)S(1)}, u32[]{:S(2)}, u32[]{:S(2)}) collective-permute-start(f32[4,32,256]{2,1,0:T(8,128)} %get-tuple-element.65), channel_id=1, source_target_pairs={{4,0},{5,1},{6,2},{7,3},{8,4},{9,5},{10,6},{11,7},{12,8},{13,9},{1... | collective-permute-start | bytes 393224 | tf_op jit(solution)/shard_map/ppermute | solution.py:34
  219.6 17.3 %collective-permute-start.5 = (f32[16,8,256]{2,1,0:T(8,128)}, f32[16,8,256]{2,1,0:T(8,128)S(1)}, u32[]{:S(2)}, u32[]{:S(2)}) collective-permute-start(f32[16,8,256]{2,1,0:T(8,128)} %get-tuple-element.66), channel_id=1, source_target_pairs={{0,1},{1,2},{2,3},{4,5},{5,6},{6,7},{8,9},{9,10},{10,11},{12,13},{... | collective-permute-start | bytes 393224 | tf_op jit(solution)/shard_map/ppermute | solution.py:34
  244.2 15.7 %collective-permute-start.51 = (f32[4,32,256]{2,1,0:T(8,128)}, f32[4,32,256]{2,1,0:T(8,128)S(1)}, u32[]{:S(2)}, u32[]{:S(2)}) collective-permute-start(f32[4,32,256]{2,1,0:T(8,128)} %get-tuple-element.101), channel_id=1, source_target_pairs={{0,4},{1,5},{2,6},{3,7},{4,8},{5,9},{6,10},{7,11},{8,12},{9,13},{1... | collective-permute-start | bytes 393224 | tf_op jit(solution)/shard_map/ppermute | solution.py:34
  344.0 19.7 %collective-permute-start.67 = (f32[2,128,256]{2,1,0:T(8,128)S(1)}, f32[2,128,256]{2,1,0:T(8,128)S(1)}, u32[]{:S(2)}, u32[]{:S(2)}) collective-permute-start(f32[2,128,256]{2,1,0:T(8,128)S(1)} %get-tuple-element.144), channel_id=1, source_target_pairs={{0,12},{1,13},{2,14},{3,15},{4,0},{5,1},{6,2},{7,3},{8,4},{9,5},{1... | collective-permute-start | bytes 786440 | tf_op jit(solution)/shard_map/ppermute | solution.py:34
  393.4 16.3 %collective-permute-start.73 = (f32[4,128,256]{2,1,0:T(8,128)S(1)}, f32[4,128,256]{2,1,0:T(8,128)S(1)}, u32[]{:S(2)}, u32[]{:S(2)}) collective-permute-start(f32[4,128,256]{2,1,0:T(8,128)S(1)} %pad_maximum_fusion.2), channel_id=1, source_target_pairs={{0,80},{1,81},{2,82},{3,83},{4,84},{5,85},{6,86},{7,87},{8,88},{9,... | collective-permute-start | bytes 1572872 | tf_op jit(solution)/shard_map/ppermute | solution.py:34
  (111 other events, 833.6 us)

commit v2 on v1

v2 whole, which is shorter than its diff:
```python
import functools

import jax
import jax.numpy as jnp
from jax import lax
from jax.experimental import pallas as pl
from jax.experimental.pallas import tpu as pltpu
from jax.sharding import PartitionSpec as P

lap_coeffs = (-205.0 / 72.0, 8.0 / 5.0, -1.0 / 5.0, 8.0 / 315.0, -1.0 / 560.0)
diff_coeffs = (4.0 / 5.0, -1.0 / 5.0, 4.0 / 105.0, -1.0 / 280.0)
time_step_sq = 0.0088

ROWS = 16
CELLS = 32
SPAN = CELLS + 16
NY = 128
NZ = 256
F32 = jnp.float32


def pairs_by(move):
    pairs = []
    for shot in range(4):
        for sub in range(32):
            x = 2 * (sub // 16) + shot // 2
            target = move(x, shot % 2, (sub // 4) % 4, sub % 4)
            if target is None:
                continue
            tx, tcore, tz, ty = target
            pairs.append((shot * 32 + sub, ((tx % 2) * 2 + tcore) * 32 + (tx // 2) * 16 + tz * 4 + ty))
    return pairs


def send(value, move):
    return lax.ppermute(value, ("shot", "sub"), pairs_by(move))


def send_x(value, steps):
    return send(value, lambda x, c, z, y: ((x + steps) % 4, c, z, y))


def send_core(value):
    return send(value, lambda x, c, z, y: (x, 1 - c, z, y))


def send_z(value, steps):
    return send(value, lambda x, c, z, y: (x, c, (z + steps) % 4, y))


def send_y(value, steps):
    return send(value, lambda x, c, z, y: (x, c, z, (y + steps) % 4))


def next_rows(x, z, steps):
    group = (x // 2) * 4 + z + steps
    if group < 0 or group > 7:
        return None
    return (2 * (group // 4) + x % 2, group % 4)


def send_group(value, steps):
    def move(x, c, z, y):
        place = next_rows(x, z, steps)
        return None if place is None else (place[0], c, place[1], y)

    return send(value, move)


def send_cells(value, steps):
    return send(value, lambda x, c, z, y: (x, c, z, y + steps) if 0 <= y + steps < 4 else None)


def shape(*sizes):
    return jax.ShapeDtypeStruct(sizes, F32)


def region(rows, cells):
    return shape(rows, 2, cells, 128)


BLOCK = region(ROWS, CELLS)
NEAR = region(ROWS + 8, SPAN)
WIDE = region(ROWS + 16, SPAN)


def call(body, outs, n_smem, operands, scratch=()):
    specs = [pl.BlockSpec(memory_space=pltpu.SMEM)] * n_smem
    specs += [pl.BlockSpec(memory_space=pltpu.VMEM)] * (len(operands) - n_smem)
    return pl.pallas_call(
        body,
        out_shape=tuple(outs),
        in_specs=specs,
        out_specs=tuple(pl.BlockSpec(memory_space=pltpu.VMEM) for _ in outs),
        scratch_shapes=[pltpu.VMEM(s.shape, s.dtype) for s in scratch],
    )(*operands)


def lanes():
    return lax.broadcasted_iota(jnp.int32, (8, 128), 1)


class Stencil:
    def __init__(self, source, row, cell, lane):
        self.source, self.row, self.cell, self.lane = source, row, cell, lane
        self.center = [self.load(0, 0, half) for half in (0, 1)]
        low, high = self.center
        self.deep = []
        for reach in range(1, 5):
            ahead = [pltpu.roll(v, 128 - reach, 1) for v in (low, high)]
            behind = [pltpu.roll(v, reach, 1) for v in (low, high)]
            front = lane < 128 - reach
            back = lane >= reach
            self.deep.append(
                (
                    (jnp.where(front, ahead[0], ahead[1]), jnp.where(front, ahead[1], 0.0)),
                    (jnp.where(back, behind[0], 0.0), jnp.where(back, behind[1], behind[0])),
                )
            )

    def load(self, rows, cells, half):
        first = self.cell + cells
        return self.source[self.row + rows, half, first : first + 8, :]

    def both(self, direction, reach, half):
        if direction == 0:
            return self.load(reach, 0, half), self.load(-reach, 0, half)
        if direction == 1:
            return self.load(0, reach, half), self.load(0, -reach, half)
        ahead, behind = self.deep[reach - 1]
        return ahead[half], behind[half]

    def derivative(self, direction, half):
        total = None
        for reach in range(1, 5):
            ahead, behind = self.both(direction, reach, half)
            part = diff_coeffs[reach - 1] * (ahead - behind)
            total = part if total is None else total + part
        return total

    def advanced(self, half, previous, speed_sq, slopes):
        center = self.center[half]
        lap = (3.0 * lap_coeffs[0]) * center
        derived = [None, None, None]
        for reach in range(1, 5):
            around = None
            for direction in range(3):
                ahead, behind = self.both(direction, reach, half)
                pair = ahead + behind
                around = pair if around is None else around + pair
                part = diff_coeffs[reach - 1] * (ahead - behind)
                derived[direction] = part if reach == 1 else derived[direction] + part
            lap = lap + lap_coeffs[reach] * around
        result = 2.0 * center - previous + speed_sq * lap
        for direction in range(3):
            result = result - slopes[direction] * derived[direction]
        return result


def over_block(visit):
    def step(row, carry):
        for cell in range(0, CELLS, 8):
            visit(row, cell)
        return carry

    lax.fori_loop(0, ROWS, step, 0)


def over_near(visit):
    def side(row, carry):
        for cell in range(8, 8 + CELLS, 8):
            visit(row, cell)
        return carry

    def middle(row, carry):
        for cell in range(4, 12 + CELLS, 8):
            visit(row, cell)
        return carry

    lax.fori_loop(0, 4, side, 0)
    lax.fori_loop(4, 4 + ROWS, middle, 0)
    lax.fori_loop(4 + ROWS, 8 + ROWS, side, 0)


def add_source(place, amount, first, target):
    @pl.when(place[first] > 0)
    def _():
        row, half = place[first + 1], place[first + 2]
        values = target[row, half]
        cell = lax.broadcasted_iota(jnp.int32, values.shape, 0)
        lane = lax.broadcasted_iota(jnp.int32, values.shape, 1)
        hit = (cell == place[first + 3]) & (lane == place[first + 4])
        target[row, half] = values + jnp.where(hit, amount, 0.0)


def near_step(source, old, model, lane, out, extra=None):
    speed_sq, slopes = model[0], model[1:]

    def visit(row, cell):
        stencil = Stencil(source, row + 4, cell, lane)
        cut = slice(cell, cell + 8)
        for half in (0, 1):
            value = stencil.advanced(
                half,
                old[row, half, cut, :],
                speed_sq[row, half, cut, :],
                [s[row, half, cut, :] for s in slopes],
            )
            if extra is not None:
                value = value + extra(row, half, cut)
            out[row, half, cut, :] = value

    over_near(visit)


def block_step(source, old, model, lane, finish):
    speed_sq, slopes = model[0], model[1:]

    def visit(row, cell):
        stencil = Stencil(source, row + 4, cell + 8, lane)
        near = slice(cell + 8, cell + 16)
        for half in (0, 1):
            value = stencil.advanced(
                half,
                old(row, half, slice(cell, cell + 8)),
                speed_sq[row + 4, half, near, :],
                [s[row + 4, half, near, :] for s in slopes],
            )
            finish(row, half, slice(cell, cell + 8), value)

    over_block(visit)


def of_block(ref):
    return lambda row, half, cut: ref[row, half, cut, :]


def of_near(ref):
    return lambda row, half, cut: ref[row + 4, half, cut.start + 8 : cut.stop + 8, :]


def of_wide(ref):
    return lambda row, half, cut: ref[row + 8, half, cut.start + 8 : cut.stop + 8, :]


def injected(maps, index, field):
    def near(row, half, cut):
        hits = maps[row, half, cut, 0:128]
        seen = maps[row, half, cut, 128 * index : 128 * index + 128]
        return hits * field[row, half, cut, :] - seen

    return near


def fill_wide(wide, block, below, above, left, right):
    wide[0:8, :, 8 : 8 + CELLS, :] = below[...]
    wide[8 : 8 + ROWS, :, 8 : 8 + CELLS, :] = block[...]
    wide[8 + ROWS : 16 + ROWS, :, 8 : 8 + CELLS, :] = above[...]
    wide[:, :, 0:8, :] = left[...]
    wide[:, :, 8 + CELLS : SPAN, :] = right[...]


def cut_body(chunks, *refs, margins):
    count = len(margins)
    slabs, pieces = refs[:count], refs[count:]
    for turn in range(4):
        chunk = chunks[turn]
        first = pl.multiple_of(chunk * CELLS, CELLS)
        before = pl.multiple_of(jnp.maximum(first - 8, 0), 8)
        after = pl.multiple_of(jnp.minimum(first + CELLS, NY - 8), 8)
        at = 0
        for slab, margin in zip(slabs, margins):
            if margin:
                pieces[turn][:, at : at + 8, :] = jnp.where(chunk > 0, slab[:, pl.ds(before, 8), :], 0.0)
                at += 8
            pieces[turn][:, at : at + CELLS, :] = slab[:, pl.ds(first, CELLS), :]
            at += CELLS
            if margin:
                pieces[turn][:, at : at + 8, :] = jnp.where(chunk < 3, slab[:, pl.ds(after, 8), :], 0.0)
                at += 8


def to_blocks(slabs, margins, chunks):
    width = sum(SPAN if margin else CELLS for margin in margins)
    pieces = call(functools.partial(cut_body, margins=margins), [shape(4, width, NZ)] * 4, 1, (chunks, *slabs))
    return [pieces[0]] + [send_y(pieces[turn], turn) for turn in (1, 2, 3)]


def place_pieces(slots, pieces, outs):
    for turn in range(4):
        slot = pl.multiple_of(slots[turn] * 4, 4)
        at = 0
        for out in outs:
            width = out.shape[2]
            for half in (0, 1):
                out[pl.ds(slot, 4), half] = pieces[turn][:, at : at + width, 128 * half : 128 * half + 128]
            at += width


def gather_body(slots, *refs, depths):
    pieces, outs = refs[:4], refs[4:]
    low, high = outs[-2:]
    place_pieces(slots, pieces, outs[:-2])
    at = 0
    for out, depth in zip(outs, depths):
        if depth:
            low[at : at + depth] = out[0:depth]
            high[at : at + depth] = out[ROWS - depth : ROWS]
            at += depth


def gather_blocks(pieces, slots, depths):
    outs = [region(ROWS, SPAN if depth else CELLS) for depth in depths]
    outs += [region(sum(depths), SPAN)] * 2
    *blocks, low, high = call(functools.partial(gather_body, depths=depths), outs, 1, (slots, *pieces))
    return blocks, send_group(high, 1), send_group(low, -1)


def stack_rows(out, below, middle, above, at, depth):
    out[0:depth] = below[at : at + depth]
    out[depth : depth + ROWS] = middle[...]
    out[depth + ROWS : 2 * depth + ROWS] = above[at : at + depth]


def fields_body(now, old, adjoint, below, above, wide, old_near, adjoint_near):
    stack_rows(wide, below, now, above, 0, 8)
    stack_rows(old_near, below, old, above, 8, 4)
    stack_rows(adjoint_near, below, adjoint, above, 12, 4)


def model_body(log_mass, speed, below, above, speed_sq, s0, s1, s2, twice, wide, speed_near):
    stack_rows(wide, below, log_mass, above, 0, 8)
    stack_rows(speed_near, below, speed, above, 8, 4)
    twice[...] = 2.0 / speed[:, :, 8 : 8 + CELLS, :]
    lane = lanes()

    def visit(row, cell):
        stencil = Stencil(wide, row + 4, cell, lane)
        cut = slice(cell, cell + 8)
        for half in (0, 1):
            value = speed_near[row, half, cut, :]
            scale = time_step_sq * value * value
            speed_sq[row, half, cut, :] = scale
            for direction, out in enumerate((s0, s1, s2)):
                out[row, half, cut, :] = scale * stencil.derivative(direction, half)

    over_near(visit)


def forward_body(place, amount, wide, old, speed_sq, s0, s1, s2, near, new, low, high):
    model = (speed_sq, s0, s1, s2)
    lane = lanes()
    near_step(wide, old, model, lane, near)
    add_source(place, amount[0], 0, near)

    def finish(row, half, cut, value):
        new[row, half, cut, :] = value

    block_step(near, of_wide(wide), model, lane, finish)
    add_source(place, amount[1], 5, new)
    low[...] = new[0:8]
    high[...] = new[8:ROWS]


def write_pieces(slots, block, pieces, at):
    for turn in range(4):
        slot = pl.multiple_of(slots[turn] * 4, 4)
        for half in (0, 1):
            pieces[turn][:, at : at + CELLS, 128 * half : 128 * half + 128] = block[pl.ds(slot, 4), half]


def turn_body(
    place, amount, slots, block, below, above, left, right, old, speed_sq, s0, s1, s2,
    adjoint, later, maps, near, new, adjoint_new, summed, low, high, p0, p1, p2, p3, wide,
):
    model = (speed_sq, s0, s1, s2)
    lane = lanes()
    fill_wide(wide, block, below, above, left, right)
    near_step(wide, old, model, lane, near)
    add_source(place, amount[2], 0, near)

    def finish(row, half, cut, value):
        new[row, half, cut, :] = value

    block_step(near, of_block(block), model, lane, finish)
    add_source(place, amount[3], 5, new)

    def finish_adjoint(row, half, cut, value):
        hits = of_near(maps)(row, half, cut)
        ahead = new[row, half, cut, :]
        value = value + (hits[:, 0:128] * ahead - hits[:, 4 * 128 : 5 * 128])
        adjoint_new[row, half, cut, :] = value
        summed[row, half, cut, :] = value * (
            ahead - 2.0 * of_near(near)(row, half, cut) + block[row, half, cut, :]
        )

    block_step(adjoint, of_block(later), model, lane, finish_adjoint)
    low[...] = adjoint_new[0:8]
    high[...] = adjoint_new[8:ROWS]
    write_pieces(slots, new, (p0, p1, p2, p3), 0)


def adjoint_body(
    block, below, above, left, right, old, speed_sq, s0, s1, s2, maps, u3, u2, u1, u0, sums,
    near, new, summed, low, high, low_cells, high_cells, wide,
):
    model = (speed_sq, s0, s1, s2)
    lane = lanes()
    fill_wide(wide, block, below, above, left, right)
    near_step(wide, old, model, lane, near, injected(maps, 3, u3))

    def finish(row, half, cut, value):
        hits = of_near(maps)(row, half, cut)
        third = of_near(u3)(row, half, cut)
        second = u2[row, half, cut, :]
        first = of_near(u1)(row, half, cut)
        zeroth = of_wide(u0)(row, half, cut)
        value = value + (hits[:, 0:128] * second - hits[:, 2 * 128 : 3 * 128])
        new[row, half, cut, :] = value
        total = sums[row, half, cut, :]
        total = total + of_near(near)(row, half, cut) * (third - 2.0 * second + first)
        summed[row, half, cut, :] = total + value * (second - 2.0 * first + zeroth)

    block_step(near, of_block(block), model, lane, finish)
    low[...] = new[0:4]
    high[...] = new[ROWS - 4 : ROWS]
    low_cells[...] = new[:, :, 0:8, :]
    high_cells[...] = new[:, :, CELLS - 8 : CELLS, :]


def last_body(
    slots, model_slots, block, below, above, left, right, old, speed_sq, s0, s1, s2, maps,
    u1, u0, u_before, sums, twice, p0, p1, p2, p3, q0, q1, q2, q3, near, new, image,
):
    near[0:4, :, 8 : 8 + CELLS, :] = below[...]
    near[4 : 4 + ROWS, :, 8 : 8 + CELLS, :] = block[...]
    near[4 + ROWS : 8 + ROWS, :, 8 : 8 + CELLS, :] = above[...]
    near[4 : 4 + ROWS, :, 0:8, :] = left[...]
    near[4 : 4 + ROWS, :, 8 + CELLS : SPAN, :] = right[...]
    lane = lanes()

    def finish(row, half, cut, value):
        hits = of_near(maps)(row, half, cut)
        first = of_near(u1)(row, half, cut)
        value = value + (hits[:, 0:128] * first - hits[:, 128:256])
        new[row, half, cut, :] = value
        curvature = first - 2.0 * of_wide(u0)(row, half, cut) + of_near(u_before)(row, half, cut)
        image[row, half, cut, :] = twice[row, half, cut, :] * (sums[row, half, cut, :] + value * curvature)

    block_step(near, of_near(old), (speed_sq, s0, s1, s2), lane, finish)
    write_pieces(model_slots, image, (q0, q1, q2, q3), 0)
    write_pieces(slots, new, (p0, p1, p2, p3), 0)


def rim_body(block, below, above, low, high):
    for out, cut in ((low, slice(0, 8)), (high, slice(CELLS - 8, CELLS))):
        out[0:8] = below[:, :, cut, :]
        out[8 : 8 + ROWS] = block[:, :, cut, :]
        out[8 + ROWS : 16 + ROWS] = above[:, :, cut, :]


def wide_halo(block, low, high):
    below, above = send_group(high, 1), send_group(low, -1)
    low_cells, high_cells = call(rim_body, [region(ROWS + 16, 8)] * 2, 0, (block, below, above))
    return below, above, send_cells(high_cells, 1), send_cells(low_cells, -1)


def spread_body(chunks, p0, p1, p2, p3, out):
    for turn, piece in enumerate((p0, p1, p2, p3)):
        first = pl.multiple_of(chunks[turn] * CELLS, CELLS)
        out[:, pl.ds(first, CELLS), :] = piece[...]


def to_slab(pieces, chunks):
    pieces = [pieces[0]] + [send_y(pieces[turn], turn) for turn in (1, 2, 3)]
    return call(spread_body, [shape(4, NY, NZ)], 1, (chunks, *pieces))[0]


def on_device(
    velocity,
    density,
    aperture_start,
    source_cell,
    receiver_cells,
    wavelet,
    observed,
    forward_old,
    forward_now,
    adjoint_later,
    adjoint_now,
):
    shot = lax.axis_index("shot")
    sub = lax.axis_index("sub")
    core = shot % 2
    x_hi = sub // 16
    x = 2 * x_hi + shot // 2
    z = (sub // 4) % 4
    y = sub % 4
    group = sub // 4
    start = aperture_start[0]
    partner_start = send_core(aperture_start)[0]

    def wanted(first_slab):
        upper = first_slab // 4 + (y < first_slab % 4).astype(jnp.int32)
        block = jnp.clip(x_hi + (upper - z + 3) // 4, 0, 7)
        position = 2 * (block % 2) + block // 4
        return (block // 2) % 2, (position - x) % 4, upper % 4

    own_core, own_step, turn_by = wanted(start)
    pair_core, pair_step, _ = wanted(partner_start)
    low = turn_by % 2 == 1
    high = turn_by // 2 == 1
    high_back = ((turn_by + 1) // 2) % 2 == 1
    high_other = jnp.where(low, high_back, high)
    turns = jnp.arange(4, dtype=jnp.int32)
    chunks_out = (y + turns) % 4
    chunks_in = (y - turns) % 4
    slots_in = (y - turns - start % 4) % 4
    slots_out = (y + turns - start % 4) % 4

    def gathered(slab):
        from_below = send_x(slab, 1)
        from_above = send_x(slab, -1)
        far = jnp.concatenate([send_x(from_below[0:2], 1), send_x(from_above[2:4], -1)])

        def pick(step):
            return jnp.where(
                step < 2, jnp.where(step == 0, slab, from_above), jnp.where(step == 2, far, from_below)
            )

        other = send_core(pick(pair_step))
        return jnp.where(own_core == core, pick(own_step), other)

    def turned(slab, direction, high_bit):
        slab = jnp.where(low, send_z(slab, direction), slab)
        return jnp.where(high_bit, send_z(slab, 2), slab)

    log_slab = turned(gathered(jnp.log(density)), -1, high)
    speed_slab = turned(gathered(velocity), 1, high_other)

    pieces = to_blocks(
        [forward_now[0], forward_old[0], adjoint_now[0], adjoint_later[0]],
        (True, True, True, False),
        chunks_out,
    )
    (now, old, adjoint, a_later), below, above = gather_blocks(pieces, chunks_in, (8, 4, 4, 0))
    u_wide, old_near, a_near = call(
        fields_body, [WIDE, NEAR, NEAR], 0, (now, old, adjoint, below, above)
    )

    def local_place(cells, rows_more, cells_more):
        rows = cells // (NY * NZ) - group * ROWS + rows_more
        columns = (cells // NZ) % NY - y * CELLS + cells_more
        inside = (rows >= 0) & (rows < ROWS + 2 * rows_more)
        inside = inside & (columns >= 0) & (columns < CELLS + 2 * cells_more)
        return inside, rows, (cells // 128) % 2, columns, cells % 128

    inside, rows, half, columns, lane = local_place(receiver_cells[0], 4, 8)
    line = jnp.where(inside, (rows * 2 + half) * SPAN + columns, -1)
    lines = (ROWS + 8) * 2 * SPAN
    on_line = (jnp.arange(lines, dtype=jnp.int32)[:, None] == line[None, :]).astype(F32)
    weights = jnp.concatenate([jnp.ones_like(observed[0, :1]), observed[0]])
    hit = lane[:, None, None] == jnp.arange(128, dtype=jnp.int32)[None, None, :]
    at_lane = jnp.where(hit, weights.T[:, :, None], 0.0).reshape(-1, 5 * 128)
    maps = jnp.dot(on_line, at_lane, precision=lax.Precision.HIGHEST)
    maps = maps.reshape(ROWS + 8, 2, SPAN, 5 * 128)

    def source_place(rows_more, cells_more):
        inside, rows, half, columns, lane = local_place(source_cell[0], rows_more, cells_more)
        rows = jnp.clip(rows, 0, ROWS + 2 * rows_more - 1)
        return [inside.astype(jnp.int32), rows, half, columns, lane]

    place = jnp.stack(source_place(4, 8) + source_place(0, 0))
    amount = wavelet[0]

    pieces = to_blocks([log_slab, speed_slab], (True, True), chunks_out)
    (log_mass, speed), below, above = gather_blocks(pieces, slots_in, (8, 4))
    *model, twice = call(
        model_body, [NEAR] * 4 + [BLOCK], 0, (log_mass, speed, below, above), (WIDE, NEAR)
    )

    edges = [region(8, CELLS)] * 2
    u1, u2, *sides = call(
        forward_body, [NEAR, BLOCK] + edges, 2, (place, amount, u_wide, old_near, *model)
    )
    halo = wide_halo(u2, *sides)
    u3, _, a3, sums, side_low, side_high, *pieces = call(
        turn_body,
        [NEAR, BLOCK, BLOCK, BLOCK] + edges + [shape(4, CELLS, NZ)] * 4,
        3,
        (place, amount, chunks_out, u2, *halo, u1, *model, a_near, a_later, maps),
        (WIDE,),
    )
    halo = wide_halo(a3, side_low, side_high)
    forward_last = to_slab(pieces, chunks_in)
    a2, a1, sums, side_low, side_high, low_cells, high_cells = call(
        adjoint_body,
        [NEAR, BLOCK, BLOCK] + [region(4, CELLS)] * 2 + [region(ROWS, 8)] * 2,
        0,
        (a3, *halo, a_near, *model, maps, u3, u2, u1, u_wide, sums),
        (WIDE,),
    )
    halo = (
        send_group(side_high, 1),
        send_group(side_low, -1),
        send_cells(high_cells, 1),
        send_cells(low_cells, -1),
    )
    pieces = call(
        last_body,
        [shape(4, CELLS, NZ)] * 8,
        2,
        (chunks_out, slots_out, a1, *halo, a2, *model, maps, u1, u_wide, old_near, sums, twice),
        (NEAR, BLOCK, BLOCK),
    )
    image = to_slab(pieces[4:], chunks_in)
    image, *pieces = lax.optimization_barrier((image, *pieces[:4]))
    adjoint_first = to_slab(pieces, chunks_in)

    def both(first_half, second_half):
        return jnp.concatenate([first_half, second_half])

    image = jnp.where(low, both(send_z(image[0:2], 1), send_z(image[2:4], -1)), image)
    arrived = send_z(image, 2)
    image = both(
        jnp.where(high, arrived[0:2], image[0:2]),
        jnp.where(high_other, arrived[2:4], image[2:4]),
    )
    other = send_core(image)

    def share(step):
        mine = jnp.where((own_core == core) & (own_step == step), image, 0.0)
        return mine + jnp.where((pair_core == core) & (pair_step == step), other, 0.0)

    far = share(2)
    passing_up = send_x(far[0:2], 1)
    passing_down = send_x(far[2:4], -1)
    up = share(1)
    down = share(3)
    up = send_x(both(up[0:2] + passing_up, up[2:4]), 1)
    down = send_x(both(down[0:2], down[2:4] + passing_down), -1)
    gradient = share(0) + up + down
    return (gradient, forward_last[None], adjoint_first[None])


def solution(mesh):
    placed = (
        P(("shot", "sub"), None, None),
        P(("shot", "sub"), None, None),
        P("shot"),
        P("shot"),
        P("shot", None),
        P("shot", None),
        P("shot", None, None),
        P("shot", "sub", None, None),
        P("shot", "sub", None, None),
        P("shot", "sub", None, None),
        P("shot", "sub", None, None),
    )
    return jax.shard_map(
        on_device,
        mesh=mesh,
        in_specs=placed,
        out_specs=(
            P(("shot", "sub"), None, None),
            P("shot", "sub", None, None),
            P("shot", "sub", None, None),
        ),
        check_vma=False,
    )
```

time: 414 us -> 358 us (0.86)
  starting transfers between devices: 180 us -> 88 us
  waiting for transfers between devices: 122 us -> 151 us
  Pallas kernels: 65.3 us -> 84.3 us
  local copies, waits for them, and re-layouts: 25.2 us -> 12.5 us
    ppermute x77 -> x54, starting transfers between devices: 180 us -> 88 us  [send(): return lax.ppermute(value, ('shot', 'sub'), pairs_by(move))]
    ppermute x77 -> x54, waiting for transfers between devices: 122 us -> 151 us  [send(): return lax.ppermute(value, ('shot', 'sub'), pairs_by(move))]
    pallas_call x14 -> x15, Pallas kernels: 65.3 us -> 84.3 us  [call(): pl.pallas_call(body, out_shape=tuple(outs), in_specs=specs, out_specs=tup...]
    slice x6 -> x0, local copies, waits for them, and re-layouts: 7.52 us -> none  [on_device(): operands = (current, *halo, later, *model, maps[0], maps[index + 1])]
    another operation x13 -> x0, other arithmetic: 5.08 us -> none  [the longest x8 3.68 us: to_blocks(): jnp.stack([lax.dynamic_slice_in_dim(slab, first, CELLS, 1) for slab in sl...]
  transfers between devices with their start and end apart: 77 -> 54, of which waited for: 31 -> 33; matrix products, arithmetic and copies ran while one was open for 6% -> 5% of each run, Pallas kernels for 9% -> 6%
where the time goes in v2:
time: 358 us
  waiting for transfers between devices  151 us (42%)
  starting transfers between devices  88 us (25%)
  Pallas kernels  84.3 us (24%)
  local copies, waits for them, and re-layouts  12.5 us (3%)
  other arithmetic  11.9 us (3%)
  between operations  5.61 us (2%)
  matrix products  5.02 us (1%)
    ppermute x54, waiting for transfers between devices, send(): return lax.ppermute(value, ('shot', 'sub'), pairs_by(move))  151 us
    ppermute x54, starting transfers between devices, send(): return lax.ppermute(value, ('shot', 'sub'), pairs_by(move))  88 us
    pallas_call x15, Pallas kernels, call(): pl.pallas_call(body, out_shape=tuple(outs), in_specs=specs, out_specs=tup...  84.3 us
    unnamed x74, local copies, waits for them, and re-layouts  7.79 us
  transfers between devices with their start and end apart: 54, of which 33 were waited for; matrix products, arithmetic and copies ran while one was open for 5% of the time, Pallas kernels for 6%

profile of v2, /device:TPU:0, one launch (start us, length us, event | category | flops | bytes accessed | tf_op | source)
XLA Modules:
  0.0 358.3 jit_solution(4921339184464878023)
XLA Ops:
  7.1 10.8 %collective-permute-done.6 = f32[4,128,256]{2,1,0:T(8,128)S(1)} collective-permute-done((f32[4,128,256]{2,1,0:T(8,128)S(1)}, f32[4,128,256]{2,1,0:T(8,128)S(1)}, u32[]{:S(2)}, u32[]{:S(2)}) %collective-permute-start.6) | collective-permute-done | bytes 524320 | tf_op jit(solution)/shard_map/ppermute | solution.py:36
  25.9 3.6 collective-permute-done.13
  44.1 4.1 %collective-permute-start.11 = (f32[4,128,256]{2,1,0:T(8,128)}, f32[4,128,256]{2,1,0:T(8,128)S(1)}, u32[]{:S(2)}, u32[]{:S(2)}) collective-permute-start(f32[4,128,256]{2,1,0:T(8,128)} %select_select_fusion.3), channel_id=1, source_target_pairs={{0,12},{1,13},{2,14},{3,15},{4,0},{5,1},{6,2},{7,3},{8,4},{9,5},{1... | collective-permute-start | bytes 1572872 | tf_op jit(solution)/shard_map/ppermute | solution.py:36
  49.6 10.8 %collective-permute-done.11 = f32[4,128,256]{2,1,0:T(8,128)S(1)} collective-permute-done((f32[4,128,256]{2,1,0:T(8,128)}, f32[4,128,256]{2,1,0:T(8,128)S(1)}, u32[]{:S(2)}, u32[]{:S(2)}) %collective-permute-start.11) | collective-permute-done | bytes 524320 | tf_op jit(solution)/shard_map/ppermute | solution.py:36
  63.8 17.8 %collective-permute-done.18 = f32[4,128,256]{2,1,0:T(8,128)S(1)} collective-permute-done((f32[4,128,256]{2,1,0:T(8,128)S(1)}, f32[4,128,256]{2,1,0:T(8,128)S(1)}, u32[]{:S(2)}, u32[]{:S(2)}) %collective-permute-start.18) | collective-permute-done | bytes 524320 | tf_op jit(solution)/shard_map/ppermute | solution.py:36
  82.3 3.3 shard_map.130
  95.9 28.7 %collective-permute-done.refs_1_ = f32[4,176,256]{2,1,0:T(8,128)S(1)} collective-permute-done((f32[4,176,256]{2,1,0:T(8,128)}, f32[4,176,256]{2,1,0:T(8,128)S(1)}, u32[]{:S(2)}, u32[]{:S(2)}) %collective-permute-start) | collective-permute-done | bytes 720928 | tf_op jit(solution)/shard_map/ppermute | solution.py:36
  126.9 3.9 %shard_map.131 = (f32[16,2,48,128]{3,2,1,0:T(8,128)}, f32[16,2,48,128]{3,2,1,0:T(8,128)}, f32[16,2,48,128]{3,2,1,0:T(8,128)}, f32[16,2,32,128]{3,2,1,0:T(8,128)}...) custom-call(s32[4]{0:T(128)} %and_select_fusion.10.slots.chunks, f32[4,176,256]{2,1,0:T(8,128)} %get-tuple-element.66.refs_0_, ...), custom_call_target="tpu_custom_call" | custom-call | tf_op jit(solution)/shard_map/pallas_call | solution.py:90
  138.2 4.8 %collective-permute-start.23 = (f32[12,2,48,128]{3,2,1,0:T(8,128)}, f32[12,2,48,128]{3,2,1,0:T(8,128)S(1)}, u32[]{:S(2)}, u32[]{:S(2)}) collective-permute-start(f32[12,2,48,128]{3,2,1,0:T(8,128)} %get-tuple-element.83), channel_id=1, source_target_pairs={{0,4},{1,5},{2,6},{3,7},{4,8},{5,9},{6,10},{7,11},{8,12},{9,13},{1... | collective-permute-start | bytes 1769480 | tf_op jit(solution)/shard_map/ppermute | solution.py:36
  149.1 4.1 %shard_map.132 = (f32[32,2,48,128]{3,2,1,0:T(8,128)}, f32[24,2,48,128]{3,2,1,0:T(8,128)}, f32[24,2,48,128]{3,2,1,0:T(8,128)}) custom-call(f32[16,2,48,128]{3,2,1,0:T(8,128)} %get-tuple-element.70.now, f32[16,2,48,128]{3,2,1,0:T(8,128)} %get-tuple-element.71.old, f32[16,2,48,128]{3,2,1,0:T(8,128)} %get-tuple-element.72.adjoint, ...), custom_call_target="tpu_custom_call" | custom-call | tf_op jit(solution)/shard_map/pallas_call | solution.py:90
  155.8 7.8 %shard_map.135 = (f32[24,2,48,128]{3,2,1,0:T(8,128)}, f32[24,2,48,128]{3,2,1,0:T(8,128)}, f32[24,2,48,128]{3,2,1,0:T(8,128)}, f32[24,2,48,128]{3,2,1,0:T(8,128)}, f32[16,2,32,128]{3,2,1,0:T(8,128)}) custom-call(f32[16,2,48,128]{3,2,1,0:T(8,128)} %get-tuple-element.81.log_mass, f32[16,2,48,128]{3,2,1,0:T(8,128)} %get-tuple-element.82.speed, ...), custom_call_target="tpu_custom_call" | custom-call | tf_op jit(solution)/shard_map/pallas_call | solution.py:90
  163.6 10.6 %shard_map.136 = (f32[24,2,48,128]{3,2,1,0:T(8,128)}, f32[16,2,32,128]{3,2,1,0:T(8,128)}, f32[8,2,32,128]{3,2,1,0:T(8,128)}, f32[8,2,32,128]{3,2,1,0:T(8,128)}) custom-call(s32[10]{0:T(128)} %stack.45.place, f32[4]{0:T(128)} %bitcast.45, f32[32,2,48,128]{3,2,1,0:T(8,128)} %get-tuple-element.75.wide.u0, f32[24,2,48,128]{3,2,1,0:T(8,128)} %get-tuple-element.76.old.u_before, ...), custom_call_target="tpu_custom_call" | custom-call | tf_op jit(solution)/shard_map/pallas_call | solution.py:90
  174.2 3.9 %collective-permute-start.25 = (f32[8,2,32,128]{3,2,1,0:T(8,128)}, f32[8,2,32,128]{3,2,1,0:T(8,128)S(1)}, u32[]{:S(2)}, u32[]{:S(2)}) collective-permute-start(f32[8,2,32,128]{3,2,1,0:T(8,128)} %get-tuple-element.90), channel_id=1, source_target_pairs={{0,4},{1,5},{2,6},{3,7},{4,8},{5,9},{6,10},{7,11},{8,12},{9,13},{1... | collective-permute-start | bytes 786440 | tf_op jit(solution)/shard_map/ppermute | solution.py:36
  182.3 4.3 %collective-permute-done.26.above = f32[8,2,32,128]{3,2,1,0:T(8,128)S(1)} collective-permute-done((f32[8,2,32,128]{3,2,1,0:T(8,128)}, f32[8,2,32,128]{3,2,1,0:T(8,128)S(1)}, u32[]{:S(2)}, u32[]{:S(2)}) %collective-permute-start.26) | collective-permute-done | bytes 262176 | tf_op jit(solution)/shard_map/ppermute | solution.py:36
  189.3 3.9 %collective-permute-start.27 = (f32[32,2,8,128]{3,2,1,0:T(8,128)}, f32[32,2,8,128]{3,2,1,0:T(8,128)S(1)}, u32[]{:S(2)}, u32[]{:S(2)}) collective-permute-start(f32[32,2,8,128]{3,2,1,0:T(8,128)} %get-tuple-element.92), channel_id=1, source_target_pairs={{0,1},{1,2},{2,3},{4,5},{5,6},{6,7},{8,9},{9,10},{10,11},{12,13},{... | collective-permute-start | bytes 786440 | tf_op jit(solution)/shard_map/ppermute | solution.py:36
  194.5 5.0 %fusion.maps = f32[24,2,48,640]{3,2,1,0:T(8,128)} fusion(f32[256,640,1,1]{0,1,3,2:T(8,128)S(1)} %bitcast.35, s32[256]{0:T(256)S(1)} %bitcast.44, s32[24,2,48]{2,1,0:T(2,128)S(1)} %multiply_add_fusion), kind=kOutput, calls=%fused_computation | convolution fusion | flops 4530438144 | bytes 6563840 | tf_op jit(solution)/shard_map/dot_general | solution.py:565
  202.4 15.8 %shard_map.138 = (f32[24,2,48,128]{3,2,1,0:T(8,128)}, f32[16,2,32,128]{3,2,1,0:T(8,128)}, f32[16,2,32,128]{3,2,1,0:T(8,128)}, f32[16,2,32,128]{3,2,1,0:T(8,128)}...) custom-call(s32[10]{0:T(128)} %stack.45.place, ...), custom_call_target="tpu_custom_call" | custom-call | tf_op jit(solution)/shard_map/pallas_call | solution.py:90
  218.2 6.7 %collective-permute-start.29 = (f32[8,2,32,128]{3,2,1,0:T(8,128)}, f32[8,2,32,128]{3,2,1,0:T(8,128)S(1)}, u32[]{:S(2)}, u32[]{:S(2)}) collective-permute-start(f32[8,2,32,128]{3,2,1,0:T(8,128)} %get-tuple-element.98), channel_id=1, source_target_pairs={{0,4},{1,5},{2,6},{3,7},{4,8},{5,9},{6,10},{7,11},{8,12},{9,13},{1... | collective-permute-start | bytes 786440 | tf_op jit(solution)/shard_map/ppermute | solution.py:36
  229.0 4.3 %collective-permute-done.30.above = f32[8,2,32,128]{3,2,1,0:T(8,128)S(1)} collective-permute-done((f32[8,2,32,128]{3,2,1,0:T(8,128)}, f32[8,2,32,128]{3,2,1,0:T(8,128)S(1)}, u32[]{:S(2)}, u32[]{:S(2)}) %collective-permute-start.30) | collective-permute-done | bytes 262176 | tf_op jit(solution)/shard_map/ppermute | solution.py:36
  242.7 4.3 %collective-permute-done.32.right = f32[32,2,8,128]{3,2,1,0:T(8,128)S(1)} collective-permute-done((f32[32,2,8,128]{3,2,1,0:T(8,128)}, f32[32,2,8,128]{3,2,1,0:T(8,128)S(1)}, u32[]{:S(2)}, u32[]{:S(2)}) %collective-permute-start.32) | collective-permute-done | bytes 262176 | tf_op jit(solution)/shard_map/ppermute | solution.py:36
  247.7 13.9 %shard_map.140 = (f32[24,2,48,128]{3,2,1,0:T(8,128)}, f32[16,2,32,128]{3,2,1,0:T(8,128)}, f32[16,2,32,128]{3,2,1,0:T(8,128)}, f32[4,2,32,128]{3,2,1,0:T(8,128)},...) custom-call(f32[16,2,32,128]{3,2,1,0:T(8,128)} %get-tuple-element.97.block, ...), custom_call_target="tpu_custom_call" | custom-call | tf_op jit(solution)/shard_map/pallas_call | solution.py:90
  261.7 5.5 %collective-permute-start.33 = (f32[4,2,32,128]{3,2,1,0:T(8,128)}, f32[4,2,32,128]{3,2,1,0:T(8,128)S(1)}, u32[]{:S(2)}, u32[]{:S(2)}) collective-permute-start(f32[4,2,32,128]{3,2,1,0:T(8,128)} %get-tuple-element.105), channel_id=1, source_target_pairs={{0,4},{1,5},{2,6},{3,7},{4,8},{5,9},{6,10},{7,11},{8,12},{9,13},{1... | collective-permute-start | bytes 393224 | tf_op jit(solution)/shard_map/ppermute | solution.py:36
  274.6 3.9 %collective-permute-done.36.right = f32[16,2,8,128]{3,2,1,0:T(8,128)S(1)} collective-permute-done((f32[16,2,8,128]{3,2,1,0:T(8,128)}, f32[16,2,8,128]{3,2,1,0:T(8,128)S(1)}, u32[]{:S(2)}, u32[]{:S(2)}) %collective-permute-start.36) | collective-permute-done | bytes 131104 | tf_op jit(solution)/shard_map/ppermute | solution.py:36
  279.2 9.7 %shard_map.141 = (f32[4,32,256]{2,1,0:T(8,128)}, f32[4,32,256]{2,1,0:T(8,128)}, f32[4,32,256]{2,1,0:T(8,128)}, f32[4,32,256]{2,1,0:T(8,128)}, f32[4,32,256]{2,1,...) custom-call(s32[4]{0:T(128)} %and_select_fusion.9.chunks.slots, ...), custom_call_target="tpu_custom_call" | custom-call | tf_op jit(solution)/shard_map/pallas_call | solution.py:90
  292.1 4.6 %collective-permute-done.37.p1 = f32[4,32,256]{2,1,0:T(8,128)S(1)} collective-permute-done((f32[4,32,256]{2,1,0:T(8,128)}, f32[4,32,256]{2,1,0:T(8,128)S(1)}, u32[]{:S(2)}, u32[]{:S(2)}) %collective-permute-start.37) | collective-permute-done | bytes 131104 | tf_op jit(solution)/shard_map/ppermute | solution.py:36
  303.8 4.2 %collective-permute-start.41 = (f32[2,128,256]{2,1,0:T(8,128)S(1)}, f32[2,128,256]{2,1,0:T(8,128)S(1)}, u32[]{:S(2)}, u32[]{:S(2)}) collective-permute-start(f32[2,128,256]{2,1,0:T(8,128)S(1)} %get-tuple-element.141), channel_id=1, source_target_pairs={{0,12},{1,13},{2,14},{3,15},{4,0},{5,1},{6,2},{7,3},{8,4},{9,5},{1... | collective-permute-start | bytes 786440 | tf_op jit(solution)/shard_map/ppermute | solution.py:36
  308.0 4.3 %collective-permute-done.40 = f32[2,128,256]{2,1,0:T(8,128)S(1)} collective-permute-done((f32[2,128,256]{2,1,0:T(8,128)S(1)}, f32[2,128,256]{2,1,0:T(8,128)S(1)}, u32[]{:S(2)}, u32[]{:S(2)}) %collective-permute-start.40) | collective-permute-done | bytes 262176 | tf_op jit(solution)/shard_map/ppermute | solution.py:36
  312.3 3.6 collective-permute-start.42
  315.9 7.2 %collective-permute-done.42 = f32[4,128,256]{2,1,0:T(8,128)S(1)} collective-permute-done((f32[4,128,256]{2,1,0:T(8,128)S(1)}, f32[4,128,256]{2,1,0:T(8,128)S(1)}, u32[]{:S(2)}, u32[]{:S(2)}) %collective-permute-start.42) | collective-permute-done | bytes 524320 | tf_op jit(solution)/shard_map/ppermute | solution.py:36
  327.5 6.3 %collective-permute-done.46 = f32[2,128,256]{2,1,0:T(8,128)S(1)} collective-permute-done((f32[2,128,256]{2,1,0:T(8,128)S(1)}, f32[2,128,256]{2,1,0:T(8,128)S(1)}, u32[]{:S(2)}, u32[]{:S(2)}) %collective-permute-start.46) | collective-permute-done | bytes 262176 | tf_op jit(solution)/shard_map/ppermute | solution.py:36
  338.5 3.4 collective-permute-start.49
  345.0 3.6 %collective-permute-done.49.p2 = f32[4,32,256]{2,1,0:T(8,128)S(1)} collective-permute-done((f32[4,32,256]{2,1,0:T(8,128)S(1)}, f32[4,32,256]{2,1,0:T(8,128)S(1)}, u32[]{:S(2)}, u32[]{:S(2)}) %collective-permute-start.49) | collective-permute-done | bytes 131104 | tf_op jit(solution)/shard_map/ppermute | solution.py:36
  (203 shorter events, 124.2 us)
Async XLA Ops:
  1.8 16.1 %collective-permute-start.6 = (f32[4,128,256]{2,1,0:T(8,128)S(1)}, f32[4,128,256]{2,1,0:T(8,128)S(1)}, u32[]{:S(2)}, u32[]{:S(2)}) collective-permute-start(f32[4,128,256]{2,1,0:T(8,128)S(1)} %log.3), channel_id=1, source_target_pairs={{0,64},{1,65},{2,66},{3,67},{4,68},{5,69},{6,70},{7,71},{8,72},{9,... | collective-permute-start | bytes 1572872 | tf_op jit(solution)/shard_map/ppermute | solution.py:36
  3.4 14.9 %collective-permute-start.5 = (f32[4,128,256]{2,1,0:T(8,128)S(1)}, f32[4,128,256]{2,1,0:T(8,128)S(1)}, u32[]{:S(2)}, u32[]{:S(2)}) collective-permute-start(f32[4,128,256]{2,1,0:T(8,128)S(1)} %log.3), channel_id=1, source_target_pairs={{0,80},{1,81},{2,82},{3,83},{4,84},{5,85},{6,86},{7,87},{8,88},{9,... | collective-permute-start | bytes 1572872 | tf_op jit(solution)/shard_map/ppermute | solution.py:36
  5.1 24.4 %collective-permute-start.13 = (f32[4,128,256]{2,1,0:T(8,128)}, f32[4,128,256]{2,1,0:T(8,128)S(1)}, u32[]{:S(2)}, u32[]{:S(2)}) collective-permute-start(f32[4,128,256]{2,1,0:T(8,128)} %param.11), channel_id=1, source_target_pairs={{0,80},{1,81},{2,82},{3,83},{4,84},{5,85},{6,86},{7,87},{8,88},{9,... | collective-permute-start | bytes 1572872 | tf_op jit(solution)/shard_map/ppermute | solution.py:36
  6.7 25.8 %collective-permute-start.14 = (f32[4,128,256]{2,1,0:T(8,128)}, f32[4,128,256]{2,1,0:T(8,128)S(1)}, u32[]{:S(2)}, u32[]{:S(2)}) collective-permute-start(f32[4,128,256]{2,1,0:T(8,128)} %param.11), channel_id=1, source_target_pairs={{0,64},{1,65},{2,66},{3,67},{4,68},{5,69},{6,70},{7,71},{8,72},{9,... | collective-permute-start | bytes 1572872 | tf_op jit(solution)/shard_map/ppermute | solution.py:36
  17.9 15.8 %collective-permute-start.7 = (f32[2,128,256]{2,1,0:T(8,128)S(1)}, f32[2,128,256]{2,1,0:T(8,128)S(1)}, u32[]{:S(2)}, u32[]{:S(2)}) collective-permute-start(f32[2,128,256]{2,1,0:T(8,128)S(1)} %slice.64), channel_id=1, source_target_pairs={{0,64},{1,65},{2,66},{3,67},{4,68},{5,69},{6,70},{7,71},{8,72},{9,... | collective-permute-start | bytes 786440 | tf_op jit(solution)/shard_map/ppermute | solution.py:36
  19.0 16.2 %collective-permute-start.8 = (f32[2,128,256]{2,1,0:T(8,128)}, f32[2,128,256]{2,1,0:T(8,128)}, u32[]{:S(2)}, u32[]{:S(2)}) collective-permute-start(f32[2,128,256]{2,1,0:T(8,128)} %slice.65), channel_id=1, source_target_pairs={{0,80},{1,81},{2,82},{3,83},{4,84},{5,85},{6,86},{7,87},{8,88},{9,... | collective-permute-start | bytes 786440 | tf_op jit(solution)/shard_map/ppermute | solution.py:36
  29.5 10.6 %collective-permute-start.16 = (f32[2,128,256]{2,1,0:T(8,128)S(1)}, f32[2,128,256]{2,1,0:T(8,128)S(1)}, u32[]{:S(2)}, u32[]{:S(2)}) collective-permute-start(f32[2,128,256]{2,1,0:T(8,128)S(1)} %slice.67), channel_id=1, source_target_pairs={{0,80},{1,81},{2,82},{3,83},{4,84},{5,85},{6,86},{7,87},{8,88},{9,... | collective-permute-start | bytes 786440 | tf_op jit(solution)/shard_map/ppermute | solution.py:36
  44.1 16.3 %collective-permute-start.11 = (f32[4,128,256]{2,1,0:T(8,128)}, f32[4,128,256]{2,1,0:T(8,128)S(1)}, u32[]{:S(2)}, u32[]{:S(2)}) collective-permute-start(f32[4,128,256]{2,1,0:T(8,128)} %select_select_fusion.3), channel_id=1, source_target_pairs={{0,12},{1,13},{2,14},{3,15},{4,0},{5,1},{6,2},{7,3},{8,4},{9,5},{1... | collective-permute-start | bytes 1572872 | tf_op jit(solution)/shard_map/ppermute | solution.py:36
  49.4 32.2 %collective-permute-start.18 = (f32[4,128,256]{2,1,0:T(8,128)S(1)}, f32[4,128,256]{2,1,0:T(8,128)S(1)}, u32[]{:S(2)}, u32[]{:S(2)}) collective-permute-start(f32[4,128,256]{2,1,0:T(8,128)S(1)} %select_select_fusion.1), channel_id=1, source_target_pairs={{0,4},{1,5},{2,6},{3,7},{4,8},{5,9},{6,10},{7,11},{8,12},{9,13},{1... | collective-permute-start | bytes 1572872 | tf_op jit(solution)/shard_map/ppermute | solution.py:36
  61.5 27.3 %collective-permute-start.12 = (f32[4,128,256]{2,1,0:T(8,128)S(1)}, f32[4,128,256]{2,1,0:T(8,128)}, u32[]{:S(2)}, u32[]{:S(2)}) collective-permute-start(f32[4,128,256]{2,1,0:T(8,128)S(1)} %broadcast_select_fusion.4), channel_id=1, source_target_pairs={{0,8},{1,9},{2,10},{3,11},{4,12},{5,13},{6,14},{7,15},{8,0},{9,1},... | collective-permute-start | bytes 1572872 | tf_op jit(solution)/shard_map/ppermute | solution.py:36
  81.7 10.9 %collective-permute-start.19 = (f32[4,128,256]{2,1,0:T(8,128)S(1)}, f32[4,128,256]{2,1,0:T(8,128)}, u32[]{:S(2)}, u32[]{:S(2)}) collective-permute-start(f32[4,128,256]{2,1,0:T(8,128)S(1)} %broadcast_select_fusion.3), channel_id=1, source_target_pairs={{0,8},{1,9},{2,10},{3,11},{4,12},{5,13},{6,14},{7,15},{8,0},{9,1},... | collective-permute-start | bytes 1572872 | tf_op jit(solution)/shard_map/ppermute | solution.py:36
  85.6 39.0 %collective-permute-start = (f32[4,176,256]{2,1,0:T(8,128)}, f32[4,176,256]{2,1,0:T(8,128)S(1)}, u32[]{:S(2)}, u32[]{:S(2)}) collective-permute-start(f32[4,176,256]{2,1,0:T(8,128)} %get-tuple-element.67), channel_id=1, source_target_pairs={{0,1},{1,2},{2,3},{3,0},{4,5},{5,6},{6,7},{7,4},{8,9},{9,10},{10,1... | collective-permute-start | bytes 2162696 | tf_op jit(solution)/shard_map/ppermute | solution.py:36
  85.6 40.2 %collective-permute-start.1 = (f32[4,176,256]{2,1,0:T(8,128)}, f32[4,176,256]{2,1,0:T(8,128)S(1)}, u32[]{:S(2)}, u32[]{:S(2)}) collective-permute-start(f32[4,176,256]{2,1,0:T(8,128)} %get-tuple-element.68), channel_id=1, source_target_pairs={{0,2},{1,3},{2,0},{3,1},{4,6},{5,7},{6,4},{7,5},{8,10},{9,11},{10,... | collective-permute-start | bytes 2162696 | tf_op jit(solution)/shard_map/ppermute | solution.py:36
  85.6 40.2 %collective-permute-start.2 = (f32[4,176,256]{2,1,0:T(8,128)}, f32[4,176,256]{2,1,0:T(8,128)S(1)}, u32[]{:S(2)}, u32[]{:S(2)}) collective-permute-start(f32[4,176,256]{2,1,0:T(8,128)} %get-tuple-element.69), channel_id=1, source_target_pairs={{0,3},{1,0},{2,1},{3,2},{4,7},{5,4},{6,5},{7,6},{8,11},{9,8},{10,9... | collective-permute-start | bytes 2162696 | tf_op jit(solution)/shard_map/ppermute | solution.py:36
  95.9 39.3 %collective-permute-start.20 = (f32[4,96,256]{2,1,0:T(8,128)}, f32[4,96,256]{2,1,0:T(8,128)}, u32[]{:S(2)}, u32[]{:S(2)}) collective-permute-start(f32[4,96,256]{2,1,0:T(8,128)} %get-tuple-element.78), channel_id=1, source_target_pairs={{0,1},{1,2},{2,3},{3,0},{4,5},{5,6},{6,7},{7,4},{8,9},{9,10},{10,1... | collective-permute-start | bytes 1179656 | tf_op jit(solution)/shard_map/ppermute | solution.py:36
  95.9 39.3 %collective-permute-start.21 = (f32[4,96,256]{2,1,0:T(8,128)}, f32[4,96,256]{2,1,0:T(8,128)}, u32[]{:S(2)}, u32[]{:S(2)}) collective-permute-start(f32[4,96,256]{2,1,0:T(8,128)} %get-tuple-element.79), channel_id=1, source_target_pairs={{0,2},{1,3},{2,0},{3,1},{4,6},{5,7},{6,4},{7,5},{8,10},{9,11},{10,... | collective-permute-start | bytes 1179656 | tf_op jit(solution)/shard_map/ppermute | solution.py:36
  124.6 10.6 %collective-permute-start.22 = (f32[4,96,256]{2,1,0:T(8,128)}, f32[4,96,256]{2,1,0:T(8,128)}, u32[]{:S(2)}, u32[]{:S(2)}) collective-permute-start(f32[4,96,256]{2,1,0:T(8,128)} %get-tuple-element.80), channel_id=1, source_target_pairs={{0,3},{1,0},{2,1},{3,2},{4,7},{5,4},{6,5},{7,6},{8,11},{9,8},{10,9... | collective-permute-start | bytes 1179656 | tf_op jit(solution)/shard_map/ppermute | solution.py:36
  130.8 15.1 %collective-permute-start.3 = (f32[16,2,48,128]{3,2,1,0:T(8,128)}, f32[16,2,48,128]{3,2,1,0:T(8,128)S(1)}, u32[]{:S(2)}, u32[]{:S(2)}) collective-permute-start(f32[16,2,48,128]{3,2,1,0:T(8,128)} %get-tuple-element.73), channel_id=1, source_target_pairs={{0,4},{1,5},{2,6},{3,7},{4,8},{5,9},{6,10},{7,11},{8,12},{9,13},{1... | collective-permute-start | bytes 2359304 | tf_op jit(solution)/shard_map/ppermute | solution.py:36
  133.9 14.3 %collective-permute-start.4 = (f32[16,2,48,128]{3,2,1,0:T(8,128)}, f32[16,2,48,128]{3,2,1,0:T(8,128)S(1)}, u32[]{:S(2)}, u32[]{:S(2)}) collective-permute-start(f32[16,2,48,128]{3,2,1,0:T(8,128)} %get-tuple-element.74), channel_id=1, source_target_pairs={{4,0},{5,1},{6,2},{7,3},{8,4},{9,5},{10,6},{11,7},{12,8},{13,9},{1... | collective-permute-start | bytes 2359304 | tf_op jit(solution)/shard_map/ppermute | solution.py:36
  138.2 15.0 %collective-permute-start.23 = (f32[12,2,48,128]{3,2,1,0:T(8,128)}, f32[12,2,48,128]{3,2,1,0:T(8,128)S(1)}, u32[]{:S(2)}, u32[]{:S(2)}) collective-permute-start(f32[12,2,48,128]{3,2,1,0:T(8,128)} %get-tuple-element.83), channel_id=1, source_target_pairs={{0,4},{1,5},{2,6},{3,7},{4,8},{5,9},{6,10},{7,11},{8,12},{9,13},{1... | collective-permute-start | bytes 1769480 | tf_op jit(solution)/shard_map/ppermute | solution.py:36
  143.0 12.0 %collective-permute-start.24 = (f32[12,2,48,128]{3,2,1,0:T(8,128)}, f32[12,2,48,128]{3,2,1,0:T(8,128)S(1)}, u32[]{:S(2)}, u32[]{:S(2)}) collective-permute-start(f32[12,2,48,128]{3,2,1,0:T(8,128)} %get-tuple-element.84), channel_id=1, source_target_pairs={{4,0},{5,1},{6,2},{7,3},{8,4},{9,5},{10,6},{11,7},{12,8},{13,9},{1... | collective-permute-start | bytes 1769480 | tf_op jit(solution)/shard_map/ppermute | solution.py:36
  189.3 10.2 %collective-permute-start.27 = (f32[32,2,8,128]{3,2,1,0:T(8,128)}, f32[32,2,8,128]{3,2,1,0:T(8,128)S(1)}, u32[]{:S(2)}, u32[]{:S(2)}) collective-permute-start(f32[32,2,8,128]{3,2,1,0:T(8,128)} %get-tuple-element.92), channel_id=1, source_target_pairs={{0,1},{1,2},{2,3},{4,5},{5,6},{6,7},{8,9},{9,10},{10,11},{12,13},{... | collective-permute-start | bytes 786440 | tf_op jit(solution)/shard_map/ppermute | solution.py:36
  193.2 8.5 %collective-permute-start.28 = (f32[32,2,8,128]{3,2,1,0:T(8,128)}, f32[32,2,8,128]{3,2,1,0:T(8,128)S(1)}, u32[]{:S(2)}, u32[]{:S(2)}) collective-permute-start(f32[32,2,8,128]{3,2,1,0:T(8,128)} %get-tuple-element.93), channel_id=1, source_target_pairs={{1,0},{2,1},{3,2},{5,4},{6,5},{7,6},{9,8},{10,9},{11,10},{13,12},{... | collective-permute-start | bytes 786440 | tf_op jit(solution)/shard_map/ppermute | solution.py:36
  218.2 10.8 %collective-permute-start.29 = (f32[8,2,32,128]{3,2,1,0:T(8,128)}, f32[8,2,32,128]{3,2,1,0:T(8,128)S(1)}, u32[]{:S(2)}, u32[]{:S(2)}) collective-permute-start(f32[8,2,32,128]{3,2,1,0:T(8,128)} %get-tuple-element.98), channel_id=1, source_target_pairs={{0,4},{1,5},{2,6},{3,7},{4,8},{5,9},{6,10},{7,11},{8,12},{9,13},{1... | collective-permute-start | bytes 786440 | tf_op jit(solution)/shard_map/ppermute | solution.py:36
  261.7 10.6 %collective-permute-start.33 = (f32[4,2,32,128]{3,2,1,0:T(8,128)}, f32[4,2,32,128]{3,2,1,0:T(8,128)S(1)}, u32[]{:S(2)}, u32[]{:S(2)}) collective-permute-start(f32[4,2,32,128]{3,2,1,0:T(8,128)} %get-tuple-element.105), channel_id=1, source_target_pairs={{0,4},{1,5},{2,6},{3,7},{4,8},{5,9},{6,10},{7,11},{8,12},{9,13},{1... | collective-permute-start | bytes 393224 | tf_op jit(solution)/shard_map/ppermute | solution.py:36
  301.3 10.9 %collective-permute-start.40 = (f32[2,128,256]{2,1,0:T(8,128)S(1)}, f32[2,128,256]{2,1,0:T(8,128)S(1)}, u32[]{:S(2)}, u32[]{:S(2)}) collective-permute-start(f32[2,128,256]{2,1,0:T(8,128)S(1)} %get-tuple-element.140), channel_id=1, source_target_pairs={{0,4},{1,5},{2,6},{3,7},{4,8},{5,9},{6,10},{7,11},{8,12},{9,13},{1... | collective-permute-start | bytes 786440 | tf_op jit(solution)/shard_map/ppermute | solution.py:36
  303.8 8.5 %collective-permute-start.41 = (f32[2,128,256]{2,1,0:T(8,128)S(1)}, f32[2,128,256]{2,1,0:T(8,128)S(1)}, u32[]{:S(2)}, u32[]{:S(2)}) collective-permute-start(f32[2,128,256]{2,1,0:T(8,128)S(1)} %get-tuple-element.141), channel_id=1, source_target_pairs={{0,12},{1,13},{2,14},{3,15},{4,0},{5,1},{6,2},{7,3},{8,4},{9,5},{1... | collective-permute-start | bytes 786440 | tf_op jit(solution)/shard_map/ppermute | solution.py:36
  312.3 10.8 %collective-permute-start.42 = (f32[4,128,256]{2,1,0:T(8,128)S(1)}, f32[4,128,256]{2,1,0:T(8,128)S(1)}, u32[]{:S(2)}, u32[]{:S(2)}) collective-permute-start(f32[4,128,256]{2,1,0:T(8,128)S(1)} %maximum_select_fusion), channel_id=1, source_target_pairs={{0,8},{1,9},{2,10},{3,11},{4,12},{5,13},{6,14},{7,15},{8,0},{9,1},... | collective-permute-start | bytes 1572872 | tf_op jit(solution)/shard_map/ppermute | solution.py:36
  325.5 11.3 %collective-permute-start.44 = (f32[2,128,256]{2,1,0:T(8,128)S(1)}, f32[2,128,256]{2,1,0:T(8,128)S(1)}, u32[]{:S(2)}, u32[]{:S(2)}) collective-permute-start(f32[2,128,256]{2,1,0:T(8,128)S(1)} %get-tuple-element.136), channel_id=1, source_target_pairs={{0,64},{1,65},{2,66},{3,67},{4,68},{5,69},{6,70},{7,71},{8,72},{9,... | collective-permute-start | bytes 786440 | tf_op jit(solution)/shard_map/ppermute | solution.py:36
  333.9 23.4 %collective-permute-start.47 = (f32[4,128,256]{2,1,0:T(8,128)S(1)}, f32[4,128,256]{2,1,0:T(8,128)S(1)}, u32[]{:S(2)}, u32[]{:S(2)}) collective-permute-start(f32[4,128,256]{2,1,0:T(8,128)S(1)} %pad_maximum_fusion.2), channel_id=1, source_target_pairs={{0,80},{1,81},{2,82},{3,83},{4,84},{5,85},{6,86},{7,87},{8,88},{9,... | collective-permute-start | bytes 1572872 | tf_op jit(solution)/shard_map/ppermute | solution.py:36
  337.0 20.4 %collective-permute-start.45 = (f32[4,128,256]{2,1,0:T(8,128)S(1)}, f32[4,128,256]{2,1,0:T(8,128)S(1)}, u32[]{:S(2)}, u32[]{:S(2)}) collective-permute-start(f32[4,128,256]{2,1,0:T(8,128)S(1)} %pad_maximum_fusion.1), channel_id=1, source_target_pairs={{0,64},{1,65},{2,66},{3,67},{4,68},{5,69},{6,70},{7,71},{8,72},{9,... | collective-permute-start | bytes 1572872 | tf_op jit(solution)/shard_map/ppermute | solution.py:36
  338.5 10.1 %collective-permute-start.49 = (f32[4,32,256]{2,1,0:T(8,128)S(1)}, f32[4,32,256]{2,1,0:T(8,128)S(1)}, u32[]{:S(2)}, u32[]{:S(2)}) collective-permute-start(f32[4,32,256]{2,1,0:T(8,128)S(1)} %copy-done.34), channel_id=1, source_target_pairs={{0,2},{1,3},{2,0},{3,1},{4,6},{5,7},{6,4},{7,5},{8,10},{9,11},{10,... | collective-permute-start | bytes 393224 | tf_op jit(solution)/shard_map/ppermute | solution.py:36
  (58 other events, 284.1 us)

commit v3 on v2

--- a/solution.py
+++ b/solution.py
@@ -63,6 +63,16 @@
     def move(x, c, z, y):
         place = next_rows(x, z, steps)
         return None if place is None else (place[0], c, place[1], y)
+
+    return send(value, move)
+
+
+def send_corner(value, steps, cells):
+    def move(x, c, z, y):
+        place = next_rows(x, z, steps)
+        if place is None or not 0 <= y + cells < 4:
+            return None
+        return (place[0], c, place[1], y + cells)
 
     return send(value, move)
 
@@ -131,16 +141,16 @@
         return ahead[half], behind[half]
 
     def derivative(self, direction, half):
-        total = None
-        for reach in range(1, 5):
+        ahead, behind = self.both(direction, 1, half)
+        total = ahead - behind
+        for reach in range(2, 5):
             ahead, behind = self.both(direction, reach, half)
-            part = diff_coeffs[reach - 1] * (ahead - behind)
-            total = part if total is None else total + part
+            total = total + (diff_coeffs[reach - 1] / diff_coeffs[0]) * (ahead - behind)
         return total
 
     def advanced(self, half, previous, speed_sq, slopes):
         center = self.center[half]
-        lap = (3.0 * lap_coeffs[0]) * center
+        lap = (3.0 * lap_coeffs[0] / lap_coeffs[1]) * center
         derived = [None, None, None]
         for reach in range(1, 5):
             around = None
@@ -148,38 +158,38 @@
                 ahead, behind = self.both(direction, reach, half)
                 pair = ahead + behind
                 around = pair if around is None else around + pair
-                part = diff_coeffs[reach - 1] * (ahead - behind)
-                derived[direction] = part if reach == 1 else derived[direction] + part
-            lap = lap + lap_coeffs[reach] * around
+                part = ahead - behind
+                if reach > 1:
+                    part = derived[direction] + (diff_coeffs[reach - 1] / diff_coeffs[0]) * part
+                derived[direction] = part
+            if reach > 1:
+                around = (lap_coeffs[reach] / lap_coeffs[1]) * around
+            lap = lap + around
         result = 2.0 * center - previous + speed_sq * lap
         for direction in range(3):
             result = result - slopes[direction] * derived[direction]
         return result
 
 
+def row_pairs(visit, first, last, cells):
+    def step(pair, carry):
+        for row in (first + 2 * pair, first + 2 * pair + 1):
+            for cell in cells:
+                visit(row, cell)
+        return carry
+
+    lax.fori_loop(0, (last - first) // 2, step, 0)
+
+
 def over_block(visit):
-    def step(row, carry):
-        for cell in range(0, CELLS, 8):
-            visit(row, cell)
-        return carry
-
-    lax.fori_loop(0, ROWS, step, 0)
+    row_pairs(visit, 0, ROWS, range(0, CELLS, 8))
 
 
 def over_near(visit):
-    def side(row, carry):
-        for cell in range(8, 8 + CELLS, 8):
-            visit(row, cell)
-        return carry
-
-    def middle(row, carry):
-        for cell in range(4, 12 + CELLS, 8):
-            visit(row, cell)
-        return carry
-
-    lax.fori_loop(0, 4, side, 0)
-    lax.fori_loop(4, 4 + ROWS, middle, 0)
-    lax.fori_loop(4 + ROWS, 8 + ROWS, side, 0)
+    sides, middle = range(8, 8 + CELLS, 8), range(4, 12 + CELLS, 8)
+    row_pairs(visit, 0, 4, sides)
+    row_pairs(visit, 4, 4 + ROWS, middle)
+    row_pairs(visit, 4 + ROWS, 8 + ROWS, sides)
 
 
 def add_source(place, amount, first, target):
@@ -252,12 +262,48 @@
     return near
 
 
-def fill_wide(wide, block, below, above, left, right):
+def fill_wide(wide, block, halo):
+    below, above, left, right, c0, c1, c2, c3 = halo
+    low, high = slice(0, 8), slice(8 + CELLS, SPAN)
     wide[0:8, :, 8 : 8 + CELLS, :] = below[...]
     wide[8 : 8 + ROWS, :, 8 : 8 + CELLS, :] = block[...]
     wide[8 + ROWS : 16 + ROWS, :, 8 : 8 + CELLS, :] = above[...]
-    wide[:, :, 0:8, :] = left[...]
-    wide[:, :, 8 + CELLS : SPAN, :] = right[...]
+    wide[8 : 8 + ROWS, :, low, :] = left[...]
+    wide[8 : 8 + ROWS, :, high, :] = right[...]
+    wide[4:8, :, low, :] = c0[...]
+    wide[4:8, :, high, :] = c1[...]
+    wide[8 + ROWS : 12 + ROWS, :, low, :] = c2[...]
+    wide[8 + ROWS : 12 + ROWS, :, high, :] = c3[...]
+
+
+WIDE_EDGES = [region(8, CELLS)] * 2 + [region(ROWS, 8)] * 2 + [region(4, 8)] * 4
+
+
+def write_wide_edges(block, edges):
+    low, high, low_cells, high_cells, c0, c1, c2, c3 = edges
+    front, back = slice(0, 8), slice(CELLS - 8, CELLS)
+    low[...] = block[0:8]
+    high[...] = block[ROWS - 8 : ROWS]
+    low_cells[...] = block[:, :, front, :]
+    high_cells[...] = block[:, :, back, :]
+    c0[...] = block[0:4, :, front, :]
+    c1[...] = block[0:4, :, back, :]
+    c2[...] = block[ROWS - 4 : ROWS, :, front, :]
+    c3[...] = block[ROWS - 4 : ROWS, :, back, :]
+
+
+def swap_wide_edges(edges):
+    low, high, low_cells, high_cells, c0, c1, c2, c3 = edges
+    return (
+        send_group(high, 1),
+        send_group(low, -1),
+        send_cells(high_cells, 1),
+        send_cells(low_cells, -1),
+        send_corner(c3, 1, 1),
+        send_corner(c2, 1, -1),
+        send_corner(c1, -1, 1),
+        send_corner(c0, -1, -1),
+    )
 
 
 def cut_body(chunks, *refs, margins):
@@ -312,8 +358,7 @@
 def gather_blocks(pieces, slots, depths):
     outs = [region(ROWS, SPAN if depth else CELLS) for depth in depths]
     outs += [region(sum(depths), SPAN)] * 2
-    *blocks, low, high = call(functools.partial(gather_body, depths=depths), outs, 1, (slots, *pieces))
-    return blocks, send_group(high, 1), send_group(low, -1)
+    return call(functools.partial(gather_body, depths=depths), outs, 1, (slots, *pieces))
 
 
 def stack_rows(out, below, middle, above, at, depth):
@@ -340,14 +385,15 @@
         for half in (0, 1):
             value = speed_near[row, half, cut, :]
             scale = time_step_sq * value * value
-            speed_sq[row, half, cut, :] = scale
+            speed_sq[row, half, cut, :] = lap_coeffs[1] * scale
+            scale = (diff_coeffs[0] * diff_coeffs[0]) * scale
             for direction, out in enumerate((s0, s1, s2)):
                 out[row, half, cut, :] = scale * stencil.derivative(direction, half)
 
     over_near(visit)
 
 
-def forward_body(place, amount, wide, old, speed_sq, s0, s1, s2, near, new, low, high):
+def forward_body(place, amount, wide, old, speed_sq, s0, s1, s2, near, new, *edges):
     model = (speed_sq, s0, s1, s2)
     lane = lanes()
     near_step(wide, old, model, lane, near)
@@ -358,8 +404,7 @@
 
     block_step(near, of_wide(wide), model, lane, finish)
     add_source(place, amount[1], 5, new)
-    low[...] = new[0:8]
-    high[...] = new[8:ROWS]
+    write_wide_edges(new, edges)
 
 
 def write_pieces(slots, block, pieces, at):
@@ -369,13 +414,13 @@
             pieces[turn][:, at : at + CELLS, 128 * half : 128 * half + 128] = block[pl.ds(slot, 4), half]
 
 
-def turn_body(
-    place, amount, slots, block, below, above, left, right, old, speed_sq, s0, s1, s2,
-    adjoint, later, maps, near, new, adjoint_new, summed, low, high, p0, p1, p2, p3, wide,
-):
+def turn_body(place, amount, slots, block, *refs):
+    halo, refs = refs[:8], refs[8:]
+    old, speed_sq, s0, s1, s2, adjoint, later, maps, near, new, adjoint_new, summed = refs[:12]
+    edges, pieces, wide = refs[12:20], refs[20:24], refs[24]
     model = (speed_sq, s0, s1, s2)
     lane = lanes()
-    fill_wide(wide, block, below, above, left, right)
+    fill_wide(wide, block, halo)
     near_step(wide, old, model, lane, near)
     add_source(place, amount[2], 0, near)
 
@@ -395,18 +440,17 @@
         )
 
     block_step(adjoint, of_block(later), model, lane, finish_adjoint)
-    low[...] = adjoint_new[0:8]
-    high[...] = adjoint_new[8:ROWS]
-    write_pieces(slots, new, (p0, p1, p2, p3), 0)
-
-
-def adjoint_body(
-    block, below, above, left, right, old, speed_sq, s0, s1, s2, maps, u3, u2, u1, u0, sums,
-    near, new, summed, low, high, low_cells, high_cells, wide,
-):
+    write_wide_edges(adjoint_new, edges)
+    write_pieces(slots, new, pieces, 0)
+
+
+def adjoint_body(block, *refs):
+    halo, refs = refs[:8], refs[8:]
+    old, speed_sq, s0, s1, s2, maps, u3, u2, u1, u0, sums = refs[:11]
+    near, new, summed, low, high, low_cells, high_cells, wide = refs[11:]
     model = (speed_sq, s0, s1, s2)
     lane = lanes()
-    fill_wide(wide, block, below, above, left, right)
+    fill_wide(wide, block, halo)
     near_step(wide, old, model, lane, near, injected(maps, 3, u3))
 
     def finish(row, half, cut, value):
@@ -430,7 +474,7 @@
 
 def last_body(
     slots, model_slots, block, below, above, left, right, old, speed_sq, s0, s1, s2, maps,
-    u1, u0, u_before, sums, twice, p0, p1, p2, p3, q0, q1, q2, q3, near, new, image,
+    u1, u0, u_before, sums, twice, p0, p1, p2, p3, near, new, image,
 ):
     near[0:4, :, 8 : 8 + CELLS, :] = below[...]
     near[4 : 4 + ROWS, :, 8 : 8 + CELLS, :] = block[...]
@@ -448,32 +492,20 @@
         image[row, half, cut, :] = twice[row, half, cut, :] * (sums[row, half, cut, :] + value * curvature)
 
     block_step(near, of_near(old), (speed_sq, s0, s1, s2), lane, finish)
-    write_pieces(model_slots, image, (q0, q1, q2, q3), 0)
-    write_pieces(slots, new, (p0, p1, p2, p3), 0)
-
-
-def rim_body(block, below, above, low, high):
-    for out, cut in ((low, slice(0, 8)), (high, slice(CELLS - 8, CELLS))):
-        out[0:8] = below[:, :, cut, :]
-        out[8 : 8 + ROWS] = block[:, :, cut, :]
-        out[8 + ROWS : 16 + ROWS] = above[:, :, cut, :]
-
-
-def wide_halo(block, low, high):
-    below, above = send_group(high, 1), send_group(low, -1)
-    low_cells, high_cells = call(rim_body, [region(ROWS + 16, 8)] * 2, 0, (block, below, above))
-    return below, above, send_cells(high_cells, 1), send_cells(low_cells, -1)
-
-
-def spread_body(chunks, p0, p1, p2, p3, out):
+    write_pieces(model_slots, image, (p0, p1, p2, p3), 0)
+    write_pieces(slots, new, (p0, p1, p2, p3), CELLS)
+
+
+def spread_body(chunks, p0, p1, p2, p3, *outs):
     for turn, piece in enumerate((p0, p1, p2, p3)):
         first = pl.multiple_of(chunks[turn] * CELLS, CELLS)
-        out[:, pl.ds(first, CELLS), :] = piece[...]
-
-
-def to_slab(pieces, chunks):
+        for index, out in enumerate(outs):
+            out[:, pl.ds(first, CELLS), :] = piece[:, CELLS * index : CELLS * index + CELLS, :]
+
+
+def to_slabs(pieces, chunks, count):
     pieces = [pieces[0]] + [send_y(pieces[turn], turn) for turn in (1, 2, 3)]
-    return call(spread_body, [shape(4, NY, NZ)], 1, (chunks, *pieces))[0]
+    return call(spread_body, [shape(4, NY, NZ)] * count, 1, (chunks, *pieces))
 
 
 def on_device(
@@ -508,10 +540,6 @@
 
     own_core, own_step, turn_by = wanted(start)
     pair_core, pair_step, _ = wanted(partner_start)
-    low = turn_by % 2 == 1
-    high = turn_by // 2 == 1
-    high_back = ((turn_by + 1) // 2) % 2 == 1
-    high_other = jnp.where(low, high_back, high)
     turns = jnp.arange(4, dtype=jnp.int32)
     chunks_out = (y + turns) % 4
     chunks_in = (y - turns) % 4
@@ -531,22 +559,21 @@
         other = send_core(pick(pair_step))
         return jnp.where(own_core == core, pick(own_step), other)
 
-    def turned(slab, direction, high_bit):
-        slab = jnp.where(low, send_z(slab, direction), slab)
-        return jnp.where(high_bit, send_z(slab, 2), slab)
-
-    log_slab = turned(gathered(jnp.log(density)), -1, high)
-    speed_slab = turned(gathered(velocity), 1, high_other)
+    def turned(arrays, steps):
+        def branch(count):
+            return lambda *values: tuple(send_z(value, count) if count else value for value in values)
+
+        return lax.switch(steps, [branch(count) for count in (0, 1, 2, -1)], *arrays)
+
+    log_slab = gathered(jnp.log(density))
+    speed_slab = gathered(velocity)
 
     pieces = to_blocks(
         [forward_now[0], forward_old[0], adjoint_now[0], adjoint_later[0]],
         (True, True, True, False),
         chunks_out,
     )
-    (now, old, adjoint, a_later), below, above = gather_blocks(pieces, chunks_in, (8, 4, 4, 0))
-    u_wide, old_near, a_near = call(
-        fields_body, [WIDE, NEAR, NEAR], 0, (now, old, adjoint, below, above)
-    )
+    now, old, adjoint, a_later, side_low, side_high = gather_blocks(pieces, chunks_in, (8, 4, 4, 0))
 
     def local_place(cells, rows_more, cells_more):
         rows = cells // (NY * NZ) - group * ROWS + rows_more
@@ -573,26 +600,37 @@
     place = jnp.stack(source_place(4, 8) + source_place(0, 0))
     amount = wavelet[0]
 
+    log_slab, speed_slab, maps, side_low, side_high = lax.optimization_barrier(
+        (log_slab, speed_slab, maps, side_low, side_high)
+    )
+    log_slab, speed_slab = turned((log_slab, speed_slab), (4 - turn_by) % 4)
+    log_slab, speed_slab, side_low, side_high = lax.optimization_barrier(
+        (log_slab, speed_slab, side_low, side_high)
+    )
     pieces = to_blocks([log_slab, speed_slab], (True, True), chunks_out)
-    (log_mass, speed), below, above = gather_blocks(pieces, slots_in, (8, 4))
+    below, above = send_group(side_high, 1), send_group(side_low, -1)
+    u_wide, old_near, a_near = call(
+        fields_body, [WIDE, NEAR, NEAR], 0, (now, old, adjoint, below, above)
+    )
+    log_mass, speed, side_low, side_high = gather_blocks(pieces, slots_in, (8, 4))
+    below, above = send_group(side_high, 1), send_group(side_low, -1)
     *model, twice = call(
         model_body, [NEAR] * 4 + [BLOCK], 0, (log_mass, speed, below, above), (WIDE, NEAR)
     )
 
-    edges = [region(8, CELLS)] * 2
-    u1, u2, *sides = call(
-        forward_body, [NEAR, BLOCK] + edges, 2, (place, amount, u_wide, old_near, *model)
-    )
-    halo = wide_halo(u2, *sides)
-    u3, _, a3, sums, side_low, side_high, *pieces = call(
+    u1, u2, *edges = call(
+        forward_body, [NEAR, BLOCK] + WIDE_EDGES, 2, (place, amount, u_wide, old_near, *model)
+    )
+    halo = swap_wide_edges(edges)
+    u3, _, a3, sums, *rest = call(
         turn_body,
-        [NEAR, BLOCK, BLOCK, BLOCK] + edges + [shape(4, CELLS, NZ)] * 4,
+        [NEAR, BLOCK, BLOCK, BLOCK] + WIDE_EDGES + [shape(4, CELLS, NZ)] * 4,
         3,
         (place, amount, chunks_out, u2, *halo, u1, *model, a_near, a_later, maps),
         (WIDE,),
     )
-    halo = wide_halo(a3, side_low, side_high)
-    forward_last = to_slab(pieces, chunks_in)
+    halo = swap_wide_edges(rest[:8])
+    (forward_last,) = to_slabs(rest[8:], chunks_in, 1)
     a2, a1, sums, side_low, side_high, low_cells, high_cells = call(
         adjoint_body,
         [NEAR, BLOCK, BLOCK] + [region(4, CELLS)] * 2 + [region(ROWS, 8)] * 2,
@@ -608,24 +646,17 @@
     )
     pieces = call(
         last_body,
-        [shape(4, CELLS, NZ)] * 8,
+        [shape(4, 2 * CELLS, NZ)] * 4,
         2,
         (chunks_out, slots_out, a1, *halo, a2, *model, maps, u1, u_wide, old_near, sums, twice),
         (NEAR, BLOCK, BLOCK),
     )
-    image = to_slab(pieces[4:], chunks_in)
-    image, *pieces = lax.optimization_barrier((image, *pieces[:4]))
-    adjoint_first = to_slab(pieces, chunks_in)
+    image, adjoint_first = to_slabs(pieces, chunks_in, 2)
 
     def both(first_half, second_half):
         return jnp.concatenate([first_half, second_half])
 
-    image = jnp.where(low, both(send_z(image[0:2], 1), send_z(image[2:4], -1)), image)
-    arrived = send_z(image, 2)
-    image = both(
-        jnp.where(high, arrived[0:2], image[0:2]),
-        jnp.where(high_other, arrived[2:4], image[2:4]),
-    )
+    (image,) = turned((image,), turn_by)
     other = send_core(image)
 
     def share(step):

time: 358 us -> 342 us (0.955); the launches traced: 358 us -> 347 us
  starting transfers between devices: 88 us -> 107 us
  waiting for transfers between devices: 151 us -> 138 us
  Pallas kernels: 84.3 us -> 71.5 us
  other arithmetic: 11.9 us -> 8.18 us
    ppermute x54 -> x55, starting transfers between devices: 88 us -> 107 us  [send(): return lax.ppermute(value, ('shot', 'sub'), pairs_by(move))]
    pallas_call x15 -> x12, Pallas kernels: 84.3 us -> 71.5 us  [call(): pl.pallas_call(body, out_shape=tuple(outs), in_specs=specs, out_specs=tup...]
    ppermute x54 -> x55, waiting for transfers between devices: 151 us -> 138 us  [send(): return lax.ppermute(value, ('shot', 'sub'), pairs_by(move))]
    unnamed x74 -> x86, local copies, waits for them, and re-layouts: 7.79 us -> 7.24 us
  transfers between devices with their start and end apart: 54 -> 55, of which waited for: 33 -> 23; matrix products, arithmetic and copies ran while one was open for 5% -> 4% of each run, Pallas kernels for 6% -> 5%
where the time goes in v3:
time: 342 us; the launch traced here: 347 us
  waiting for transfers between devices  138 us (40%)
  starting transfers between devices  107 us (31%)
  Pallas kernels  71.5 us (21%)
  local copies, waits for them, and re-layouts  11.6 us (3%)
  other arithmetic  8.18 us (2%)
  between operations  5.68 us (2%)
  matrix products  5.02 us (1%)
    ppermute x55, waiting for transfers between devices, send(): return lax.ppermute(value, ('shot', 'sub'), pairs_by(move))  138 us
    ppermute x55, starting transfers between devices, send(): return lax.ppermute(value, ('shot', 'sub'), pairs_by(move))  107 us
    pallas_call x12, Pallas kernels, call(): pl.pallas_call(body, out_shape=tuple(outs), in_specs=specs, out_specs=tup...  71.5 us
    unnamed x86, local copies, waits for them, and re-layouts  7.24 us
  transfers between devices with their start and end apart: 55, of which 23 were waited for; matrix products, arithmetic and copies ran while one was open for 4% of the time, Pallas kernels for 5%

profile of v3, /device:TPU:0, one launch (start us, length us, event | category | flops | bytes accessed | tf_op | source)
XLA Modules:
  0.0 347.2 jit_solution(18182374049640107644)
XLA Ops:
  9.4 8.5 %collective-permute-done.13 = f32[4,128,256]{2,1,0:T(8,128)S(1)} collective-permute-done((f32[4,128,256]{2,1,0:T(8,128)S(1)}, f32[4,128,256]{2,1,0:T(8,128)S(1)}, u32[]{:S(2)}, u32[]{:S(2)}) %collective-permute-start.13) | collective-permute-done | bytes 524320 | tf_op jit(solution)/shard_map/ppermute | solution.py:36
  38.9 5.7 %collective-permute-done.20 = f32[2,128,256]{2,1,0:T(8,128)S(1)} collective-permute-done((f32[2,128,256]{2,1,0:T(8,128)S(1)}, f32[2,128,256]{2,1,0:T(8,128)S(1)}, u32[]{:S(2)}, u32[]{:S(2)}) %collective-permute-start.20) | collective-permute-done | bytes 262176 | tf_op jit(solution)/shard_map/ppermute | solution.py:36
  46.1 5.0 %fusion.refs_15_.refs_13_.maps = f32[24,2,48,640]{3,2,1,0:T(8,128)} fusion(f32[256,640,1,1]{0,1,3,2:T(8,128)S(1)} %bitcast.35, s32[256]{0:T(256)S(1)} %bitcast.43, s32[24,2,48]{2,1,0:T(2,128)S(1)} %multiply_add_fusion), kind=kOutput, calls=%fused_computation | convolution fusion | flops 4530438144 | bytes 6563840 | tf_op jit(solution)/shard_map/dot_general | solution.py:592
  52.5 7.0 %collective-permute-done.10.refs_2_ = f32[4,176,256]{2,1,0:T(8,128)} collective-permute-done((f32[4,176,256]{2,1,0:T(8,128)}, f32[4,176,256]{2,1,0:T(8,128)}, u32[]{:S(2)}, u32[]{:S(2)}) %collective-permute-start.10) | collective-permute-done | bytes 720928 | tf_op jit(solution)/shard_map/ppermute | solution.py:36
  62.4 4.0 %shard_map.131 = (f32[16,2,48,128]{3,2,1,0:T(8,128)}, f32[16,2,48,128]{3,2,1,0:T(8,128)}, f32[16,2,48,128]{3,2,1,0:T(8,128)}, f32[16,2,32,128]{3,2,1,0:T(8,128)}...) custom-call(s32[4]{0:T(128)} %and_select_fusion.10.slots.chunks, f32[4,176,256]{2,1,0:T(8,128)} %get-tuple-element.109.refs_0_, ...), custom_call_target="tpu_custom_call" | custom-call | tf_op jit(solution)/shard_map/pallas_call | solution.py:100
  68.5 20.9 %conditional.2 = ((f32[4,128,256]{2,1,0:T(8,128)S(1)}, f32[4,128,256]{2,1,0:T(8,128)S(1)})) conditional(s32[]{:T(128)} %clamp.7, (f32[4,128,256]{2,1,0:T(8,128)S(1)}, f32[4,128,256]{2,1,0:T(8,128)S(1)}) %tuple.58, (f32[4,128,256]{2,1,0:T(8,128)S(1)}, f32[4,128,256]{2,1,0:T(8,128)S(1)}) %tuple.59, ...), branch_computations={%region_0.1_spmd, %region_1.2_spmd, %region_2.3_spmd, %region_3.4_... | conditional | bytes 6291560 | solution.py:566
  68.5 3.9 %collective-permute-start.2 = (f32[4,128,256]{2,1,0:T(8,128)S(1)}, f32[4,128,256]{2,1,0:T(8,128)S(1)}, u32[]{:S(2)}, u32[]{:S(2)}) collective-permute-start(f32[4,128,256]{2,1,0:T(8,128)S(1)} %get-tuple-element.27), channel_id=1, source_target_pairs={{0,8},{1,9},{2,10},{3,11},{4,12},{5,13},{6,14},{7,15},{8,0},{9,1},... | collective-permute-start | bytes 1572872 | tf_op jit(solution)/shard_map/cond/branch_2_fun/ppermute | solution.py:36
  72.4 7.1 %collective-permute-done.2 = f32[4,128,256]{2,1,0:T(8,128)S(1)} collective-permute-done((f32[4,128,256]{2,1,0:T(8,128)S(1)}, f32[4,128,256]{2,1,0:T(8,128)S(1)}, u32[]{:S(2)}, u32[]{:S(2)}) %collective-permute-start.2) | collective-permute-done | bytes 524320 | tf_op jit(solution)/shard_map/cond/branch_2_fun/ppermute | solution.py:36
  79.5 9.8 %collective-permute-done.3 = f32[4,128,256]{2,1,0:T(8,128)S(1)} collective-permute-done((f32[4,128,256]{2,1,0:T(8,128)S(1)}, f32[4,128,256]{2,1,0:T(8,128)S(1)}, u32[]{:S(2)}, u32[]{:S(2)}) %collective-permute-start.3) | collective-permute-done | bytes 524320 | tf_op jit(solution)/shard_map/cond/branch_2_fun/ppermute | solution.py:36
  99.4 5.3 %collective-permute-done.25.refs_1_ = f32[4,96,256]{2,1,0:T(8,128)S(1)} collective-permute-done((f32[4,96,256]{2,1,0:T(8,128)}, f32[4,96,256]{2,1,0:T(8,128)S(1)}, u32[]{:S(2)}, u32[]{:S(2)}) %collective-permute-start.25) | collective-permute-done | bytes 393248 | tf_op jit(solution)/shard_map/ppermute | solution.py:36
  114.8 4.0 %shard_map.132 = (f32[32,2,48,128]{3,2,1,0:T(8,128)}, f32[24,2,48,128]{3,2,1,0:T(8,128)}, f32[24,2,48,128]{3,2,1,0:T(8,128)}) custom-call(f32[16,2,48,128]{3,2,1,0:T(8,128)} %get-tuple-element.113.now, f32[16,2,48,128]{3,2,1,0:T(8,128)} %get-tuple-element.114.old, f32[16,2,48,128]{3,2,1,0:T(8,128)} %get-tuple-element.115.adjoint, ...), custom_call_target="tpu_custom_call" | custom-call | tf_op jit(solution)/shard_map/pallas_call | solution.py:100
  118.8 6.3 %collective-permute-done.29.above = f32[12,2,48,128]{3,2,1,0:T(8,128)S(1)} collective-permute-done((f32[12,2,48,128]{3,2,1,0:T(8,128)}, f32[12,2,48,128]{3,2,1,0:T(8,128)S(1)}, u32[]{:S(2)}, u32[]{:S(2)}) %collective-permute-start.29) | collective-permute-done | bytes 589856 | tf_op jit(solution)/shard_map/ppermute | solution.py:36
  126.0 7.0 %shard_map.135 = (f32[24,2,48,128]{3,2,1,0:T(8,128)}, f32[24,2,48,128]{3,2,1,0:T(8,128)}, f32[24,2,48,128]{3,2,1,0:T(8,128)}, f32[24,2,48,128]{3,2,1,0:T(8,128)}, f32[16,2,32,128]{3,2,1,0:T(8,128)}) custom-call(f32[16,2,48,128]{3,2,1,0:T(8,128)} %get-tuple-element.134.log_mass, f32[16,2,48,128]{3,2,1,0:T(8,128)} %get-tuple-element.135.speed, ...), custom_call_target="tpu_custom_call" | custom-call | tf_op jit(solution)/shard_map/pallas_call | solution.py:100
  132.9 9.2 %shard_map.136 = (f32[24,2,48,128]{3,2,1,0:T(8,128)}, f32[16,2,32,128]{3,2,1,0:T(8,128)}, f32[8,2,32,128]{3,2,1,0:T(8,128)}, f32[8,2,32,128]{3,2,1,0:T(8,128)}, ...) custom-call(s32[10]{0:T(128)} %stack.45.place, ...), custom_call_target="tpu_custom_call" | custom-call | tf_op jit(solution)/shard_map/pallas_call | solution.py:100
  142.1 3.9 %collective-permute-start.30 = (f32[8,2,32,128]{3,2,1,0:T(8,128)}, f32[8,2,32,128]{3,2,1,0:T(8,128)S(1)}, u32[]{:S(2)}, u32[]{:S(2)}) collective-permute-start(f32[8,2,32,128]{3,2,1,0:T(8,128)} %get-tuple-element.143), channel_id=1, source_target_pairs={{0,4},{1,5},{2,6},{3,7},{4,8},{5,9},{6,10},{7,11},{8,12},{9,13},{1... | collective-permute-start | bytes 786440 | tf_op jit(solution)/shard_map/ppermute | solution.py:36
  147.4 5.6 %collective-permute-start.34 = (f32[4,2,8,128]{3,2,1,0:T(8,128)}, f32[4,2,8,128]{3,2,1,0:T(8,128)S(1)}, u32[]{:S(2)}, u32[]{:S(2)}) collective-permute-start(f32[4,2,8,128]{3,2,1,0:T(8,128)} %get-tuple-element.147), channel_id=1, source_target_pairs={{0,5},{1,6},{2,7},{4,9},{5,10},{6,11},{8,13},{9,14},{10,15},{12,17... | collective-permute-start | bytes 98312 | tf_op jit(solution)/shard_map/ppermute | solution.py:36
  159.5 22.3 %collective-permute-done.37.refs_7_ = f32[4,2,8,128]{3,2,1,0:T(8,128)S(1)} collective-permute-done((f32[4,2,8,128]{3,2,1,0:T(8,128)}, f32[4,2,8,128]{3,2,1,0:T(8,128)S(1)}, u32[]{:S(2)}, u32[]{:S(2)}) %collective-permute-start.37) | collective-permute-done | bytes 32800 | tf_op jit(solution)/shard_map/ppermute | solution.py:36
  182.7 13.7 %shard_map.137 = (f32[24,2,48,128]{3,2,1,0:T(8,128)}, f32[16,2,32,128]{3,2,1,0:T(8,128)}, f32[16,2,32,128]{3,2,1,0:T(8,128)}, f32[16,2,32,128]{3,2,1,0:T(8,128)}...) custom-call(s32[10]{0:T(128)} %stack.45.place, ...), custom_call_target="tpu_custom_call" | custom-call | tf_op jit(solution)/shard_map/pallas_call | solution.py:100
  196.4 3.9 %collective-permute-start.38 = (f32[8,2,32,128]{3,2,1,0:T(8,128)}, f32[8,2,32,128]{3,2,1,0:T(8,128)S(1)}, u32[]{:S(2)}, u32[]{:S(2)}) collective-permute-start(f32[8,2,32,128]{3,2,1,0:T(8,128)} %get-tuple-element.156), channel_id=1, source_target_pairs={{0,4},{1,5},{2,6},{3,7},{4,8},{5,9},{6,10},{7,11},{8,12},{9,13},{1... | collective-permute-start | bytes 786440 | tf_op jit(solution)/shard_map/ppermute | solution.py:36
  201.6 10.9 %collective-permute-start.42 = (f32[4,2,8,128]{3,2,1,0:T(8,128)}, f32[4,2,8,128]{3,2,1,0:T(8,128)S(1)}, u32[]{:S(2)}, u32[]{:S(2)}) collective-permute-start(f32[4,2,8,128]{3,2,1,0:T(8,128)} %get-tuple-element.160), channel_id=1, source_target_pairs={{0,5},{1,6},{2,7},{4,9},{5,10},{6,11},{8,13},{9,14},{10,15},{12,17... | collective-permute-start | bytes 98312 | tf_op jit(solution)/shard_map/ppermute | solution.py:36
  218.0 25.4 %collective-permute-done.45.refs_7_ = f32[4,2,8,128]{3,2,1,0:T(8,128)S(1)} collective-permute-done((f32[4,2,8,128]{3,2,1,0:T(8,128)}, f32[4,2,8,128]{3,2,1,0:T(8,128)S(1)}, u32[]{:S(2)}, u32[]{:S(2)}) %collective-permute-start.45) | collective-permute-done | bytes 32800 | tf_op jit(solution)/shard_map/ppermute | solution.py:36
  244.3 12.5 %shard_map.138 = (f32[24,2,48,128]{3,2,1,0:T(8,128)}, f32[16,2,32,128]{3,2,1,0:T(8,128)}, f32[16,2,32,128]{3,2,1,0:T(8,128)}, f32[4,2,32,128]{3,2,1,0:T(8,128)},...) custom-call(f32[16,2,32,128]{3,2,1,0:T(8,128)} %get-tuple-element.155.block, ...), custom_call_target="tpu_custom_call" | custom-call | tf_op jit(solution)/shard_map/pallas_call | solution.py:100
  256.8 3.9 %collective-permute-start.46 = (f32[4,2,32,128]{3,2,1,0:T(8,128)}, f32[4,2,32,128]{3,2,1,0:T(8,128)S(1)}, u32[]{:S(2)}, u32[]{:S(2)}) collective-permute-start(f32[4,2,32,128]{3,2,1,0:T(8,128)} %get-tuple-element.167), channel_id=1, source_target_pairs={{0,4},{1,5},{2,6},{3,7},{4,8},{5,9},{6,10},{7,11},{8,12},{9,13},{1... | collective-permute-start | bytes 393224 | tf_op jit(solution)/shard_map/ppermute | solution.py:36
  262.0 4.1 %collective-permute-start.48 = (f32[16,2,8,128]{3,2,1,0:T(8,128)}, f32[16,2,8,128]{3,2,1,0:T(8,128)S(1)}, u32[]{:S(2)}, u32[]{:S(2)}) collective-permute-start(f32[16,2,8,128]{3,2,1,0:T(8,128)} %get-tuple-element.169), channel_id=1, source_target_pairs={{0,1},{1,2},{2,3},{4,5},{5,6},{6,7},{8,9},{9,10},{10,11},{12,13},{... | collective-permute-start | bytes 393224 | tf_op jit(solution)/shard_map/ppermute | solution.py:36
  268.0 5.3 %collective-permute-done.47.above = f32[4,2,32,128]{3,2,1,0:T(8,128)S(1)} collective-permute-done((f32[4,2,32,128]{3,2,1,0:T(8,128)}, f32[4,2,32,128]{3,2,1,0:T(8,128)S(1)}, u32[]{:S(2)}, u32[]{:S(2)}) %collective-permute-start.47) | collective-permute-done | bytes 131104 | tf_op jit(solution)/shard_map/ppermute | solution.py:36
  274.0 8.9 %shard_map.139 = (f32[4,64,256]{2,1,0:T(8,128)}, f32[4,64,256]{2,1,0:T(8,128)}, f32[4,64,256]{2,1,0:T(8,128)}, f32[4,64,256]{2,1,0:T(8,128)}) custom-call(s32[4]{0:T(128)} %and_select_fusion.9.chunks.slots, s32[4]{0:T(128)} %and_select_fusion.8.model_slots, f32[16,2,32,128]{3,2,1,0:T(8,128)} %get-tuple-element.166.block, f32[4,2,32,128]{3,2,1,0:T(8,128)} %copy-done.25, ...), custom_call_target="tpu_custom_call" | custom-call | tf_op jit(solution)/shard_map/pallas_call | solution.py:100
  286.9 6.7 %collective-permute-done.50.p1 = f32[4,64,256]{2,1,0:T(8,128)S(1)} collective-permute-done((f32[4,64,256]{2,1,0:T(8,128)}, f32[4,64,256]{2,1,0:T(8,128)S(1)}, u32[]{:S(2)}, u32[]{:S(2)}) %collective-permute-start.50) | collective-permute-done | bytes 262176 | tf_op jit(solution)/shard_map/ppermute | solution.py:36
  297.3 20.2 %conditional.3 = (f32[4,128,256]{2,1,0:T(8,128)S(1)}) conditional(s32[]{:T(128)} %clamp.6, f32[4,128,256]{2,1,0:T(8,128)S(1)} %get-tuple-element.178, f32[4,128,256]{2,1,0:T(8,128)S(1)} %get-tuple-element.178, f32[4,128,256]{2,1,0:T(8,128)S(1)} %get-tuple-element.178, f32[4,128,256]{2,1,0:T(8,128)S(1)} %get-tuple-element.178), branch_computations={%region_4.5_spmd, %region_5.6_spmd, %region_6.7_spmd, %region_7.8_... | conditional | bytes 3145776 | solution.py:566
  297.3 13.0 %collective-permute-start.7 = (f32[4,128,256]{2,1,0:T(8,128)S(1)}, f32[4,128,256]{2,1,0:T(8,128)S(1)}, u32[]{:S(2)}, u32[]{:S(2)}) collective-permute-start(f32[4,128,256]{2,1,0:T(8,128)S(1)} %param.6), channel_id=1, source_target_pairs={{0,8},{1,9},{2,10},{3,11},{4,12},{5,13},{6,14},{7,15},{8,0},{9,1},... | collective-permute-start | bytes 1572872 | tf_op jit(solution)/shard_map/cond/branch_2_fun/ppermute | solution.py:36
  310.3 7.2 %collective-permute-done.7 = f32[4,128,256]{2,1,0:T(8,128)S(1)} collective-permute-done((f32[4,128,256]{2,1,0:T(8,128)S(1)}, f32[4,128,256]{2,1,0:T(8,128)S(1)}, u32[]{:S(2)}, u32[]{:S(2)}) %collective-permute-start.7) | collective-permute-done | bytes 524320 | tf_op jit(solution)/shard_map/cond/branch_2_fun/ppermute | solution.py:36
  321.8 6.3 %collective-permute-done.56 = f32[2,128,256]{2,1,0:T(8,128)S(1)} collective-permute-done((f32[2,128,256]{2,1,0:T(8,128)S(1)}, f32[2,128,256]{2,1,0:T(8,128)S(1)}, u32[]{:S(2)}, u32[]{:S(2)}) %collective-permute-start.56) | collective-permute-done | bytes 262176 | tf_op jit(solution)/shard_map/ppermute | solution.py:36
  335.5 4.3 %collective-permute-done.58.p1 = f32[4,32,256]{2,1,0:T(8,128)S(1)} collective-permute-done((f32[4,32,256]{2,1,0:T(8,128)}, f32[4,32,256]{2,1,0:T(8,128)S(1)}, u32[]{:S(2)}, u32[]{:S(2)}) %collective-permute-start.58) | collective-permute-done | bytes 131104 | tf_op jit(solution)/shard_map/ppermute | solution.py:36
  (211 shorter events, 100.9 us)
Async XLA Ops:
  1.8 16.1 %collective-permute-start.13 = (f32[4,128,256]{2,1,0:T(8,128)S(1)}, f32[4,128,256]{2,1,0:T(8,128)S(1)}, u32[]{:S(2)}, u32[]{:S(2)}) collective-permute-start(f32[4,128,256]{2,1,0:T(8,128)S(1)} %log.3), channel_id=1, source_target_pairs={{0,64},{1,65},{2,66},{3,67},{4,68},{5,69},{6,70},{7,71},{8,72},{9,... | collective-permute-start | bytes 1572872 | tf_op jit(solution)/shard_map/ppermute | solution.py:36
  3.4 14.9 %collective-permute-start.12 = (f32[4,128,256]{2,1,0:T(8,128)S(1)}, f32[4,128,256]{2,1,0:T(8,128)S(1)}, u32[]{:S(2)}, u32[]{:S(2)}) collective-permute-start(f32[4,128,256]{2,1,0:T(8,128)S(1)} %log.3), channel_id=1, source_target_pairs={{0,80},{1,81},{2,82},{3,83},{4,84},{5,85},{6,86},{7,87},{8,88},{9,... | collective-permute-start | bytes 1572872 | tf_op jit(solution)/shard_map/ppermute | solution.py:36
  5.1 25.2 %collective-permute-start.18 = (f32[4,128,256]{2,1,0:T(8,128)}, f32[4,128,256]{2,1,0:T(8,128)S(1)}, u32[]{:S(2)}, u32[]{:S(2)}) collective-permute-start(f32[4,128,256]{2,1,0:T(8,128)} %param.19), channel_id=1, source_target_pairs={{0,80},{1,81},{2,82},{3,83},{4,84},{5,85},{6,86},{7,87},{8,88},{9,... | collective-permute-start | bytes 1572872 | tf_op jit(solution)/shard_map/ppermute | solution.py:36
  6.7 26.5 %collective-permute-start.19 = (f32[4,128,256]{2,1,0:T(8,128)}, f32[4,128,256]{2,1,0:T(8,128)S(1)}, u32[]{:S(2)}, u32[]{:S(2)}) collective-permute-start(f32[4,128,256]{2,1,0:T(8,128)} %param.19), channel_id=1, source_target_pairs={{0,64},{1,65},{2,66},{3,67},{4,68},{5,69},{6,70},{7,71},{8,72},{9,... | collective-permute-start | bytes 1572872 | tf_op jit(solution)/shard_map/ppermute | solution.py:36
  7.1 18.8 %collective-permute-start.16 = (s32[1]{0:T(128)}, s32[1]{0:T(128)}, u32[]{:S(2)}, u32[]{:S(2)}) collective-permute-start(s32[1]{0:T(128)} %param.21), channel_id=1, source_target_pairs={{0,32},{1,33},{2,34},{3,35},{4,36},{5,37},{6,38},{7,39},{8,40},{9,... | collective-permute-start | bytes 20 | tf_op jit(solution)/shard_map/ppermute | solution.py:36
  17.9 16.8 %collective-permute-start.14 = (f32[2,128,256]{2,1,0:T(8,128)S(1)}, f32[2,128,256]{2,1,0:T(8,128)S(1)}, u32[]{:S(2)}, u32[]{:S(2)}) collective-permute-start(f32[2,128,256]{2,1,0:T(8,128)S(1)} %slice.40), channel_id=1, source_target_pairs={{0,64},{1,65},{2,66},{3,67},{4,68},{5,69},{6,70},{7,71},{8,72},{9,... | collective-permute-start | bytes 786440 | tf_op jit(solution)/shard_map/ppermute | solution.py:36
  19.1 17.8 %collective-permute-start.15 = (f32[2,128,256]{2,1,0:T(8,128)}, f32[2,128,256]{2,1,0:T(8,128)}, u32[]{:S(2)}, u32[]{:S(2)}) collective-permute-start(f32[2,128,256]{2,1,0:T(8,128)} %slice.41), channel_id=1, source_target_pairs={{0,80},{1,81},{2,82},{3,83},{4,84},{5,85},{6,86},{7,87},{8,88},{9,... | collective-permute-start | bytes 786440 | tf_op jit(solution)/shard_map/ppermute | solution.py:36
  25.9 26.6 %collective-permute-start.9 = (f32[4,176,256]{2,1,0:T(8,128)}, f32[4,176,256]{2,1,0:T(8,128)}, u32[]{:S(2)}, u32[]{:S(2)}) collective-permute-start(f32[4,176,256]{2,1,0:T(8,128)} %get-tuple-element.110), channel_id=1, source_target_pairs={{0,1},{1,2},{2,3},{3,0},{4,5},{5,6},{6,7},{7,4},{8,9},{9,10},{10,1... | collective-permute-start | bytes 2162696 | tf_op jit(solution)/shard_map/ppermute | solution.py:36
  30.2 29.3 %collective-permute-start.10 = (f32[4,176,256]{2,1,0:T(8,128)}, f32[4,176,256]{2,1,0:T(8,128)}, u32[]{:S(2)}, u32[]{:S(2)}) collective-permute-start(f32[4,176,256]{2,1,0:T(8,128)} %get-tuple-element.111), channel_id=1, source_target_pairs={{0,2},{1,3},{2,0},{3,1},{4,6},{5,7},{6,4},{7,5},{8,10},{9,11},{10,... | collective-permute-start | bytes 2162696 | tf_op jit(solution)/shard_map/ppermute | solution.py:36
  33.3 29.1 %collective-permute-start.11 = (f32[4,176,256]{2,1,0:T(8,128)}, f32[4,176,256]{2,1,0:T(8,128)}, u32[]{:S(2)}, u32[]{:S(2)}) collective-permute-start(f32[4,176,256]{2,1,0:T(8,128)} %get-tuple-element.112), channel_id=1, source_target_pairs={{0,3},{1,0},{2,1},{3,2},{4,7},{5,4},{6,5},{7,6},{8,11},{9,8},{10,9... | collective-permute-start | bytes 2162696 | tf_op jit(solution)/shard_map/ppermute | solution.py:36
  44.6 21.8 %collective-permute-start.17 = (f32[4,128,256]{2,1,0:T(8,128)}, f32[4,128,256]{2,1,0:T(8,128)}, u32[]{:S(2)}, u32[]{:S(2)}) collective-permute-start(f32[4,128,256]{2,1,0:T(8,128)} %select_select_fusion.2), channel_id=1, source_target_pairs={{0,32},{1,33},{2,34},{3,35},{4,36},{5,37},{6,38},{7,39},{8,40},{9,... | collective-permute-start | bytes 1572872 | tf_op jit(solution)/shard_map/ppermute | solution.py:36
  45.6 21.7 %collective-permute-start.22 = (f32[4,128,256]{2,1,0:T(8,128)}, f32[4,128,256]{2,1,0:T(8,128)}, u32[]{:S(2)}, u32[]{:S(2)}) collective-permute-start(f32[4,128,256]{2,1,0:T(8,128)} %select_select_fusion), channel_id=1, source_target_pairs={{0,32},{1,33},{2,34},{3,35},{4,36},{5,37},{6,38},{7,39},{8,40},{9,... | collective-permute-start | bytes 1572872 | tf_op jit(solution)/shard_map/ppermute | solution.py:36
  72.3 17.0 %collective-permute-start.3 = (f32[4,128,256]{2,1,0:T(8,128)S(1)}, f32[4,128,256]{2,1,0:T(8,128)S(1)}, u32[]{:S(2)}, u32[]{:S(2)}) collective-permute-start(f32[4,128,256]{2,1,0:T(8,128)S(1)} %get-tuple-element.28), channel_id=1, source_target_pairs={{0,8},{1,9},{2,10},{3,11},{4,12},{5,13},{6,14},{7,15},{8,0},{9,1},... | collective-permute-start | bytes 1572872 | tf_op jit(solution)/shard_map/cond/branch_2_fun/ppermute | solution.py:36
  91.3 13.4 %collective-permute-start.25 = (f32[4,96,256]{2,1,0:T(8,128)}, f32[4,96,256]{2,1,0:T(8,128)S(1)}, u32[]{:S(2)}, u32[]{:S(2)}) collective-permute-start(f32[4,96,256]{2,1,0:T(8,128)} %get-tuple-element.131), channel_id=1, source_target_pairs={{0,1},{1,2},{2,3},{3,0},{4,5},{5,6},{6,7},{7,4},{8,9},{9,10},{10,1... | collective-permute-start | bytes 1179656 | tf_op jit(solution)/shard_map/ppermute | solution.py:36
  96.2 17.2 %collective-permute-start.23 = (f32[16,2,48,128]{3,2,1,0:T(8,128)}, f32[16,2,48,128]{3,2,1,0:T(8,128)S(1)}, u32[]{:S(2)}, u32[]{:S(2)}) collective-permute-start(f32[16,2,48,128]{3,2,1,0:T(8,128)} %get-tuple-element.124), channel_id=1, source_target_pairs={{0,4},{1,5},{2,6},{3,7},{4,8},{5,9},{6,10},{7,11},{8,12},{9,13},{1... | collective-permute-start | bytes 2359304 | tf_op jit(solution)/shard_map/ppermute | solution.py:36
  97.5 16.4 %collective-permute-start.24 = (f32[16,2,48,128]{3,2,1,0:T(8,128)S(1)}, f32[16,2,48,128]{3,2,1,0:T(8,128)S(1)}, u32[]{:S(2)}, u32[]{:S(2)}) collective-permute-start(f32[16,2,48,128]{3,2,1,0:T(8,128)S(1)} %copy-done.41), channel_id=1, source_target_pairs={{4,0},{5,1},{6,2},{7,3},{8,4},{9,5},{10,6},{11,7},{12,8},{13,9},{1... | collective-permute-start | bytes 2359304 | tf_op jit(solution)/shard_map/ppermute | solution.py:36
  110.6 14.5 %collective-permute-start.29 = (f32[12,2,48,128]{3,2,1,0:T(8,128)}, f32[12,2,48,128]{3,2,1,0:T(8,128)S(1)}, u32[]{:S(2)}, u32[]{:S(2)}) collective-permute-start(f32[12,2,48,128]{3,2,1,0:T(8,128)} %get-tuple-element.137), channel_id=1, source_target_pairs={{4,0},{5,1},{6,2},{7,3},{8,4},{9,5},{10,6},{11,7},{12,8},{13,9},{1... | collective-permute-start | bytes 1769480 | tf_op jit(solution)/shard_map/ppermute | solution.py:36
  142.1 39.7 %collective-permute-start.30 = (f32[8,2,32,128]{3,2,1,0:T(8,128)}, f32[8,2,32,128]{3,2,1,0:T(8,128)S(1)}, u32[]{:S(2)}, u32[]{:S(2)}) collective-permute-start(f32[8,2,32,128]{3,2,1,0:T(8,128)} %get-tuple-element.143), channel_id=1, source_target_pairs={{0,4},{1,5},{2,6},{3,7},{4,8},{5,9},{6,10},{7,11},{8,12},{9,13},{1... | collective-permute-start | bytes 786440 | tf_op jit(solution)/shard_map/ppermute | solution.py:36
  146.1 35.8 %collective-permute-start.31 = (f32[8,2,32,128]{3,2,1,0:T(8,128)}, f32[8,2,32,128]{3,2,1,0:T(8,128)S(1)}, u32[]{:S(2)}, u32[]{:S(2)}) collective-permute-start(f32[8,2,32,128]{3,2,1,0:T(8,128)} %get-tuple-element.144), channel_id=1, source_target_pairs={{4,0},{5,1},{6,2},{7,3},{8,4},{9,5},{10,6},{11,7},{12,8},{13,9},{1... | collective-permute-start | bytes 786440 | tf_op jit(solution)/shard_map/ppermute | solution.py:36
  153.0 28.8 %collective-permute-start.32 = (f32[16,2,8,128]{3,2,1,0:T(8,128)}, f32[16,2,8,128]{3,2,1,0:T(8,128)S(1)}, u32[]{:S(2)}, u32[]{:S(2)}) collective-permute-start(f32[16,2,8,128]{3,2,1,0:T(8,128)} %get-tuple-element.145), channel_id=1, source_target_pairs={{0,1},{1,2},{2,3},{4,5},{5,6},{6,7},{8,9},{9,10},{10,11},{12,13},{... | collective-permute-start | bytes 393224 | tf_op jit(solution)/shard_map/ppermute | solution.py:36
  155.5 26.3 %collective-permute-start.33 = (f32[16,2,8,128]{3,2,1,0:T(8,128)}, f32[16,2,8,128]{3,2,1,0:T(8,128)S(1)}, u32[]{:S(2)}, u32[]{:S(2)}) collective-permute-start(f32[16,2,8,128]{3,2,1,0:T(8,128)} %get-tuple-element.146), channel_id=1, source_target_pairs={{1,0},{2,1},{3,2},{5,4},{6,5},{7,6},{9,8},{10,9},{11,10},{13,12},{... | collective-permute-start | bytes 393224 | tf_op jit(solution)/shard_map/ppermute | solution.py:36
  158.2 23.6 %collective-permute-start.37 = (f32[4,2,8,128]{3,2,1,0:T(8,128)}, f32[4,2,8,128]{3,2,1,0:T(8,128)S(1)}, u32[]{:S(2)}, u32[]{:S(2)}) collective-permute-start(f32[4,2,8,128]{3,2,1,0:T(8,128)} %get-tuple-element.150), channel_id=1, source_target_pairs={{5,0},{6,1},{7,2},{9,4},{10,5},{11,6},{13,8},{14,9},{15,10},{17,12... | collective-permute-start | bytes 98312 | tf_op jit(solution)/shard_map/ppermute | solution.py:36
  196.4 47.1 %collective-permute-start.38 = (f32[8,2,32,128]{3,2,1,0:T(8,128)}, f32[8,2,32,128]{3,2,1,0:T(8,128)S(1)}, u32[]{:S(2)}, u32[]{:S(2)}) collective-permute-start(f32[8,2,32,128]{3,2,1,0:T(8,128)} %get-tuple-element.156), channel_id=1, source_target_pairs={{0,4},{1,5},{2,6},{3,7},{4,8},{5,9},{6,10},{7,11},{8,12},{9,13},{1... | collective-permute-start | bytes 786440 | tf_op jit(solution)/shard_map/ppermute | solution.py:36
  200.3 43.2 %collective-permute-start.39 = (f32[8,2,32,128]{3,2,1,0:T(8,128)}, f32[8,2,32,128]{3,2,1,0:T(8,128)S(1)}, u32[]{:S(2)}, u32[]{:S(2)}) collective-permute-start(f32[8,2,32,128]{3,2,1,0:T(8,128)} %get-tuple-element.157), channel_id=1, source_target_pairs={{4,0},{5,1},{6,2},{7,3},{8,4},{9,5},{10,6},{11,7},{12,8},{13,9},{1... | collective-permute-start | bytes 786440 | tf_op jit(solution)/shard_map/ppermute | solution.py:36
  201.6 13.7 %collective-permute-start.42 = (f32[4,2,8,128]{3,2,1,0:T(8,128)}, f32[4,2,8,128]{3,2,1,0:T(8,128)S(1)}, u32[]{:S(2)}, u32[]{:S(2)}) collective-permute-start(f32[4,2,8,128]{3,2,1,0:T(8,128)} %get-tuple-element.160), channel_id=1, source_target_pairs={{0,5},{1,6},{2,7},{4,9},{5,10},{6,11},{8,13},{9,14},{10,15},{12,17... | collective-permute-start | bytes 98312 | tf_op jit(solution)/shard_map/ppermute | solution.py:36
  212.5 30.9 %collective-permute-start.40 = (f32[16,2,8,128]{3,2,1,0:T(8,128)}, f32[16,2,8,128]{3,2,1,0:T(8,128)S(1)}, u32[]{:S(2)}, u32[]{:S(2)}) collective-permute-start(f32[16,2,8,128]{3,2,1,0:T(8,128)} %get-tuple-element.158), channel_id=1, source_target_pairs={{0,1},{1,2},{2,3},{4,5},{5,6},{6,7},{8,9},{9,10},{10,11},{12,13},{... | collective-permute-start | bytes 393224 | tf_op jit(solution)/shard_map/ppermute | solution.py:36
  214.0 29.4 %collective-permute-start.41 = (f32[16,2,8,128]{3,2,1,0:T(8,128)}, f32[16,2,8,128]{3,2,1,0:T(8,128)S(1)}, u32[]{:S(2)}, u32[]{:S(2)}) collective-permute-start(f32[16,2,8,128]{3,2,1,0:T(8,128)} %get-tuple-element.159), channel_id=1, source_target_pairs={{1,0},{2,1},{3,2},{5,4},{6,5},{7,6},{9,8},{10,9},{11,10},{13,12},{... | collective-permute-start | bytes 393224 | tf_op jit(solution)/shard_map/ppermute | solution.py:36
  216.7 26.7 %collective-permute-start.45 = (f32[4,2,8,128]{3,2,1,0:T(8,128)}, f32[4,2,8,128]{3,2,1,0:T(8,128)S(1)}, u32[]{:S(2)}, u32[]{:S(2)}) collective-permute-start(f32[4,2,8,128]{3,2,1,0:T(8,128)} %get-tuple-element.163), channel_id=1, source_target_pairs={{5,0},{6,1},{7,2},{9,4},{10,5},{11,6},{13,8},{14,9},{15,10},{17,12... | collective-permute-start | bytes 98312 | tf_op jit(solution)/shard_map/ppermute | solution.py:36
  260.7 12.5 %collective-permute-start.47 = (f32[4,2,32,128]{3,2,1,0:T(8,128)}, f32[4,2,32,128]{3,2,1,0:T(8,128)S(1)}, u32[]{:S(2)}, u32[]{:S(2)}) collective-permute-start(f32[4,2,32,128]{3,2,1,0:T(8,128)} %get-tuple-element.168), channel_id=1, source_target_pairs={{4,0},{5,1},{6,2},{7,3},{8,4},{9,5},{10,6},{11,7},{12,8},{13,9},{1... | collective-permute-start | bytes 393224 | tf_op jit(solution)/shard_map/ppermute | solution.py:36
  297.3 20.2 %collective-permute-start.7 = (f32[4,128,256]{2,1,0:T(8,128)S(1)}, f32[4,128,256]{2,1,0:T(8,128)S(1)}, u32[]{:S(2)}, u32[]{:S(2)}) collective-permute-start(f32[4,128,256]{2,1,0:T(8,128)S(1)} %param.6), channel_id=1, source_target_pairs={{0,8},{1,9},{2,10},{3,11},{4,12},{5,13},{6,14},{7,15},{8,0},{9,1},... | collective-permute-start | bytes 1572872 | tf_op jit(solution)/shard_map/cond/branch_2_fun/ppermute | solution.py:36
  328.2 15.9 %collective-permute-start.57 = (f32[4,128,256]{2,1,0:T(8,128)S(1)}, f32[4,128,256]{2,1,0:T(8,128)S(1)}, u32[]{:S(2)}, u32[]{:S(2)}) collective-permute-start(f32[4,128,256]{2,1,0:T(8,128)S(1)} %pad_maximum_fusion.1), channel_id=1, source_target_pairs={{0,80},{1,81},{2,82},{3,83},{4,84},{5,85},{6,86},{7,87},{8,88},{9,... | collective-permute-start | bytes 1572872 | tf_op jit(solution)/shard_map/ppermute | solution.py:36
  331.8 14.4 %collective-permute-start.55 = (f32[4,128,256]{2,1,0:T(8,128)S(1)}, f32[4,128,256]{2,1,0:T(8,128)S(1)}, u32[]{:S(2)}, u32[]{:S(2)}) collective-permute-start(f32[4,128,256]{2,1,0:T(8,128)S(1)} %pad_maximum_fusion), channel_id=1, source_target_pairs={{0,64},{1,65},{2,66},{3,67},{4,68},{5,69},{6,70},{7,71},{8,72},{9,... | collective-permute-start | bytes 1572872 | tf_op jit(solution)/shard_map/ppermute | solution.py:36
  (65 other events, 437.6 us)
